TPU v7x, 128 devices: a whole 4x4x4 slice. The times are simulated.
128 devices in a mesh: seq: 16 (over x_lo, y, core), tp: 8 (over z, x_hi).
Axes of the slice: x: 4 (x_hi: 2, x_lo: 2; x = x_hi * 2 + x_lo), y: 4, z: 4, core: 2. Of those that a mesh axis runs over, the one named last changes fastest.
Arguments:
- selected_hidden: bfloat16 [32, 104, 2048], P('seq', None, 'tp'), may hold values from -6 to 6
- cached_keys: bfloat16 [32, 1024, 1024], P('seq', None, 'tp'), may hold values from -48 to 48
- cached_values: bfloat16 [32, 1024, 1024], P('seq', None, 'tp'), may hold values from -6 to 6
- slot_spans: int32 [32], replicated, may hold values from 0 to 31, each once
- span_order: int32 [4, 8], replicated, may hold values from 0 to 7, each once within a row
- cache_start: int32 [4, 8], replicated, may hold values from 0 to 16383
- selected_index: int32 [32, 104], replicated, may hold values from 0 to 1023, as said below
- input_gain: bfloat16 [2048], replicated, may hold values from 0.5 to 2
- query_weight: bfloat16 [2048, 2048], P(None, 'tp'), may hold values from -0.125 to 0.125
- key_weight: bfloat16 [2048, 1024], P(None, 'tp'), may hold values from -0.125 to 0.125
- value_weight: bfloat16 [2048, 1024], P(None, 'tp'), may hold values from -0.125 to 0.125
- query_gain: bfloat16 [128], replicated, may hold values from 1 to 2
- key_gain: bfloat16 [128], replicated, may hold values from 1 to 2
- output_weight: bfloat16 [2048, 2048], P('tp'), may hold values from -0.125 to 0.125
- post_gain: bfloat16 [2048], replicated, may hold values from 0.5 to 2
- gate_weight: bfloat16 [2048, 6144], P(None, 'tp'), may hold values from -0.125 to 0.125
- up_weight: bfloat16 [2048, 6144], P(None, 'tp'), may hold values from -0.125 to 0.125
- down_weight: bfloat16 [6144, 2048], P('tp'), may hold values from -0.078125 to 0.078125
Outputs:
- new_hidden: bfloat16 [32, 104, 2048], P('seq', None, 'tp')
Inputs may be any that keep to these rules, and one draw needn't show every extreme that they name: `selected_index`: each row holds 104 distinct positions in increasing order. `slot_spans`: each span of each request is held by exactly one slot. `span_order`: each row places the 8 spans of a request in some order.
All inputs are finite; a program needn't handle non-finite values.
Results may differ from a plain program's by a relative error of at most 0.027.
Values may be sent and summed in bfloat16 or wider, within the bound.
No kernel may reach another device: no remote copies, remote signals or barrier semaphores. Data moves between devices by JAX's collectives and lax.ppermute only.
A program may use at most 128 MiB of HBM per device.

v0:
```python
import jax
import jax.numpy as jnp
from jax import lax
from jax.sharding import PartitionSpec as P

theta_base = 1000000.0
norm_eps = 1e-06


def rms_scale(values):
    return values * lax.rsqrt(jnp.mean(values * values, axis=-1, keepdims=True) + norm_eps)


def rotary(values, positions):
    half_len = values.shape[-1] // 2
    frequency = jnp.exp(
        -jnp.log(theta_base) * jnp.arange(half_len, dtype=jnp.float32) * 2.0 / values.shape[-1]
    )
    angles = positions.astype(jnp.float32)[..., None] * frequency
    cosine = jnp.cos(angles)[..., None, :]
    sine_part = jnp.sin(angles)[..., None, :]
    lower_half = values[..., :half_len]
    upper_half = values[..., half_len:]
    return jnp.concatenate(
        [
            lower_half * cosine - upper_half * sine_part,
            upper_half * cosine + lower_half * sine_part,
        ],
        axis=-1,
    )


def slot_table(slot_ids, slot_spans, span_order, cache_start, span_len):
    slot_count = slot_spans.shape[0]
    span_count = span_order.shape[1]
    slot_match = (slot_ids[:, None] == jnp.arange(slot_count, dtype=jnp.int32)[None, :]).astype(
        jnp.int32
    )
    span_ids = jnp.sum(slot_match * slot_spans[None, :], axis=1)
    span_match = (
        span_ids[:, None] == jnp.arange(span_order.size, dtype=jnp.int32)[None, :]
    ).astype(jnp.int32)
    new_place = jnp.sum(span_match * span_order.reshape(-1)[None, :], axis=1)
    old_start = jnp.sum(span_match * cache_start.reshape(-1)[None, :], axis=1)
    return (span_ids // span_count, new_place * span_len, old_start)


def on_device(
    selected_hidden,
    cached_keys,
    cached_values,
    slot_spans,
    span_order,
    cache_start,
    selected_index,
    input_gain,
    query_weight,
    key_weight,
    value_weight,
    query_gain,
    key_gain,
    output_weight,
    post_gain,
    gate_weight,
    up_weight,
    down_weight,
):
    slot_local, select_count, width_local = selected_hidden.shape
    span_len = cached_keys.shape[1]
    head_dim = query_gain.shape[0]
    kv_local = cached_keys.shape[2] // head_dim
    query_local = query_weight.shape[1] // head_dim
    group_size = query_local // kv_local
    row_count = slot_local * select_count
    score_scale = head_dim ** (-0.5)
    first_slot = lax.axis_index("seq") * slot_local
    local_slots = first_slot + jnp.arange(slot_local, dtype=jnp.int32)
    local_request, local_base, local_start = slot_table(
        local_slots, slot_spans, span_order, cache_start, span_len
    )
    local_index = lax.dynamic_slice_in_dim(selected_index, first_slot, slot_local, 0)
    query_pos = (local_base[:, None] + local_index).reshape(-1)
    query_request = jnp.broadcast_to(local_request[:, None], (slot_local, select_count)).reshape(-1)
    hidden_local = selected_hidden.reshape(row_count, width_local)
    hidden_full = lax.all_gather(hidden_local, "tp", axis=1, tiled=True)
    normed = (rms_scale(hidden_full.astype(jnp.float32)) * input_gain.astype(jnp.float32)).astype(
        jnp.bfloat16
    )
    query_proj = jnp.dot(normed, query_weight, preferred_element_type=jnp.float32).reshape(
        row_count, query_local, head_dim
    )
    queries = rotary(rms_scale(query_proj) * query_gain.astype(jnp.float32), query_pos).astype(
        jnp.bfloat16
    )
    key_proj = jnp.dot(normed, key_weight, preferred_element_type=jnp.float32).reshape(
        row_count, kv_local, head_dim
    )
    new_keys = rotary(rms_scale(key_proj) * key_gain.astype(jnp.float32), query_pos).astype(
        jnp.bfloat16
    )
    new_values = (
        jnp.dot(normed, value_weight, preferred_element_type=jnp.float32)
        .astype(jnp.bfloat16)
        .reshape(row_count, kv_local, head_dim)
    )
    shift_pos = jnp.broadcast_to((local_base - local_start)[:, None], (slot_local, span_len))
    shifted = rotary(
        cached_keys.reshape(slot_local, span_len, kv_local, head_dim).astype(jnp.float32), shift_pos
    ).astype(jnp.bfloat16)
    slot_rows = jnp.arange(slot_local, dtype=jnp.int32)[:, None]
    joined_keys = (
        shifted.at[slot_rows, local_index]
        .set(new_keys.reshape(slot_local, select_count, kv_local, head_dim))
        .reshape(slot_local, span_len, kv_local * head_dim)
    )
    joined_values = (
        cached_values.reshape(slot_local, span_len, kv_local, head_dim)
        .at[slot_rows, local_index]
        .set(new_values.reshape(slot_local, select_count, kv_local, head_dim))
        .reshape(slot_local, span_len, kv_local * head_dim)
    )

    def attend_block(state_in, query_set, key_block, value_block, slot_id):
        query_vecs, positions, requests = query_set
        key_request, key_base, unused_start = slot_table(
            slot_id[None], slot_spans, span_order, cache_start, span_len
        )
        key_pos = key_base[0] + jnp.arange(span_len, dtype=jnp.int32)
        visible = (requests[:, None] == key_request[0]) & (key_pos[None, :] <= positions[:, None])
        run_max, run_sum, run_acc = state_in
        grouped = query_vecs.reshape(-1, kv_local, group_size, head_dim)
        key_heads = key_block.reshape(span_len, kv_local, head_dim)
        value_heads = value_block.reshape(span_len, kv_local, head_dim)
        scores = (
            jnp.einsum("qkgd,lkd->qkgl", grouped, key_heads, preferred_element_type=jnp.float32)
            * score_scale
        )
        key_mask = visible[:, None, None, :]
        scores = jnp.where(key_mask, scores, -jnp.inf)
        new_max = jnp.maximum(run_max, jnp.max(scores, axis=-1))
        safe_max = jnp.where(new_max == -jnp.inf, 0.0, new_max)
        rescale = jnp.exp(run_max - safe_max)
        weights = jnp.where(key_mask, jnp.exp(scores - safe_max[..., None]), 0.0)
        new_sum = rescale * run_sum + jnp.sum(weights, axis=-1)
        new_acc = rescale[..., None] * run_acc + jnp.einsum(
            "qkgl,lkd->qkgd",
            weights.astype(jnp.bfloat16),
            value_heads,
            preferred_element_type=jnp.float32,
        )
        return (new_max, new_sum, new_acc)

    local_set = (queries, query_pos, query_request)
    piece_keys = lax.all_gather(joined_keys, "seq", axis=0, tiled=True)
    piece_values = lax.all_gather(joined_values, "seq", axis=0, tiled=True)

    def step_slot(running, slot_item):
        block_keys, block_values, offset = slot_item
        return (attend_block(running, local_set, block_keys, block_values, offset), None)

    state_out, unused_out = lax.scan(
        step_slot,
        (
            jnp.full((row_count, kv_local, group_size), -jnp.inf, jnp.float32),
            jnp.zeros((row_count, kv_local, group_size), jnp.float32),
            jnp.zeros((row_count, kv_local, group_size, head_dim), jnp.float32),
        ),
        (piece_keys, piece_values, jnp.arange(piece_keys.shape[0], dtype=jnp.int32)),
    )
    run_max, run_sum, run_acc = state_out
    attended = (run_acc / run_sum[..., None]).astype(jnp.bfloat16)
    out_part = jnp.dot(
        attended.reshape(row_count, query_local * head_dim),
        output_weight,
        preferred_element_type=jnp.float32,
    )
    attention_sum = lax.psum(out_part.astype(jnp.bfloat16), "tp").astype(jnp.float32)
    stream = (hidden_full.astype(jnp.float32) + attention_sum).astype(jnp.bfloat16)
    normed_post = (rms_scale(stream.astype(jnp.float32)) * post_gain.astype(jnp.float32)).astype(
        jnp.bfloat16
    )
    gate_values = jnp.dot(normed_post, gate_weight, preferred_element_type=jnp.float32)
    up_values = jnp.dot(normed_post, up_weight, preferred_element_type=jnp.float32)
    active = (jax.nn.silu(gate_values) * up_values).astype(jnp.bfloat16)
    feedforward_sum = lax.psum(
        jnp.dot(active, down_weight, preferred_element_type=jnp.float32).astype(jnp.bfloat16), "tp"
    ).astype(jnp.float32)
    result_full = (stream.astype(jnp.float32) + feedforward_sum).astype(jnp.bfloat16)
    result = lax.dynamic_slice_in_dim(
        result_full, lax.axis_index("tp") * width_local, width_local, 1
    )
    return result.reshape(slot_local, select_count, width_local)


def solution(mesh):
    in_specs = (
        P("seq", None, "tp"),
        P("seq", None, "tp"),
        P("seq", None, "tp"),
        P(),
        P(),
        P(),
        P(),
        P(),
        P(None, "tp"),
        P(None, "tp"),
        P(None, "tp"),
        P(),
        P(),
        P("tp", None),
        P(),
        P(None, "tp"),
        P(None, "tp"),
        P("tp", None),
    )
    out_specs = P("seq", None, "tp")
    return jax.shard_map(
        on_device, mesh=mesh, in_specs=in_specs, out_specs=out_specs, check_vma=False
    )
```

profile of v0, /device:TPU:0, one launch (start us, length us, event | category | flops | bytes accessed | tf_op | source)
XLA Modules:
  0.0 828.1 jit_solution(6008349107138852399)
XLA Ops:
  19.5 38.6 %all_gather.9 = bf16[208,2048]{1,0:T(8,128)(2,1)S(1)} all-gather(bf16[208,256]{1,0:T(8,128)(2,1)S(1)} %bitcast.112), channel_id=1, replica_groups=mesh['seq'=16,'tp'=8] {'tp'}, dimensions={1}, use_global_device_ids=true | all-gather | bytes 958464 | tf_op jit(solution)/shard_map/all_gather | solution.py:85
  60.4 22.1 %scatter_fusion = bf16[2,1024,128]{2,1,0:T(8,128)(2,1)} fusion(bf16[2,1024,128]{2,1,0:T(8,128)(2,1)} %copy.36, s32[208]{0:T(256)S(1)} %reshape.474, bf16[208,128]{1,0:T(8,128)(2,1)S(1)} %bitcast.111), kind=kCustom, calls=%fused_computation | custom fusion | bytes 161408 | tf_op jit(solution)/shard_map/scatter | solution.py:113
  84.3 22.0 %scatter_fusion.1 = bf16[2,1024,128]{2,1,0:T(8,128)(2,1)} fusion(bf16[2,1024,128]{2,1,0:T(8,128)(2,1)} %copy.64, s32[208]{0:T(256)S(1)} %reshape.474, bf16[208,128]{1,0:T(8,128)(2,1)S(1)} %convolution_convert_fusion.2), kind=kCustom, calls=%fused_computation.1 | custom fusion | bytes 161408 | tf_op jit(solution)/shard_map/scatter | solution.py:119
  106.5 2.7 fusion.63
  112.5 23.5 %all-gather.5.cloned.1.call-done = bf16[32,1024,128]{2,1,0:T(8,128)(2,1)} async-done(((bf16[2,1024,128]{2,1,0:T(8,128)(2,1)}), bf16[32,1024,128]{2,1,0:T(8,128)(2,1)}) %all-gather.5.cloned.1.call-update) | async-done | bytes 8388624 | tf_op jit(solution)/shard_map/all_gather | solution.py:154
  136.0 54.8 %all-gather.7.cloned.1.call-done = bf16[32,1024,128]{2,1,0:T(8,128)(2,1)} async-done(((bf16[2,1024,128]{2,1,0:T(8,128)(2,1)}), bf16[32,1024,128]{2,1,0:T(8,128)(2,1)}) %all-gather.7.cloned.1.call-update) | async-done | bytes 8388624 | tf_op jit(solution)/shard_map/all_gather | solution.py:155
  190.9 436.8 %while.18 = (s32[]{:T(128)}, f32[208,1,2]{0,2,1:T(2,128)S(1)}, f32[208,1,2]{0,2,1:T(2,128)S(1)}, f32[208,1,2,128]{3,0,2,1:T(8,128)}, s32[32]{0:T(128)S(1)}, /*in...) while((s32[]{:T(128)}, f32[208,1,2]{0,2,1:T(2,128)S(1)}, ...), condition=%wide.wide.region_13.14_spmd.clone, body=%wide.wide.region_8.13_spmd.clone.sunk | while | flops 222529680 | bytes 15580799 | solution.py:161
  211.1 2.6 fusion.101
  224.8 2.6 fusion.101
  238.4 2.6 fusion.101
  252.1 2.6 fusion.101
  265.7 2.6 fusion.101
  279.4 2.6 fusion.101
  293.0 2.6 fusion.101
  306.7 2.6 fusion.101
  320.3 2.6 fusion.101
  334.0 2.6 fusion.101
  347.6 2.6 fusion.101
  361.3 2.6 fusion.101
  374.9 2.6 fusion.101
  388.6 2.6 fusion.101
  402.2 2.6 fusion.101
  415.9 2.6 fusion.101
  429.5 2.6 fusion.101
  443.2 2.6 fusion.101
  456.8 2.6 fusion.101
  470.5 2.6 fusion.101
  631.5 89.7 %all-reduce.3.cloned.1.call-done = bf16[208,2048]{1,0:T(8,128)(2,1)} async-done(((bf16[208,2048]{1,0:T(8,128)(2,1)}), bf16[208,2048]{1,0:T(8,128)(2,1)}) %all-reduce.3.cloned.1.call-update) | async-done | bytes 851984 | tf_op jit(solution)/shard_map/psum | solution.py:177
  721.1 3.0 multiply_reduce_fusion
  724.2 3.7 fusion.58
  727.8 5.3 convolution_convert_fusion
  733.2 86.7 %all-reduce.5.cloned.1.call-done = bf16[208,2048]{1,0:T(8,128)(2,1)} async-done(((bf16[208,2048]{1,0:T(8,128)(2,1)}), bf16[208,2048]{1,0:T(8,128)(2,1)}) %all-reduce.5.cloned.1.call-update) | async-done | bytes 851984 | tf_op jit(solution)/shard_map/psum | solution.py:185
  (734 shorter events, 313.2 us)
Async XLA Ops:
  6.5 721.3 %copy-start = (bf16[768,2048]{1,0:T(8,128)(2,1)S(1)}, bf16[768,2048]{1,0:T(8,128)(2,1)}, u32[]{:S(2)}) copy-start(bf16[768,2048]{1,0:T(8,128)(2,1)} %param.37) | copy-start | bytes 9437188
  6.5 129.5 %all-gather.5.cloned.1.call-start = ((), (), s32[]{:S(2)}) async-start(), calls=%async_computation.2 | async-start | bytes 8912896 | tf_op jit(solution)/shard_map/all_gather | solution.py:154
  12.6 98.0 %copy-start.11 = (s32[2,104]{1,0:T(2,128)}, s32[2,104]{1,0:T(2,128)S(1)}, u32[]{:S(2)}) copy-start(s32[2,104]{1,0:T(2,128)S(1)} %get-tuple-element.392) | copy-start | bytes 2500
  15.8 3.7 copy-start.7
  16.5 41.6 %copy-start.9 = (bf16[2048]{0:T(1024)(128)(2,1)S(1)}, bf16[2048]{0:T(1024)(128)(2,1)}, u32[]{:S(2)}) copy-start(bf16[2048]{0:T(1024)(128)(2,1)} %param.27) | copy-start | bytes 12292
  16.5 41.9 %copy-start.13 = (bf16[128]{0:T(256)(128)(2,1)S(1)}, bf16[128]{0:T(256)(128)(2,1)}, u32[]{:S(2)}) copy-start(bf16[128]{0:T(256)(128)(2,1)} %param.32) | copy-start | bytes 772
  19.5 39.5 %copy-start.12 = (bf16[2048,128]{1,0:T(8,128)(2,1)S(1)}, bf16[2048,128]{1,0:T(8,128)(2,1)}, u32[]{:S(2)}) copy-start(bf16[2048,128]{1,0:T(8,128)(2,1)} %param.29) | copy-start | bytes 1572868
  82.5 24.0 %copy-start.14 = (bf16[128]{0:T(256)(128)(2,1)S(1)}, bf16[128]{0:T(256)(128)(2,1)}, u32[]{:S(2)}) copy-start(bf16[128]{0:T(256)(128)(2,1)} %param.31) | copy-start | bytes 772
  82.5 108.4 %all-gather.7.cloned.1.call-start = ((), (), s32[]{:S(2)}) async-start(), calls=%async_computation.3 | async-start | bytes 8912896 | tf_op jit(solution)/shard_map/all_gather | solution.py:155
  106.4 614.8 %all-reduce.3.cloned.1.call-start = ((), (), s32[]{:S(2)}) async-start(), calls=%async_computation | async-start | bytes 1703936 | tf_op jit(solution)/shard_map/psum | solution.py:177
  109.1 81.7 %copy-start.8 = (s32[4,8]{1,0:T(4,128)S(1)}, s32[4,8]{1,0:T(4,128)}, u32[]{:S(2)}) copy-start(s32[4,8]{1,0:T(4,128)} %param.24) | copy-start | bytes 388
  109.1 81.7 %copy-start.15 = (s32[32]{0:T(128)S(1)}, s32[32]{0:T(128)}, u32[]{:S(2)}) copy-start(s32[32]{0:T(128)} %param.23) | copy-start | bytes 388
  200.1 2.2 copy-start.5
  213.7 2.2 copy-start.5
  227.4 2.2 copy-start.5
  241.0 2.2 copy-start.5
  254.7 2.2 copy-start.5
  282.0 2.2 copy-start.5
  295.6 2.2 copy-start.5
  322.9 2.2 copy-start.5
  336.6 2.2 copy-start.5
  363.9 2.2 copy-start.5
  377.5 2.2 copy-start.5
  391.2 2.2 copy-start.5
  404.8 2.2 copy-start.5
  418.5 2.2 copy-start.5
  432.1 2.2 copy-start.5
  445.8 2.2 copy-start.5
  627.7 3.8 copy-start.10
  631.4 188.5 %all-reduce.5.cloned.1.call-start = ((), (), s32[]{:S(2)}) async-start(), calls=%async_computation.1 | async-start | bytes 1703936 | tf_op jit(solution)/shard_map/psum | solution.py:185
  721.1 3.0 copy-start.3
  721.1 3.0 copy-start.4
  (81 other events, 128.2 us)
Sparse Core Ops, SparseCore 0:
  82.6 53.3 all-gather.4
  137.7 53.0 all-gather.6
  631.5 89.5 all-reduce.2
  733.3 86.5 all-reduce.4
where the time goes:
time: 833 us; the launch traced here: 828 us
  waiting for transfers between devices  255 us (31%)
  other arithmetic  173 us (21%)
  matrix products  149 us (18%)
  local copies, waits for them, and re-layouts  102 us (12%)
  loops' own time  96.9 us (12%)
  blocking collectives  38.6 us (5%)
  between operations  13.4 us (2%)
    another operation x1, loops' own time, on_device(): lax.scan(step_slot, (jnp.full((row_count, kv_local, group_size), -jnp.inf...  96.9 us
    psum x1, waiting for transfers between devices, on_device(): lax.psum(out_part.astype(jnp.bfloat16), 'tp').astype(jnp.float32)  89.7 us
    psum x1, waiting for transfers between devices, on_device(): lax.psum(jnp.dot(active, down_weight, preferred_element_type=jnp.float32)...  86.7 us
    dot_general x32, matrix products, attend_block(): jnp.einsum('qkgd,lkd->qkgl', grouped, key_heads, preferred_element_type=j...  84.1 us
    reduce_sum x32, other arithmetic, attend_block(): new_sum = rescale * run_sum + jnp.sum(weights, axis=-1)  68.4 us
    all_gather x1, waiting for transfers between devices, on_device(): piece_values = lax.all_gather(joined_values, 'seq', axis=0, tiled=True)  54.8 us
    dot_general x32, matrix products, attend_block(): jnp.einsum('qkgl,lkd->qkgd', weights.astype(jnp.bfloat16), value_heads, p...  48.8 us
    reduce_sum x33, other arithmetic, slot_table(): span_ids = jnp.sum(slot_match * slot_spans[None, :], axis=1)  42.8 us
  transfers between devices with their start and end apart: 4, of which 4 were waited for; matrix products, arithmetic and copies ran while one was open for 4% of the time, Pallas kernels for 0%

commit v1 on v0

v1 whole, which is shorter than its diff:
```python
import functools

import jax
import jax.numpy as jnp
from jax import lax
from jax.experimental import pallas as pl
from jax.experimental.pallas import tpu as pltpu
from jax.sharding import Mesh
from jax.sharding import PartitionSpec as P

theta_base = 1000000.0
norm_eps = 1e-06
NEG = -1e30
FAR = 1e9
TP = ("z", "xhi")
SEQ = ("xlo", "yhi", "ylo", "core")
VMEM = pl.BlockSpec(memory_space=pltpu.VMEM)
SMEM = pl.BlockSpec(memory_space=pltpu.SMEM)
ANY = pl.BlockSpec(memory_space=pl.ANY)
F32 = jnp.float32
BF16 = jnp.bfloat16


def rotation_tables(positions, head_dim):
    half = head_dim // 2
    frequency = jnp.exp(-jnp.log(theta_base) * jnp.arange(half, dtype=F32) * 2.0 / head_dim)
    angles = positions.astype(F32)[..., None] * frequency
    cosine, sine = jnp.cos(angles), jnp.sin(angles)
    return jnp.concatenate([cosine, cosine], -1), jnp.concatenate([-sine, sine], -1)


def rotate(values, cosine, sine):
    return values * cosine + pltpu.roll(values, values.shape[-1] // 2, values.ndim - 1) * sine


def swap(x, axes, mask, size):
    return lax.ppermute(x, axes, [(i, i ^ mask) for i in range(size)])


def rotate_keys_kernel(k_ref, c_ref, s_ref, o_ref):
    o_ref[0] = rotate(k_ref[0].astype(F32), c_ref[0], s_ref[0]).astype(BF16)


def rotate_keys(keys, cosine, sine):
    slots, span, hd = keys.shape
    return pl.pallas_call(
        rotate_keys_kernel,
        grid=(slots,),
        in_specs=[
            pl.BlockSpec((1, span, hd), lambda i: (i, 0, 0)),
            pl.BlockSpec((1, 1, hd), lambda i: (i, 0, 0)),
            pl.BlockSpec((1, 1, hd), lambda i: (i, 0, 0)),
        ],
        out_specs=pl.BlockSpec((1, span, hd), lambda i: (i, 0, 0)),
        out_shape=jax.ShapeDtypeStruct(keys.shape, BF16),
        name="rotate_keys",
    )(keys, cosine, sine)


def scale_of(pieces, width):
    total = jnp.sum(pieces[0] * pieces[0], axis=-1, keepdims=True)
    for piece in pieces[1:]:
        total = total + jnp.sum(piece * piece, axis=-1, keepdims=True)
    return lax.rsqrt(total / width + norm_eps)


def head_norm(values):
    return values * lax.rsqrt(jnp.mean(values * values, axis=-1, keepdims=True) + norm_eps)


def project_kernel(n, me_ref, *refs):
    pieces = refs[:n]
    gain, wq, wk, wv, qg, kg, cos, sin, q_out, kv_out = refs[n:]
    me = me_ref[0]
    width = pieces[0].shape[1]
    hd = qg.shape[1]
    xs = [p[...].astype(F32) for p in pieces]
    scale = scale_of(xs, n * width)
    q = k = v = None
    for step in range(n):
        src = jnp.bitwise_xor(me, step)
        rows = pl.ds(pl.multiple_of(src * width, width), width)
        x = (xs[step] * scale * gain[pl.ds(src, 1), :]).astype(BF16)
        dq = jnp.dot(x, wq[rows, :], preferred_element_type=F32)
        dk = jnp.dot(x, wk[rows, :], preferred_element_type=F32)
        dv = jnp.dot(x, wv[rows, :], preferred_element_type=F32)
        q, k, v = (dq, dk, dv) if q is None else (q + dq, k + dk, v + dv)
    c, s = cos[...], sin[...]
    for h in range(q.shape[1] // hd):
        part = q[:, h * hd : (h + 1) * hd]
        q_out[:, h * hd : (h + 1) * hd] = rotate(head_norm(part) * qg[...], c, s).astype(BF16)
    kv_out[:, :hd] = rotate(head_norm(k) * kg[...], c, s).astype(BF16)
    kv_out[:, hd:] = v.astype(BF16)


def attend_kernel(count, ids, tab, kpos, tq, *refs):
    q_in, kv_in, k_in, v_in = refs[0:4], refs[4:8], refs[8:12], refs[12:16]
    outs = refs[16:20]
    keys, values, queries, run_m, run_l, run_acc, sems = refs[20:]
    hd = keys.shape[2]
    span = k_in[0].shape[1]
    slots = keys.shape[0]
    place_at = tab.shape[0] // 2
    xy, mk = ids[0], ids[1]
    copies = []
    for p in range(4):
        for which, (src, dst) in enumerate(((k_in[p], keys), (v_in[p], values))):
            copies.append(
                pltpu.make_async_copy(
                    src, dst.at[pl.ds(2 * p, 2), pl.ds(0, span), :], sems.at[which, p]
                )
            )
    for c in copies:
        c.start()
    pad = keys.shape[1] - span - count
    for p in range(4):
        for j in range(2):
            fresh = kv_in[p][j * count : (j + 1) * count, :]
            zero = jnp.zeros((pad, hd), BF16)
            keys[2 * p + j, span:, :] = jnp.concatenate([fresh[:, :hd], zero], 0)
            values[2 * p + j, span:, :] = jnp.concatenate([fresh[:, hd:], zero], 0)
            rows = q_in[p][j * count : (j + 1) * count, :]
            queries[2 * p + j] = jnp.concatenate([rows[:, :hd], rows[:, hd:]], 0)
    for c in copies:
        c.wait()
    factor = hd**-0.5

    def one_query(qi, _):
        q_nat = jnp.bitwise_xor(xy, qi // 2)
        q_slot = q_nat * 8 + mk * 2 + qi % 2
        q_req, q_place = tab[q_slot], tab[place_at + q_slot]
        run_m[...] = jnp.full(run_m.shape, NEG, F32)
        run_l[...] = jnp.zeros(run_l.shape, F32)
        run_acc[...] = jnp.zeros(run_acc.shape, F32)

        def one_key(ki, _):
            k_nat = jnp.bitwise_xor(mk, ki // 2) * 2 + ki % 2
            k_slot = xy * 8 + k_nat
            k_req, k_place = tab[k_slot], tab[place_at + k_slot]

            @pl.when(jnp.logical_and(k_req == q_req, k_place <= q_place))
            def _():
                limit = jnp.where(k_place < q_place, 65536.0, 0.0)
                bound = tq[q_nat * 2 + qi % 2] + limit
                scores = lax.dot_general(
                    queries[qi], keys[ki], (((1,), (1,)), ((), ())), preferred_element_type=F32
                )
                scores = jnp.where(kpos[pl.ds(k_nat, 1), :] <= bound, scores, NEG)
                old = run_m[...]
                new = jnp.maximum(old, jnp.max(scores, axis=-1, keepdims=True))
                shrink = jnp.exp((old - new) * factor)
                weights = jnp.exp((scores - new) * factor)
                run_m[...] = new
                run_l[...] = run_l[...] * shrink + jnp.sum(weights, axis=-1, keepdims=True)
                run_acc[...] = run_acc[...] * shrink + jnp.dot(
                    weights.astype(BF16), values[ki], preferred_element_type=F32
                )

            return 0

        lax.fori_loop(0, slots, one_key, 0)
        total = run_l[...]
        some = total > 0.0
        safe = jnp.where(some, total, 1.0)
        out = (run_acc[...] / safe).astype(BF16)
        lse = jnp.where(some, run_m[...] * factor + jnp.log(safe), NEG)
        high = lse.astype(BF16)
        rest = lse - high.astype(F32)
        mid = rest.astype(BF16)
        low = (rest - mid.astype(F32)).astype(BF16)
        lane = lax.broadcasted_iota(jnp.int32, out.shape, 1)
        stats = jnp.where(
            lane == 0,
            high.astype(F32),
            jnp.where(lane == 1, mid.astype(F32), jnp.where(lane == 2, low.astype(F32), 0.0)),
        ).astype(BF16)
        for p in range(4):

            @pl.when(qi // 2 == p)
            def _(p=p):
                outs[p][qi % 2] = jnp.concatenate([out, stats], axis=1)

        return 0

    lax.fori_loop(0, slots, one_query, 0)


def merge_kernel(n, count, me_ref, *refs):
    parts, wo, outs = refs[:4], refs[4], refs[5:]
    me = me_ref[0]
    hd = parts[0].shape[2] // 2
    width = outs[0].shape[1]
    rows = [[], []]
    for j in range(2):
        lses = []
        for part in parts:
            st = part[j, :, hd:].astype(F32)
            lses.append(st[:, 0:1] + st[:, 1:2] + st[:, 2:3])
        top = functools.reduce(jnp.maximum, lses)
        total = acc = None
        for lse, part in zip(lses, parts):
            w = jnp.exp(lse - top)
            term = w * part[j, :, :hd].astype(F32)
            total, acc = (w, term) if total is None else (total + w, acc + term)
        acc = acc / total
        for h in range(2):
            rows[h].append(acc[h * count : (h + 1) * count])
    att = jnp.concatenate([jnp.concatenate(r, 0) for r in rows], 1).astype(BF16)
    for step in range(n):
        src = jnp.bitwise_xor(me, step)
        cols = pl.ds(pl.multiple_of(src * width, width), width)
        outs[step][...] = jnp.dot(att, wo[:, cols], preferred_element_type=F32).astype(BF16)


def feed_kernel(n, me_ref, *refs):
    pieces = refs[:n]
    gain, wg, wu, wd = refs[n : n + 4]
    outs = refs[n + 4 :]
    me = me_ref[0]
    width = pieces[0].shape[1]
    xs = [p[...].astype(F32) for p in pieces]
    scale = scale_of(xs, n * width)
    g = u = None
    for step in range(n):
        src = jnp.bitwise_xor(me, step)
        rows = pl.ds(pl.multiple_of(src * width, width), width)
        x = (xs[step] * scale * gain[pl.ds(src, 1), :]).astype(BF16)
        dg = jnp.dot(x, wg[rows, :], preferred_element_type=F32)
        du = jnp.dot(x, wu[rows, :], preferred_element_type=F32)
        g, u = (dg, du) if g is None else (g + dg, u + du)
    active = (g / (1.0 + jnp.exp(-g)) * u).astype(BF16)
    for step in range(n):
        src = jnp.bitwise_xor(me, step)
        cols = pl.ds(pl.multiple_of(src * width, width), width)
        outs[step][...] = jnp.dot(active, wd[:, cols], preferred_element_type=F32).astype(BF16)


def on_device(
    selected_hidden,
    cached_keys,
    cached_values,
    slot_spans,
    span_order,
    cache_start,
    selected_index,
    input_gain,
    query_weight,
    key_weight,
    value_weight,
    query_gain,
    key_gain,
    output_weight,
    post_gain,
    gate_weight,
    up_weight,
    down_weight,
):
    slot_local, count, width = selected_hidden.shape
    span = cached_keys.shape[1]
    hd = query_gain.shape[0]
    rows = slot_local * count
    spans = span_order.shape[1]
    n = 8
    params = pltpu.CompilerParams(vmem_limit_bytes=48 << 20)

    def shaped(*shape, dtype=BF16):
        return jax.ShapeDtypeStruct(shape, dtype)

    xy = lax.axis_index(("xlo", "yhi"))
    mk = lax.axis_index(("ylo", "core"))
    me = lax.axis_index(TP).reshape(1)
    first_slot = lax.axis_index(SEQ) * slot_local

    hit = slot_spans[:, None] == jnp.arange(span_order.size, dtype=jnp.int32)[None, :]
    place = jnp.sum(jnp.where(hit, span_order.reshape(-1)[None, :], 0), axis=1)
    start = jnp.sum(jnp.where(hit, cache_start.reshape(-1)[None, :], 0), axis=1)
    table = jnp.concatenate([slot_spans // spans, place])
    ids = jnp.stack([xy, mk])
    base_here = lax.dynamic_slice_in_dim(place * span, first_slot, slot_local, 0)
    start_here = lax.dynamic_slice_in_dim(start, first_slot, slot_local, 0)
    index_here = lax.dynamic_slice_in_dim(selected_index, first_slot, slot_local, 0)

    hidden = selected_hidden.reshape(rows, width)
    pieces = [hidden] + [swap(hidden, TP, k, n) for k in range(1, n)]

    kc, ks = rotation_tables(base_here - start_here, hd)
    keys = rotate_keys(cached_keys, kc[:, None, :], ks[:, None, :])
    keys_y = swap(keys, "ylo", 1, 2)
    values_y = swap(cached_values, "ylo", 1, 2)
    key_set = [keys, swap(keys, "core", 1, 2), keys_y, swap(keys_y, "core", 1, 2)]
    value_set = [
        cached_values,
        swap(cached_values, "core", 1, 2),
        values_y,
        swap(values_y, "core", 1, 2),
    ]

    qc, qs = rotation_tables((base_here[:, None] + index_here).reshape(-1), hd)
    queries, fresh = pl.pallas_call(
        functools.partial(project_kernel, n),
        in_specs=[SMEM] + [VMEM] * (n + 8),
        out_specs=[VMEM, VMEM],
        out_shape=[shaped(rows, query_weight.shape[1]), shaped(rows, 2 * hd)],
        compiler_params=params,
        name="project",
    )(
        me,
        *pieces,
        input_gain.astype(F32).reshape(n, width),
        query_weight,
        key_weight,
        value_weight,
        query_gain.astype(F32)[None],
        key_gain.astype(F32)[None],
        qc,
        qs,
    )
    fresh_y = swap(fresh, "ylo", 1, 2)
    fresh_set = [fresh, swap(fresh, "core", 1, 2), fresh_y, swap(fresh_y, "core", 1, 2)]
    query_set = [queries] + [swap(queries, ("xlo", "yhi"), k, 4) for k in (1, 2, 3)]

    group_index = lax.dynamic_slice_in_dim(selected_index, xy * 8, 8, 0)
    token = jnp.arange(span, dtype=jnp.int32)
    taken = jnp.any(group_index[:, :, None] == token[None, None, :], axis=1)
    kpos = jnp.concatenate(
        [
            jnp.where(taken, FAR, token[None, :].astype(F32)),
            group_index.astype(F32),
            jnp.full((8, 128 - count), FAR, F32),
        ],
        axis=1,
    )
    query_index = lax.dynamic_slice_in_dim(
        selected_index.reshape(4, 4, slot_local, count), mk, 1, 1
    ).reshape(8, count)
    tq = jnp.concatenate([query_index, query_index], axis=1).astype(F32)[:, :, None]

    key_rows = span + 128
    parts = pl.pallas_call(
        functools.partial(attend_kernel, count),
        in_specs=[SMEM, SMEM, VMEM, VMEM] + [VMEM] * 8 + [ANY] * 8,
        out_specs=[VMEM] * 4,
        out_shape=[shaped(slot_local, 2 * count, 2 * hd)] * 4,
        scratch_shapes=[
            pltpu.VMEM((8, key_rows, hd), BF16),
            pltpu.VMEM((8, key_rows, hd), BF16),
            pltpu.VMEM((8, 2 * count, hd), BF16),
            pltpu.VMEM((2 * count, 1), F32),
            pltpu.VMEM((2 * count, 1), F32),
            pltpu.VMEM((2 * count, hd), F32),
            pltpu.SemaphoreType.DMA((2, 4)),
        ],
        compiler_params=params,
        name="attend",
    )(ids, table, kpos, tq, *query_set, *fresh_set, *key_set, *value_set)
    parts = [parts[0]] + [swap(parts[k], ("xlo", "yhi"), k, 4) for k in (1, 2, 3)]

    projected = pl.pallas_call(
        functools.partial(merge_kernel, n, count),
        in_specs=[SMEM] + [VMEM] * 5,
        out_specs=[VMEM] * n,
        out_shape=[shaped(rows, width)] * n,
        compiler_params=params,
        name="merge",
    )(me, *parts, output_weight)
    total = hidden.astype(F32) + projected[0].astype(F32)
    for k in range(1, n):
        total = total + swap(projected[k], TP, k, n).astype(F32)
    stream = total.astype(BF16)

    pieces = [stream] + [swap(stream, TP, k, n) for k in range(1, n)]
    downs = pl.pallas_call(
        functools.partial(feed_kernel, n),
        in_specs=[SMEM] + [VMEM] * (n + 4),
        out_specs=[VMEM] * n,
        out_shape=[shaped(rows, width)] * n,
        compiler_params=params,
        name="feed",
    )(
        me,
        *pieces,
        post_gain.astype(F32).reshape(n, width),
        gate_weight,
        up_weight,
        down_weight,
    )
    total = stream.astype(F32) + downs[0].astype(F32)
    for k in range(1, n):
        total = total + swap(downs[k], TP, k, n).astype(F32)
    return total.astype(BF16).reshape(slot_local, count, width)


def solution(mesh):
    fine = Mesh(
        mesh.devices.reshape(2, 2, 2, 2, 4, 2), ("xlo", "yhi", "ylo", "core", "z", "xhi")
    )
    in_specs = (
        P(SEQ, None, TP),
        P(SEQ, None, TP),
        P(SEQ, None, TP),
        P(),
        P(),
        P(),
        P(),
        P(),
        P(None, TP),
        P(None, TP),
        P(None, TP),
        P(),
        P(),
        P(TP, None),
        P(),
        P(None, TP),
        P(None, TP),
        P(TP, None),
    )
    return jax.shard_map(
        on_device, mesh=fine, in_specs=in_specs, out_specs=P(SEQ, None, TP), check_vma=False
    )
```

time: 833 us -> 173 us (0.21)
  waiting for transfers between devices: 255 us -> 44.5 us
  other arithmetic: 173 us -> 6.51 us
  matrix products: 149 us -> 0 us
  loops' own time: 96.9 us -> 0 us
  local copies, waits for them, and re-layouts: 102 us -> 14 us
  starting transfers between devices: 0.13 us -> 82.2 us
  blocking collectives: 38.6 us -> 0 us
  Pallas kernels: 0 us -> 24.9 us
  between operations: 13.4 us -> 0.21 us
    psum x2 -> x0, waiting for transfers between devices: 176 us -> none  [the longest x1 89.7 us: on_device(): lax.psum(out_part.astype(jnp.bfloat16), 'tp').astype(jnp.float32)]
    reduce_sum x101 -> x1, other arithmetic: 156 us -> 0.83 us  [on_device(): start = jnp.sum(jnp.where(hit, cache_start.reshape(-1)[None, :], 0), axis=1)]
    dot_general x70 -> x0, matrix products: 149 us -> none  [the longest x32 84.1 us: attend_block(): jnp.einsum('qkgd,lkd->qkgl', grouped, key_heads, preferred_element_type=j...]
    another operation x1 -> x0, loops' own time: 96.9 us -> none  [on_device(): lax.scan(step_slot, (jnp.full((row_count, kv_local, group_size), -jnp.inf...]
    ppermute x0 -> x43, starting transfers between devices: none -> 82.2 us  [swap(): return lax.ppermute(x, axes, [(i, i ^ mask) for i in range(size)])]
    all_gather x2 -> x0, waiting for transfers between devices: 78.3 us -> none  [the longest x1 54.8 us: on_device(): piece_values = lax.all_gather(joined_values, 'seq', axis=0, tiled=True)]
    ppermute x0 -> x43, waiting for transfers between devices: none -> 44.5 us  [swap(): return lax.ppermute(x, axes, [(i, i ^ mask) for i in range(size)])]
    scatter x2 -> x0, local copies, waits for them, and re-layouts: 44.1 us -> none  [the longest x1 22.1 us: on_device(): joined_keys = shifted.at[slot_rows, local_index].set(new_keys.reshape(slo...]
  transfers between devices with their start and end apart: 4 -> 43, of which waited for: 4 -> 19; matrix products, arithmetic and copies ran while one was open for 4% -> 6% of each run, Pallas kernels for 0% -> 2%
where the time goes in v1:
time: 173 us; the launch traced here: 172 us
  starting transfers between devices  82.2 us (48%)
  waiting for transfers between devices  44.5 us (26%)
  Pallas kernels  24.9 us (14%)
  local copies, waits for them, and re-layouts  14 us (8%)
  other arithmetic  6.51 us (4%)
    ppermute x43, starting transfers between devices, swap(): return lax.ppermute(x, axes, [(i, i ^ mask) for i in range(size)])  82.2 us
    ppermute x43, waiting for transfers between devices, swap(): return lax.ppermute(x, axes, [(i, i ^ mask) for i in range(size)])  44.5 us
    pallas_call x1, Pallas kernels, on_device(): pl.pallas_call(functools.partial(attend_kernel, count), in_specs=[SMEM, S...  14.9 us
    unnamed x34, local copies, waits for them, and re-layouts  9.62 us
    pallas_call x1, Pallas kernels, on_device(): pl.pallas_call(functools.partial(feed_kernel, n), in_specs=[SMEM] + [VMEM...  5.59 us
  transfers between devices with their start and end apart: 43, of which 19 were waited for; matrix products, arithmetic and copies ran while one was open for 6% of the time, Pallas kernels for 2%

profile of v1, /device:TPU:0, one launch (start us, length us, event | category | flops | bytes accessed | tf_op | source)
XLA Modules:
  0.0 172.3 jit_solution(7901988171945575290)
XLA Ops:
  0.0 3.1 %collective-permute-start = (bf16[208,256]{1,0:T(8,128)(2,1)}, bf16[208,256]{1,0:T(8,128)(2,1)S(1)}, u32[]{:S(2)}, u32[]{:S(2)}) collective-permute-start(bf16[208,256]{1,0:T(8,128)(2,1)} %bitcast.20), channel_id=1, source_target_pairs={{0,1},{1,0},{2,3},{3,2},{4,5},{5,4},{6,7},{7,6},{8,9},{9,8},{10,11... | collective-permute-start | bytes 319496 | tf_op jit(solution)/shard_map/ppermute | solution.py:37
  8.3 2.0 %rotate_keys.1.refs_8_ = bf16[2,1024,128]{2,1,0:T(8,128)(2,1)} custom-call(bf16[2,1024,128]{2,1,0:T(8,128)(2,1)} %k_ref.1, f32[2,1,128]{2,1,0:T(1,128)} %bitcast.30, f32[2,1,128]{2,1,0:T(1,128)} %bitcast.31), custom_call_target="tpu_custom_call" | custom-call | tf_op jit(solution)/shard_map/rotate_keys/pallas_call | solution.py:46
  16.6 4.0 %collective-permute-start.3 = (bf16[208,256]{1,0:T(8,128)(2,1)}, bf16[208,256]{1,0:T(8,128)(2,1)S(1)}, u32[]{:S(2)}, u32[]{:S(2)}) collective-permute-start(bf16[208,256]{1,0:T(8,128)(2,1)} %bitcast.23), channel_id=1, source_target_pairs={{0,4},{1,5},{2,6},{3,7},{4,0},{5,1},{6,2},{7,3},{8,12},{9,13},{10,... | collective-permute-start | bytes 319496 | tf_op jit(solution)/shard_map/ppermute | solution.py:37
  20.8 2.6 %collective-permute-start.4 = (bf16[208,256]{1,0:T(8,128)(2,1)}, bf16[208,256]{1,0:T(8,128)(2,1)S(1)}, u32[]{:S(2)}, u32[]{:S(2)}) collective-permute-start(bf16[208,256]{1,0:T(8,128)(2,1)} %bitcast.24), channel_id=1, source_target_pairs={{0,5},{1,4},{2,7},{3,6},{4,1},{5,0},{6,3},{7,2},{8,13},{9,12},{10,... | collective-permute-start | bytes 319496 | tf_op jit(solution)/shard_map/ppermute | solution.py:37
  23.3 3.7 %collective-permute-start.5 = (bf16[208,256]{1,0:T(8,128)(2,1)}, bf16[208,256]{1,0:T(8,128)(2,1)S(1)}, u32[]{:S(2)}, u32[]{:S(2)}) collective-permute-start(bf16[208,256]{1,0:T(8,128)(2,1)} %bitcast.25), channel_id=1, source_target_pairs={{0,6},{1,7},{2,4},{3,5},{4,2},{5,3},{6,0},{7,1},{8,14},{9,15},{10,... | collective-permute-start | bytes 319496 | tf_op jit(solution)/shard_map/ppermute | solution.py:37
  27.0 3.9 %collective-permute-start.6 = (bf16[208,256]{1,0:T(8,128)(2,1)}, bf16[208,256]{1,0:T(8,128)(2,1)S(1)}, u32[]{:S(2)}, u32[]{:S(2)}) collective-permute-start(bf16[208,256]{1,0:T(8,128)(2,1)} %bitcast.26), channel_id=1, source_target_pairs={{0,7},{1,6},{2,5},{3,4},{4,3},{5,2},{6,1},{7,0},{8,15},{9,14},{10,... | collective-permute-start | bytes 319496 | tf_op jit(solution)/shard_map/ppermute | solution.py:37
  31.4 4.1 %collective-permute-done.6.refs_7_ = bf16[208,256]{1,0:T(8,128)(2,1)S(1)} collective-permute-done((bf16[208,256]{1,0:T(8,128)(2,1)}, bf16[208,256]{1,0:T(8,128)(2,1)S(1)}, u32[]{:S(2)}, u32[]{:S(2)}) %collective-permute-start.6) | collective-permute-done | bytes 106528 | tf_op jit(solution)/shard_map/ppermute | solution.py:37
  42.8 3.1 %collective-permute-done.11.refs_6_ = bf16[208,256]{1,0:T(8,128)(2,1)S(1)} collective-permute-done((bf16[208,256]{1,0:T(8,128)(2,1)S(1)}, bf16[208,256]{1,0:T(8,128)(2,1)S(1)}, u32[]{:S(2)}, u32[]{:S(2)}) %collective-permute-start.11) | collective-permute-done | bytes 106528 | tf_op jit(solution)/shard_map/ppermute | solution.py:37
  47.3 3.2 %collective-permute-start.7 = (bf16[208,256]{1,0:T(8,128)(2,1)S(1)}, bf16[208,256]{1,0:T(8,128)(2,1)S(1)}, u32[]{:S(2)}, u32[]{:S(2)}) collective-permute-start(bf16[208,256]{1,0:T(8,128)(2,1)S(1)} %get-tuple-element.27.refs_0_), channel_id=1, source_target_pairs={{0,32},{32,0},{64,96},{96,64},{1,33},{33,1},{65,97},{97,65},{2,34}... | collective-permute-start | bytes 319496 | tf_op jit(solution)/shard_map/ppermute | solution.py:37
  51.2 2.6 %collective-permute-done.7.refs_1_ = bf16[208,256]{1,0:T(8,128)(2,1)S(1)} collective-permute-done((bf16[208,256]{1,0:T(8,128)(2,1)S(1)}, bf16[208,256]{1,0:T(8,128)(2,1)S(1)}, u32[]{:S(2)}, u32[]{:S(2)}) %collective-permute-start.7) | collective-permute-done | bytes 106528 | tf_op jit(solution)/shard_map/ppermute | solution.py:37
  55.8 2.7 %collective-permute-done.8.refs_2_ = bf16[208,256]{1,0:T(8,128)(2,1)S(1)} collective-permute-done((bf16[208,256]{1,0:T(8,128)(2,1)S(1)}, bf16[208,256]{1,0:T(8,128)(2,1)S(1)}, u32[]{:S(2)}, u32[]{:S(2)}) %collective-permute-start.8) | collective-permute-done | bytes 106528 | tf_op jit(solution)/shard_map/ppermute | solution.py:37
  59.1 3.2 %collective-permute-start.9 = (bf16[208,256]{1,0:T(8,128)(2,1)S(1)}, bf16[208,256]{1,0:T(8,128)(2,1)S(1)}, u32[]{:S(2)}, u32[]{:S(2)}) collective-permute-start(bf16[208,256]{1,0:T(8,128)(2,1)S(1)} %get-tuple-element.27.refs_0_), channel_id=1, source_target_pairs={{0,96},{32,64},{64,32},{96,0},{1,97},{33,65},{65,33},{97,1},{2,98}... | collective-permute-start | bytes 319496 | tf_op jit(solution)/shard_map/ppermute | solution.py:37
  62.4 3.8 %collective-permute-done.9.refs_3_ = bf16[208,256]{1,0:T(8,128)(2,1)S(1)} collective-permute-done((bf16[208,256]{1,0:T(8,128)(2,1)S(1)}, bf16[208,256]{1,0:T(8,128)(2,1)S(1)}, u32[]{:S(2)}, u32[]{:S(2)}) %collective-permute-start.9) | collective-permute-done | bytes 106528 | tf_op jit(solution)/shard_map/ppermute | solution.py:37
  72.4 14.9 %attend.1 = (bf16[2,208,256]{2,1,0:T(8,128)(2,1)S(1)}, bf16[2,208,256]{2,1,0:T(8,128)(2,1)S(1)}, bf16[2,208,256]{2,1,0:T(8,128)(2,1)S(1)}, bf16[2,208,256]{2,1,0:T(8,128)(2,1)S(1)}) custom-call(s32[2]{0:T(128)S(1)} %pad_add_fusion.ids, s32[64]{0:T(128)S(1)} %pad_add_fusion.1.tab, f32[8,1152]{1,0:T(8,128)S(1)} %concatenate.31.kpos, f32[8,208,1]{2,1,0:T(8,128)} %copy.33.tq, ...), custom_call_target="tpu_custom_call" | custom-call | tf_op jit(solution)/shard_map/attend/pallas_call | solution.py:339
  87.3 6.8 %collective-permute-start.19 = (bf16[2,208,256]{2,1,0:T(8,128)(2,1)S(1)}, bf16[2,208,256]{2,1,0:T(8,128)(2,1)S(1)}, u32[]{:S(2)}, u32[]{:S(2)}) collective-permute-start(bf16[2,208,256]{2,1,0:T(8,128)(2,1)S(1)} %get-tuple-element.30), channel_id=1, source_target_pairs={{0,32},{32,0},{64,96},{96,64},{1,33},{33,1},{65,97},{97,65},{2,34}... | collective-permute-start | bytes 638984 | tf_op jit(solution)/shard_map/ppermute | solution.py:37
  95.6 4.1 %collective-permute-done.19.refs_1_ = bf16[2,208,256]{2,1,0:T(8,128)(2,1)S(1)} collective-permute-done((bf16[2,208,256]{2,1,0:T(8,128)(2,1)S(1)}, bf16[2,208,256]{2,1,0:T(8,128)(2,1)S(1)}, u32[]{:S(2)}, u32[]{:S(2)}) %collective-permute-start.19) | collective-permute-done | bytes 213024 | tf_op jit(solution)/shard_map/ppermute | solution.py:37
  101.4 2.6 %collective-permute-done.21.refs_3_ = bf16[2,208,256]{2,1,0:T(8,128)(2,1)S(1)} collective-permute-done((bf16[2,208,256]{2,1,0:T(8,128)(2,1)S(1)}, bf16[2,208,256]{2,1,0:T(8,128)(2,1)S(1)}, u32[]{:S(2)}, u32[]{:S(2)}) %collective-permute-start.21) | collective-permute-done | bytes 213024 | tf_op jit(solution)/shard_map/ppermute | solution.py:37
  106.8 3.5 %collective-permute-start.24 = (bf16[208,256]{1,0:T(8,128)(2,1)S(1)}, bf16[208,256]{1,0:T(8,128)(2,1)S(1)}, u32[]{:S(2)}, u32[]{:S(2)}) collective-permute-start(bf16[208,256]{1,0:T(8,128)(2,1)S(1)} %get-tuple-element.36), channel_id=1, source_target_pairs={{0,3},{1,2},{2,1},{3,0},{4,7},{5,6},{6,5},{7,4},{8,11},{9,10},{10,... | collective-permute-start | bytes 319496 | tf_op jit(solution)/shard_map/ppermute | solution.py:37
  111.5 3.3 %collective-permute-start.26 = (bf16[208,256]{1,0:T(8,128)(2,1)S(1)}, bf16[208,256]{1,0:T(8,128)(2,1)S(1)}, u32[]{:S(2)}, u32[]{:S(2)}) collective-permute-start(bf16[208,256]{1,0:T(8,128)(2,1)S(1)} %get-tuple-element.38), channel_id=1, source_target_pairs={{0,5},{1,4},{2,7},{3,6},{4,1},{5,0},{6,3},{7,2},{8,13},{9,12},{10,... | collective-permute-start | bytes 319496 | tf_op jit(solution)/shard_map/ppermute | solution.py:37
  114.8 3.1 %collective-permute-start.27 = (bf16[208,256]{1,0:T(8,128)(2,1)S(1)}, bf16[208,256]{1,0:T(8,128)(2,1)S(1)}, u32[]{:S(2)}, u32[]{:S(2)}) collective-permute-start(bf16[208,256]{1,0:T(8,128)(2,1)S(1)} %get-tuple-element.39), channel_id=1, source_target_pairs={{0,6},{1,7},{2,4},{3,5},{4,2},{5,3},{6,0},{7,1},{8,14},{9,15},{10,... | collective-permute-start | bytes 319496 | tf_op jit(solution)/shard_map/ppermute | solution.py:37
  120.8 3.1 %collective-permute-done.27 = bf16[208,256]{1,0:T(8,128)(2,1)S(1)} collective-permute-done((bf16[208,256]{1,0:T(8,128)(2,1)S(1)}, bf16[208,256]{1,0:T(8,128)(2,1)S(1)}, u32[]{:S(2)}, u32[]{:S(2)}) %collective-permute-start.27) | collective-permute-done | bytes 106528 | tf_op jit(solution)/shard_map/ppermute | solution.py:37
  123.8 2.3 %collective-permute-done.28 = bf16[208,256]{1,0:T(8,128)(2,1)S(1)} collective-permute-done((bf16[208,256]{1,0:T(8,128)(2,1)S(1)}, bf16[208,256]{1,0:T(8,128)(2,1)S(1)}, u32[]{:S(2)}, u32[]{:S(2)}) %collective-permute-start.28) | collective-permute-done | bytes 106528 | tf_op jit(solution)/shard_map/ppermute | solution.py:37
  127.1 4.2 %collective-permute-start.31 = (bf16[208,256]{1,0:T(8,128)(2,1)S(1)}, bf16[208,256]{1,0:T(8,128)(2,1)}, u32[]{:S(2)}, u32[]{:S(2)}) collective-permute-start(bf16[208,256]{1,0:T(8,128)(2,1)S(1)} %add_convert_fusion.1.refs_0_), channel_id=1, source_target_pairs={{0,3},{1,2},{2,1},{3,0},{4,7},{5,6},{6,5},{7,4},{8,11},{9,10},{10,... | collective-permute-start | bytes 319496 | tf_op jit(solution)/shard_map/ppermute | solution.py:37
  132.0 3.1 %collective-permute-start.33 = (bf16[208,256]{1,0:T(8,128)(2,1)S(1)}, bf16[208,256]{1,0:T(8,128)(2,1)}, u32[]{:S(2)}, u32[]{:S(2)}) collective-permute-start(bf16[208,256]{1,0:T(8,128)(2,1)S(1)} %add_convert_fusion.1.refs_0_), channel_id=1, source_target_pairs={{0,5},{1,4},{2,7},{3,6},{4,1},{5,0},{6,3},{7,2},{8,13},{9,12},{10,... | collective-permute-start | bytes 319496 | tf_op jit(solution)/shard_map/ppermute | solution.py:37
  136.6 4.0 %collective-permute-start.35 = (bf16[208,256]{1,0:T(8,128)(2,1)S(1)}, bf16[208,256]{1,0:T(8,128)(2,1)}, u32[]{:S(2)}, u32[]{:S(2)}) collective-permute-start(bf16[208,256]{1,0:T(8,128)(2,1)S(1)} %add_convert_fusion.1.refs_0_), channel_id=1, source_target_pairs={{0,7},{1,6},{2,5},{3,4},{4,3},{5,2},{6,1},{7,0},{8,15},{9,14},{10,... | collective-permute-start | bytes 319496 | tf_op jit(solution)/shard_map/ppermute | solution.py:37
  142.5 2.5 %collective-permute-done.35.refs_7_ = bf16[208,256]{1,0:T(8,128)(2,1)} collective-permute-done((bf16[208,256]{1,0:T(8,128)(2,1)S(1)}, bf16[208,256]{1,0:T(8,128)(2,1)}, u32[]{:S(2)}, u32[]{:S(2)}) %collective-permute-start.35) | collective-permute-done | bytes 106528 | tf_op jit(solution)/shard_map/ppermute | solution.py:37
  145.0 5.6 %feed.1 = (bf16[208,256]{1,0:T(8,128)(2,1)S(1)}, bf16[208,256]{1,0:T(8,128)(2,1)S(1)}, bf16[208,256]{1,0:T(8,128)(2,1)S(1)}, bf16[208,256]{1,0:T(8,128)(2,1)S(1)...) custom-call(s32[1]{0:T(128)} %bitcast.1.me_ref, ...), custom_call_target="tpu_custom_call" | custom-call | tf_op jit(solution)/shard_map/feed/pallas_call | solution.py:372
  150.6 2.5 %collective-permute-start.36 = (bf16[208,256]{1,0:T(8,128)(2,1)S(1)}, bf16[208,256]{1,0:T(8,128)(2,1)S(1)}, u32[]{:S(2)}, u32[]{:S(2)}) collective-permute-start(bf16[208,256]{1,0:T(8,128)(2,1)S(1)} %get-tuple-element.42), channel_id=1, source_target_pairs={{0,1},{1,0},{2,3},{3,2},{4,5},{5,4},{6,7},{7,6},{8,9},{9,8},{10,11... | collective-permute-start | bytes 319496 | tf_op jit(solution)/shard_map/ppermute | solution.py:37
  153.1 2.5 %collective-permute-start.38 = (bf16[208,256]{1,0:T(8,128)(2,1)S(1)}, bf16[208,256]{1,0:T(8,128)(2,1)S(1)}, u32[]{:S(2)}, u32[]{:S(2)}) collective-permute-start(bf16[208,256]{1,0:T(8,128)(2,1)S(1)} %get-tuple-element.44), channel_id=1, source_target_pairs={{0,3},{1,2},{2,1},{3,0},{4,7},{5,6},{6,5},{7,4},{8,11},{9,10},{10,... | collective-permute-start | bytes 319496 | tf_op jit(solution)/shard_map/ppermute | solution.py:37
  156.9 4.2 %collective-permute-start.40 = (bf16[208,256]{1,0:T(8,128)(2,1)S(1)}, bf16[208,256]{1,0:T(8,128)(2,1)S(1)}, u32[]{:S(2)}, u32[]{:S(2)}) collective-permute-start(bf16[208,256]{1,0:T(8,128)(2,1)S(1)} %get-tuple-element.46), channel_id=1, source_target_pairs={{0,5},{1,4},{2,7},{3,6},{4,1},{5,0},{6,3},{7,2},{8,13},{9,12},{10,... | collective-permute-start | bytes 319496 | tf_op jit(solution)/shard_map/ppermute | solution.py:37
  161.1 2.1 %collective-permute-start.41 = (bf16[208,256]{1,0:T(8,128)(2,1)S(1)}, bf16[208,256]{1,0:T(8,128)(2,1)S(1)}, u32[]{:S(2)}, u32[]{:S(2)}) collective-permute-start(bf16[208,256]{1,0:T(8,128)(2,1)S(1)} %get-tuple-element.47), channel_id=1, source_target_pairs={{0,6},{1,7},{2,4},{3,5},{4,2},{5,3},{6,0},{7,1},{8,14},{9,15},{10,... | collective-permute-start | bytes 319496 | tf_op jit(solution)/shard_map/ppermute | solution.py:37
  167.0 4.5 %collective-permute-done.42 = bf16[208,256]{1,0:T(8,128)(2,1)S(1)} collective-permute-done((bf16[208,256]{1,0:T(8,128)(2,1)S(1)}, bf16[208,256]{1,0:T(8,128)(2,1)S(1)}, u32[]{:S(2)}, u32[]{:S(2)}) %collective-permute-start.42) | collective-permute-done | bytes 106528 | tf_op jit(solution)/shard_map/ppermute | solution.py:37
  (122 shorter events, 51.1 us)
Async XLA Ops:
  0.0 16.6 %collective-permute-start = (bf16[208,256]{1,0:T(8,128)(2,1)}, bf16[208,256]{1,0:T(8,128)(2,1)S(1)}, u32[]{:S(2)}, u32[]{:S(2)}) collective-permute-start(bf16[208,256]{1,0:T(8,128)(2,1)} %bitcast.20), channel_id=1, source_target_pairs={{0,1},{1,0},{2,3},{3,2},{4,5},{5,4},{6,7},{7,6},{8,9},{9,8},{10,11... | collective-permute-start | bytes 319496 | tf_op jit(solution)/shard_map/ppermute | solution.py:37
  3.1 17.6 %collective-permute-start.1 = (bf16[208,256]{1,0:T(8,128)(2,1)}, bf16[208,256]{1,0:T(8,128)(2,1)S(1)}, u32[]{:S(2)}, u32[]{:S(2)}) collective-permute-start(bf16[208,256]{1,0:T(8,128)(2,1)} %bitcast.21), channel_id=1, source_target_pairs={{0,2},{1,3},{2,0},{3,1},{4,6},{5,7},{6,4},{7,5},{8,10},{9,11},{10,... | collective-permute-start | bytes 319496 | tf_op jit(solution)/shard_map/ppermute | solution.py:37
  5.0 18.3 %collective-permute-start.2 = (bf16[208,256]{1,0:T(8,128)(2,1)}, bf16[208,256]{1,0:T(8,128)(2,1)S(1)}, u32[]{:S(2)}, u32[]{:S(2)}) collective-permute-start(bf16[208,256]{1,0:T(8,128)(2,1)} %bitcast.22), channel_id=1, source_target_pairs={{0,3},{1,2},{2,1},{3,0},{4,7},{5,6},{6,5},{7,4},{8,11},{9,10},{10,... | collective-permute-start | bytes 319496 | tf_op jit(solution)/shard_map/ppermute | solution.py:37
  10.3 35.6 %collective-permute-start.14 = (bf16[2,1024,128]{2,1,0:T(8,128)(2,1)}, bf16[2,1024,128]{2,1,0:T(8,128)(2,1)}, u32[]{:S(2)}, u32[]{:S(2)}) collective-permute-start(bf16[2,1024,128]{2,1,0:T(8,128)(2,1)} %rotate_keys.1.refs_8_), channel_id=1, source_target_pairs={{0,16},{16,0},{1,17},{17,1},{2,18},{18,2},{3,19},{19,3},{4,20},{20... | collective-permute-start | bytes 1572872 | tf_op jit(solution)/shard_map/ppermute | solution.py:37
  11.9 34.5 %collective-permute-start.17 = (bf16[2,1024,128]{2,1,0:T(8,128)(2,1)}, bf16[2,1024,128]{2,1,0:T(8,128)(2,1)}, u32[]{:S(2)}, u32[]{:S(2)}) collective-permute-start(bf16[2,1024,128]{2,1,0:T(8,128)(2,1)} %refs_12_.1), channel_id=1, source_target_pairs={{0,16},{16,0},{1,17},{17,1},{2,18},{18,2},{3,19},{19,3},{4,20},{20... | collective-permute-start | bytes 1572872 | tf_op jit(solution)/shard_map/ppermute | solution.py:37
  16.6 10.4 %collective-permute-start.3 = (bf16[208,256]{1,0:T(8,128)(2,1)}, bf16[208,256]{1,0:T(8,128)(2,1)S(1)}, u32[]{:S(2)}, u32[]{:S(2)}) collective-permute-start(bf16[208,256]{1,0:T(8,128)(2,1)} %bitcast.23), channel_id=1, source_target_pairs={{0,4},{1,5},{2,6},{3,7},{4,0},{5,1},{6,2},{7,3},{8,12},{9,13},{10,... | collective-permute-start | bytes 319496 | tf_op jit(solution)/shard_map/ppermute | solution.py:37
  20.8 10.2 %collective-permute-start.4 = (bf16[208,256]{1,0:T(8,128)(2,1)}, bf16[208,256]{1,0:T(8,128)(2,1)S(1)}, u32[]{:S(2)}, u32[]{:S(2)}) collective-permute-start(bf16[208,256]{1,0:T(8,128)(2,1)} %bitcast.24), channel_id=1, source_target_pairs={{0,5},{1,4},{2,7},{3,6},{4,1},{5,0},{6,3},{7,2},{8,13},{9,12},{10,... | collective-permute-start | bytes 319496 | tf_op jit(solution)/shard_map/ppermute | solution.py:37
  27.0 8.5 %collective-permute-start.6 = (bf16[208,256]{1,0:T(8,128)(2,1)}, bf16[208,256]{1,0:T(8,128)(2,1)S(1)}, u32[]{:S(2)}, u32[]{:S(2)}) collective-permute-start(bf16[208,256]{1,0:T(8,128)(2,1)} %bitcast.26), channel_id=1, source_target_pairs={{0,7},{1,6},{2,5},{3,4},{4,3},{5,2},{6,1},{7,0},{8,15},{9,14},{10,... | collective-permute-start | bytes 319496 | tf_op jit(solution)/shard_map/ppermute | solution.py:37
  30.9 36.6 %collective-permute-start.13 = (bf16[2,1024,128]{2,1,0:T(8,128)(2,1)}, bf16[2,1024,128]{2,1,0:T(8,128)(2,1)}, u32[]{:S(2)}, u32[]{:S(2)}) collective-permute-start(bf16[2,1024,128]{2,1,0:T(8,128)(2,1)} %rotate_keys.1.refs_8_), channel_id=1, source_target_pairs={{0,8},{8,0},{1,9},{9,1},{2,10},{10,2},{3,11},{11,3},{4,12},{12,4},... | collective-permute-start | bytes 1572872 | tf_op jit(solution)/shard_map/ppermute | solution.py:37
  30.9 36.6 %collective-permute-start.16 = (bf16[2,1024,128]{2,1,0:T(8,128)(2,1)}, bf16[2,1024,128]{2,1,0:T(8,128)(2,1)}, u32[]{:S(2)}, u32[]{:S(2)}) collective-permute-start(bf16[2,1024,128]{2,1,0:T(8,128)(2,1)} %refs_12_.1), channel_id=1, source_target_pairs={{0,8},{8,0},{1,9},{9,1},{2,10},{10,2},{3,11},{11,3},{4,12},{12,4},... | collective-permute-start | bytes 1572872 | tf_op jit(solution)/shard_map/ppermute | solution.py:37
  45.9 21.7 %collective-permute-start.15 = (bf16[2,1024,128]{2,1,0:T(8,128)(2,1)}, bf16[2,1024,128]{2,1,0:T(8,128)(2,1)}, u32[]{:S(2)}, u32[]{:S(2)}) collective-permute-start(bf16[2,1024,128]{2,1,0:T(8,128)(2,1)} %collective-permute-done.14.refs_10_), channel_id=1, source_target_pairs={{0,8},{8,0},{1,9},{9,1},{2,10},{10,2},{3,11},{11,3},{4,12},{12,4},... | collective-permute-start | bytes 1572872 | tf_op jit(solution)/shard_map/ppermute | solution.py:37
  46.4 21.2 %collective-permute-start.18 = (bf16[2,1024,128]{2,1,0:T(8,128)(2,1)}, bf16[2,1024,128]{2,1,0:T(8,128)(2,1)}, u32[]{:S(2)}, u32[]{:S(2)}) collective-permute-start(bf16[2,1024,128]{2,1,0:T(8,128)(2,1)} %collective-permute-done.17.refs_14_), channel_id=1, source_target_pairs={{0,8},{8,0},{1,9},{9,1},{2,10},{10,2},{3,11},{11,3},{4,12},{12,4},... | collective-permute-start | bytes 1572872 | tf_op jit(solution)/shard_map/ppermute | solution.py:37
  87.3 12.4 %collective-permute-start.19 = (bf16[2,208,256]{2,1,0:T(8,128)(2,1)S(1)}, bf16[2,208,256]{2,1,0:T(8,128)(2,1)S(1)}, u32[]{:S(2)}, u32[]{:S(2)}) collective-permute-start(bf16[2,208,256]{2,1,0:T(8,128)(2,1)S(1)} %get-tuple-element.30), channel_id=1, source_target_pairs={{0,32},{32,0},{64,96},{96,64},{1,33},{33,1},{65,97},{97,65},{2,34}... | collective-permute-start | bytes 638984 | tf_op jit(solution)/shard_map/ppermute | solution.py:37
  94.0 9.9 %collective-permute-start.21 = (bf16[2,208,256]{2,1,0:T(8,128)(2,1)S(1)}, bf16[2,208,256]{2,1,0:T(8,128)(2,1)S(1)}, u32[]{:S(2)}, u32[]{:S(2)}) collective-permute-start(bf16[2,208,256]{2,1,0:T(8,128)(2,1)S(1)} %get-tuple-element.32), channel_id=1, source_target_pairs={{0,96},{32,64},{64,32},{96,0},{1,97},{33,65},{65,33},{97,1},{2,98}... | collective-permute-start | bytes 638984 | tf_op jit(solution)/shard_map/ppermute | solution.py:37
  105.0 9.7 %collective-permute-start.22 = (bf16[208,256]{1,0:T(8,128)(2,1)S(1)}, bf16[208,256]{1,0:T(8,128)(2,1)S(1)}, u32[]{:S(2)}, u32[]{:S(2)}) collective-permute-start(bf16[208,256]{1,0:T(8,128)(2,1)S(1)} %get-tuple-element.34), channel_id=1, source_target_pairs={{0,1},{1,0},{2,3},{3,2},{4,5},{5,4},{6,7},{7,6},{8,9},{9,8},{10,11... | collective-permute-start | bytes 319496 | tf_op jit(solution)/shard_map/ppermute | solution.py:37
  106.8 11.0 %collective-permute-start.23 = (bf16[208,256]{1,0:T(8,128)(2,1)S(1)}, bf16[208,256]{1,0:T(8,128)(2,1)S(1)}, u32[]{:S(2)}, u32[]{:S(2)}) collective-permute-start(bf16[208,256]{1,0:T(8,128)(2,1)S(1)} %get-tuple-element.35), channel_id=1, source_target_pairs={{0,2},{1,3},{2,0},{3,1},{4,6},{5,7},{6,4},{7,5},{8,10},{9,11},{10,... | collective-permute-start | bytes 319496 | tf_op jit(solution)/shard_map/ppermute | solution.py:37
  106.8 12.7 %collective-permute-start.24 = (bf16[208,256]{1,0:T(8,128)(2,1)S(1)}, bf16[208,256]{1,0:T(8,128)(2,1)S(1)}, u32[]{:S(2)}, u32[]{:S(2)}) collective-permute-start(bf16[208,256]{1,0:T(8,128)(2,1)S(1)} %get-tuple-element.36), channel_id=1, source_target_pairs={{0,3},{1,2},{2,1},{3,0},{4,7},{5,6},{6,5},{7,4},{8,11},{9,10},{10,... | collective-permute-start | bytes 319496 | tf_op jit(solution)/shard_map/ppermute | solution.py:37
  110.3 10.5 %collective-permute-start.25 = (bf16[208,256]{1,0:T(8,128)(2,1)S(1)}, bf16[208,256]{1,0:T(8,128)(2,1)S(1)}, u32[]{:S(2)}, u32[]{:S(2)}) collective-permute-start(bf16[208,256]{1,0:T(8,128)(2,1)S(1)} %get-tuple-element.37), channel_id=1, source_target_pairs={{0,4},{1,5},{2,6},{3,7},{4,0},{5,1},{6,2},{7,3},{8,12},{9,13},{10,... | collective-permute-start | bytes 319496 | tf_op jit(solution)/shard_map/ppermute | solution.py:37
  111.5 9.2 %collective-permute-start.26 = (bf16[208,256]{1,0:T(8,128)(2,1)S(1)}, bf16[208,256]{1,0:T(8,128)(2,1)S(1)}, u32[]{:S(2)}, u32[]{:S(2)}) collective-permute-start(bf16[208,256]{1,0:T(8,128)(2,1)S(1)} %get-tuple-element.38), channel_id=1, source_target_pairs={{0,5},{1,4},{2,7},{3,6},{4,1},{5,0},{6,3},{7,2},{8,13},{9,12},{10,... | collective-permute-start | bytes 319496 | tf_op jit(solution)/shard_map/ppermute | solution.py:37
  114.8 9.0 %collective-permute-start.27 = (bf16[208,256]{1,0:T(8,128)(2,1)S(1)}, bf16[208,256]{1,0:T(8,128)(2,1)S(1)}, u32[]{:S(2)}, u32[]{:S(2)}) collective-permute-start(bf16[208,256]{1,0:T(8,128)(2,1)S(1)} %get-tuple-element.39), channel_id=1, source_target_pairs={{0,6},{1,7},{2,4},{3,5},{4,2},{5,3},{6,0},{7,1},{8,14},{9,15},{10,... | collective-permute-start | bytes 319496 | tf_op jit(solution)/shard_map/ppermute | solution.py:37
  126.3 8.8 %collective-permute-start.29 = (bf16[208,256]{1,0:T(8,128)(2,1)S(1)}, bf16[208,256]{1,0:T(8,128)(2,1)S(1)}, u32[]{:S(2)}, u32[]{:S(2)}) collective-permute-start(bf16[208,256]{1,0:T(8,128)(2,1)S(1)} %add_convert_fusion.1.refs_0_), channel_id=1, source_target_pairs={{0,1},{1,0},{2,3},{3,2},{4,5},{5,4},{6,7},{7,6},{8,9},{9,8},{10,11... | collective-permute-start | bytes 319496 | tf_op jit(solution)/shard_map/ppermute | solution.py:37
  127.1 9.4 %collective-permute-start.30 = (bf16[208,256]{1,0:T(8,128)(2,1)S(1)}, bf16[208,256]{1,0:T(8,128)(2,1)S(1)}, u32[]{:S(2)}, u32[]{:S(2)}) collective-permute-start(bf16[208,256]{1,0:T(8,128)(2,1)S(1)} %add_convert_fusion.1.refs_0_), channel_id=1, source_target_pairs={{0,2},{1,3},{2,0},{3,1},{4,6},{5,7},{6,4},{7,5},{8,10},{9,11},{10,... | collective-permute-start | bytes 319496 | tf_op jit(solution)/shard_map/ppermute | solution.py:37
  127.1 13.4 %collective-permute-start.31 = (bf16[208,256]{1,0:T(8,128)(2,1)S(1)}, bf16[208,256]{1,0:T(8,128)(2,1)}, u32[]{:S(2)}, u32[]{:S(2)}) collective-permute-start(bf16[208,256]{1,0:T(8,128)(2,1)S(1)} %add_convert_fusion.1.refs_0_), channel_id=1, source_target_pairs={{0,3},{1,2},{2,1},{3,0},{4,7},{5,6},{6,5},{7,4},{8,11},{9,10},{10,... | collective-permute-start | bytes 319496 | tf_op jit(solution)/shard_map/ppermute | solution.py:37
  131.4 9.2 %collective-permute-start.32 = (bf16[208,256]{1,0:T(8,128)(2,1)S(1)}, bf16[208,256]{1,0:T(8,128)(2,1)}, u32[]{:S(2)}, u32[]{:S(2)}) collective-permute-start(bf16[208,256]{1,0:T(8,128)(2,1)S(1)} %add_convert_fusion.1.refs_0_), channel_id=1, source_target_pairs={{0,4},{1,5},{2,6},{3,7},{4,0},{5,1},{6,2},{7,3},{8,12},{9,13},{10,... | collective-permute-start | bytes 319496 | tf_op jit(solution)/shard_map/ppermute | solution.py:37
  132.0 9.4 %collective-permute-start.33 = (bf16[208,256]{1,0:T(8,128)(2,1)S(1)}, bf16[208,256]{1,0:T(8,128)(2,1)}, u32[]{:S(2)}, u32[]{:S(2)}) collective-permute-start(bf16[208,256]{1,0:T(8,128)(2,1)S(1)} %add_convert_fusion.1.refs_0_), channel_id=1, source_target_pairs={{0,5},{1,4},{2,7},{3,6},{4,1},{5,0},{6,3},{7,2},{8,13},{9,12},{10,... | collective-permute-start | bytes 319496 | tf_op jit(solution)/shard_map/ppermute | solution.py:37
  136.6 8.4 %collective-permute-start.35 = (bf16[208,256]{1,0:T(8,128)(2,1)S(1)}, bf16[208,256]{1,0:T(8,128)(2,1)}, u32[]{:S(2)}, u32[]{:S(2)}) collective-permute-start(bf16[208,256]{1,0:T(8,128)(2,1)S(1)} %add_convert_fusion.1.refs_0_), channel_id=1, source_target_pairs={{0,7},{1,6},{2,5},{3,4},{4,3},{5,2},{6,1},{7,0},{8,15},{9,14},{10,... | collective-permute-start | bytes 319496 | tf_op jit(solution)/shard_map/ppermute | solution.py:37
  150.6 10.5 %collective-permute-start.36 = (bf16[208,256]{1,0:T(8,128)(2,1)S(1)}, bf16[208,256]{1,0:T(8,128)(2,1)S(1)}, u32[]{:S(2)}, u32[]{:S(2)}) collective-permute-start(bf16[208,256]{1,0:T(8,128)(2,1)S(1)} %get-tuple-element.42), channel_id=1, source_target_pairs={{0,1},{1,0},{2,3},{3,2},{4,5},{5,4},{6,7},{7,6},{8,9},{9,8},{10,11... | collective-permute-start | bytes 319496 | tf_op jit(solution)/shard_map/ppermute | solution.py:37
  153.1 10.1 %collective-permute-start.37 = (bf16[208,256]{1,0:T(8,128)(2,1)S(1)}, bf16[208,256]{1,0:T(8,128)(2,1)S(1)}, u32[]{:S(2)}, u32[]{:S(2)}) collective-permute-start(bf16[208,256]{1,0:T(8,128)(2,1)S(1)} %get-tuple-element.43), channel_id=1, source_target_pairs={{0,2},{1,3},{2,0},{3,1},{4,6},{5,7},{6,4},{7,5},{8,10},{9,11},{10,... | collective-permute-start | bytes 319496 | tf_op jit(solution)/shard_map/ppermute | solution.py:37
  153.1 11.7 %collective-permute-start.38 = (bf16[208,256]{1,0:T(8,128)(2,1)S(1)}, bf16[208,256]{1,0:T(8,128)(2,1)S(1)}, u32[]{:S(2)}, u32[]{:S(2)}) collective-permute-start(bf16[208,256]{1,0:T(8,128)(2,1)S(1)} %get-tuple-element.44), channel_id=1, source_target_pairs={{0,3},{1,2},{2,1},{3,0},{4,7},{5,6},{6,5},{7,4},{8,11},{9,10},{10,... | collective-permute-start | bytes 319496 | tf_op jit(solution)/shard_map/ppermute | solution.py:37
  155.7 9.2 %collective-permute-start.39 = (bf16[208,256]{1,0:T(8,128)(2,1)S(1)}, bf16[208,256]{1,0:T(8,128)(2,1)S(1)}, u32[]{:S(2)}, u32[]{:S(2)}) collective-permute-start(bf16[208,256]{1,0:T(8,128)(2,1)S(1)} %get-tuple-element.45), channel_id=1, source_target_pairs={{0,4},{1,5},{2,6},{3,7},{4,0},{5,1},{6,2},{7,3},{8,12},{9,13},{10,... | collective-permute-start | bytes 319496 | tf_op jit(solution)/shard_map/ppermute | solution.py:37
  156.9 8.6 %collective-permute-start.40 = (bf16[208,256]{1,0:T(8,128)(2,1)S(1)}, bf16[208,256]{1,0:T(8,128)(2,1)S(1)}, u32[]{:S(2)}, u32[]{:S(2)}) collective-permute-start(bf16[208,256]{1,0:T(8,128)(2,1)S(1)} %get-tuple-element.46), channel_id=1, source_target_pairs={{0,5},{1,4},{2,7},{3,6},{4,1},{5,0},{6,3},{7,2},{8,13},{9,12},{10,... | collective-permute-start | bytes 319496 | tf_op jit(solution)/shard_map/ppermute | solution.py:37
  163.2 8.3 %collective-permute-start.42 = (bf16[208,256]{1,0:T(8,128)(2,1)S(1)}, bf16[208,256]{1,0:T(8,128)(2,1)S(1)}, u32[]{:S(2)}, u32[]{:S(2)}) collective-permute-start(bf16[208,256]{1,0:T(8,128)(2,1)S(1)} %get-tuple-element.48), channel_id=1, source_target_pairs={{0,7},{1,6},{2,5},{3,4},{4,3},{5,2},{6,1},{7,0},{8,15},{9,14},{10,... | collective-permute-start | bytes 319496 | tf_op jit(solution)/shard_map/ppermute | solution.py:37
  (28 other events, 388.3 us)

commit v2 on v1

--- a/solution.py
+++ b/solution.py
@@ -14,6 +14,8 @@
 FAR = 1e9
 TP = ("z", "xhi")
 SEQ = ("xlo", "yhi", "ylo", "core")
+ROUND = ("xlo", "yhi", "ylo")
+FAR_MASKS = (3, 4, 7)
 VMEM = pl.BlockSpec(memory_space=pltpu.VMEM)
 SMEM = pl.BlockSpec(memory_space=pltpu.SMEM)
 ANY = pl.BlockSpec(memory_space=pl.ANY)
@@ -33,28 +35,36 @@
     return values * cosine + pltpu.roll(values, values.shape[-1] // 2, values.ndim - 1) * sine
 
 
+def grant(mib):
+    return pltpu.CompilerParams(vmem_limit_bytes=mib << 20)
+
+
 def swap(x, axes, mask, size):
     return lax.ppermute(x, axes, [(i, i ^ mask) for i in range(size)])
 
 
-def rotate_keys_kernel(k_ref, c_ref, s_ref, o_ref):
-    o_ref[0] = rotate(k_ref[0].astype(F32), c_ref[0], s_ref[0]).astype(BF16)
-
-
-def rotate_keys(keys, cosine, sine):
+def rotate_keys_kernel(k_ref, v_ref, c_ref, s_ref, o_ref):
+    hd = k_ref.shape[2]
+    o_ref[0, :, :hd] = rotate(k_ref[0].astype(F32), c_ref[0], s_ref[0]).astype(BF16)
+    o_ref[0, :, hd:] = v_ref[0]
+
+
+def rotate_keys(keys, values, cosine, sine):
     slots, span, hd = keys.shape
     return pl.pallas_call(
         rotate_keys_kernel,
         grid=(slots,),
         in_specs=[
             pl.BlockSpec((1, span, hd), lambda i: (i, 0, 0)),
+            pl.BlockSpec((1, span, hd), lambda i: (i, 0, 0)),
             pl.BlockSpec((1, 1, hd), lambda i: (i, 0, 0)),
             pl.BlockSpec((1, 1, hd), lambda i: (i, 0, 0)),
         ],
-        out_specs=pl.BlockSpec((1, span, hd), lambda i: (i, 0, 0)),
-        out_shape=jax.ShapeDtypeStruct(keys.shape, BF16),
+        out_specs=pl.BlockSpec((1, span, 2 * hd), lambda i: (i, 0, 0)),
+        out_shape=jax.ShapeDtypeStruct((slots, span, 2 * hd), BF16),
+        compiler_params=grant(8),
         name="rotate_keys",
-    )(keys, cosine, sine)
+    )(keys, values, cosine, sine)
 
 
 def scale_of(pieces, width):
@@ -69,12 +79,12 @@
 
 
 def project_kernel(n, me_ref, *refs):
-    pieces = refs[:n]
-    gain, wq, wk, wv, qg, kg, cos, sin, q_out, kv_out = refs[n:]
+    pairs = refs[: n // 2]
+    gain, wq, wk, wv, qg, kg, cos, sin, q_out, kv_out = refs[n // 2 :]
     me = me_ref[0]
-    width = pieces[0].shape[1]
+    width = pairs[0].shape[2]
     hd = qg.shape[1]
-    xs = [p[...].astype(F32) for p in pieces]
+    xs = [p[i].astype(F32) for p in pairs for i in range(2)]
     scale = scale_of(xs, n * width)
     q = k = v = None
     for step in range(n):
@@ -93,21 +103,29 @@
     kv_out[:, hd:] = v.astype(BF16)
 
 
-def attend_kernel(count, ids, tab, kpos, tq, *refs):
-    q_in, kv_in, k_in, v_in = refs[0:4], refs[4:8], refs[8:12], refs[12:16]
-    outs = refs[16:20]
-    keys, values, queries, run_m, run_l, run_acc, sems = refs[20:]
+def identity(rows, cols, period):
+    row = lax.broadcasted_iota(jnp.int32, (rows, cols), 0)
+    col = lax.broadcasted_iota(jnp.int32, (rows, cols), 1)
+    return jnp.where(lax.rem(row, period) == col, 1.0, 0.0).astype(BF16)
+
+
+def attend_kernel(count, ids, tab, kpos, q_index, *refs):
+    q_in, kv_in, cached = refs[0:4], refs[4:8], refs[8:12]
+    outs = refs[12:16]
+    keys, values, queries, tq, run_m, run_l, run_acc, sems = refs[16:]
     hd = keys.shape[2]
-    span = k_in[0].shape[1]
+    span = cached[0].shape[1]
     slots = keys.shape[0]
     place_at = tab.shape[0] // 2
     xy, mk = ids[0], ids[1]
     copies = []
     for p in range(4):
-        for which, (src, dst) in enumerate(((k_in[p], keys), (v_in[p], values))):
+        for which, dst in enumerate((keys, values)):
             copies.append(
                 pltpu.make_async_copy(
-                    src, dst.at[pl.ds(2 * p, 2), pl.ds(0, span), :], sems.at[which, p]
+                    cached[p].at[:, :, pl.ds(which * hd, hd)],
+                    dst.at[pl.ds(2 * p, 2), pl.ds(0, span), :],
+                    sems.at[which, p],
                 )
             )
     for c in copies:
@@ -121,13 +139,27 @@
             values[2 * p + j, span:, :] = jnp.concatenate([fresh[:, hd:], zero], 0)
             rows = q_in[p][j * count : (j + 1) * count, :]
             queries[2 * p + j] = jnp.concatenate([rows[:, :hd], rows[:, hd:]], 0)
+    index = q_index[...].astype(F32)
+    upper = jnp.floor(index * 0.125)
+    digits = jnp.concatenate([upper, index - 8.0 * upper], 0).astype(BF16)
+    columns = lax.dot_general(
+        identity(2 * count, count, count),
+        digits,
+        (((1,), (1,)), ((), ())),
+        preferred_element_type=F32,
+    )
+    for q in range(slots):
+        tq[q] = 8.0 * columns[:, q : q + 1] + columns[:, slots + q : slots + q + 1]
+    turn = identity(2 * count, 2 * hd, 4 * count)
     for c in copies:
         c.wait()
     factor = hd**-0.5
 
     def one_query(qi, _):
-        q_nat = jnp.bitwise_xor(xy, qi // 2)
-        q_slot = q_nat * 8 + mk * 2 + qi % 2
+        p = qi // 2
+        q_nat = jnp.bitwise_xor(xy, p)
+        q_mk = jnp.bitwise_xor(mk, (p % 2) * 2)
+        q_slot = q_nat * 8 + q_mk * 2 + qi % 2
         q_req, q_place = tab[q_slot], tab[place_at + q_slot]
         run_m[...] = jnp.full(run_m.shape, NEG, F32)
         run_l[...] = jnp.zeros(run_l.shape, F32)
@@ -141,7 +173,7 @@
             @pl.when(jnp.logical_and(k_req == q_req, k_place <= q_place))
             def _():
                 limit = jnp.where(k_place < q_place, 65536.0, 0.0)
-                bound = tq[q_nat * 2 + qi % 2] + limit
+                bound = tq[qi] + limit
                 scores = lax.dot_general(
                     queries[qi], keys[ki], (((1,), (1,)), ((), ())), preferred_element_type=F32
                 )
@@ -174,11 +206,14 @@
             high.astype(F32),
             jnp.where(lane == 1, mid.astype(F32), jnp.where(lane == 2, low.astype(F32), 0.0)),
         ).astype(BF16)
-        for p in range(4):
-
-            @pl.when(qi // 2 == p)
-            def _(p=p):
-                outs[p][qi % 2] = jnp.concatenate([out, stats], axis=1)
+        flat = lax.dot_general(
+            stats, turn, (((0,), (0,)), ((), ())), preferred_element_type=F32
+        )[:8].astype(BF16)
+        for dest in range(4):
+
+            @pl.when(p == dest)
+            def _(dest=dest):
+                outs[dest][qi % 2] = jnp.concatenate([out, flat[:, :hd], flat[:, hd:]], axis=0)
 
         return 0
 
@@ -188,19 +223,29 @@
 def merge_kernel(n, count, me_ref, *refs):
     parts, wo, outs = refs[:4], refs[4], refs[5:]
     me = me_ref[0]
-    hd = parts[0].shape[2] // 2
+    hd = parts[0].shape[2]
     width = outs[0].shape[1]
+    turn = identity(2 * count, 2 * hd, 4 * count)
     rows = [[], []]
     for j in range(2):
         lses = []
         for part in parts:
-            st = part[j, :, hd:].astype(F32)
+            flat = part[j, 2 * count :, :]
+            st = sum(
+                lax.dot_general(
+                    turn[:, i * hd : (i + 1) * hd],
+                    flat,
+                    (((1,), (1,)), ((), ())),
+                    preferred_element_type=F32,
+                )[:, 8 * i : 8 * i + 8]
+                for i in range(2)
+            )
             lses.append(st[:, 0:1] + st[:, 1:2] + st[:, 2:3])
         top = functools.reduce(jnp.maximum, lses)
         total = acc = None
         for lse, part in zip(lses, parts):
             w = jnp.exp(lse - top)
-            term = w * part[j, :, :hd].astype(F32)
+            term = w * part[j, : 2 * count, :].astype(F32)
             total, acc = (w, term) if total is None else (total + w, acc + term)
         acc = acc / total
         for h in range(2):
@@ -261,7 +306,6 @@
     rows = slot_local * count
     spans = span_order.shape[1]
     n = 8
-    params = pltpu.CompilerParams(vmem_limit_bytes=48 << 20)
 
     def shaped(*shape, dtype=BF16):
         return jax.ShapeDtypeStruct(shape, dtype)
@@ -271,55 +315,31 @@
     me = lax.axis_index(TP).reshape(1)
     first_slot = lax.axis_index(SEQ) * slot_local
 
-    hit = slot_spans[:, None] == jnp.arange(span_order.size, dtype=jnp.int32)[None, :]
-    place = jnp.sum(jnp.where(hit, span_order.reshape(-1)[None, :], 0), axis=1)
-    start = jnp.sum(jnp.where(hit, cache_start.reshape(-1)[None, :], 0), axis=1)
+    number = lax.broadcasted_iota(jnp.int32, span_order.shape, 0) * spans
+    number = number + lax.broadcasted_iota(jnp.int32, span_order.shape, 1)
+    hit = slot_spans[:, None, None] == number[None]
+    place = jnp.sum(jnp.where(hit, span_order[None], 0), axis=(1, 2))
+    start = jnp.sum(jnp.where(hit, cache_start[None], 0), axis=(1, 2))
     table = jnp.concatenate([slot_spans // spans, place])
     ids = jnp.stack([xy, mk])
     base_here = lax.dynamic_slice_in_dim(place * span, first_slot, slot_local, 0)
     start_here = lax.dynamic_slice_in_dim(start, first_slot, slot_local, 0)
-    index_here = lax.dynamic_slice_in_dim(selected_index, first_slot, slot_local, 0)
 
     hidden = selected_hidden.reshape(rows, width)
-    pieces = [hidden] + [swap(hidden, TP, k, n) for k in range(1, n)]
+    pair = jnp.stack([hidden, swap(hidden, "xhi", 1, 2)])
+
+    pair, selected_later, input_gain, post_gain = lax.optimization_barrier(
+        (pair, selected_index, input_gain, post_gain)
+    )
+    pairs = [pair] + [swap(pair, "z", k, 4) for k in (1, 2, 3)]
 
     kc, ks = rotation_tables(base_here - start_here, hd)
-    keys = rotate_keys(cached_keys, kc[:, None, :], ks[:, None, :])
-    keys_y = swap(keys, "ylo", 1, 2)
-    values_y = swap(cached_values, "ylo", 1, 2)
-    key_set = [keys, swap(keys, "core", 1, 2), keys_y, swap(keys_y, "core", 1, 2)]
-    value_set = [
-        cached_values,
-        swap(cached_values, "core", 1, 2),
-        values_y,
-        swap(values_y, "core", 1, 2),
-    ]
-
+    cached = rotate_keys(cached_keys, cached_values, kc[:, None, :], ks[:, None, :])
+    cached_y = swap(cached, "ylo", 1, 2)
+
+    index_here = lax.dynamic_slice_in_dim(selected_later, first_slot, slot_local, 0)
     qc, qs = rotation_tables((base_here[:, None] + index_here).reshape(-1), hd)
-    queries, fresh = pl.pallas_call(
-        functools.partial(project_kernel, n),
-        in_specs=[SMEM] + [VMEM] * (n + 8),
-        out_specs=[VMEM, VMEM],
-        out_shape=[shaped(rows, query_weight.shape[1]), shaped(rows, 2 * hd)],
-        compiler_params=params,
-        name="project",
-    )(
-        me,
-        *pieces,
-        input_gain.astype(F32).reshape(n, width),
-        query_weight,
-        key_weight,
-        value_weight,
-        query_gain.astype(F32)[None],
-        key_gain.astype(F32)[None],
-        qc,
-        qs,
-    )
-    fresh_y = swap(fresh, "ylo", 1, 2)
-    fresh_set = [fresh, swap(fresh, "core", 1, 2), fresh_y, swap(fresh_y, "core", 1, 2)]
-    query_set = [queries] + [swap(queries, ("xlo", "yhi"), k, 4) for k in (1, 2, 3)]
-
-    group_index = lax.dynamic_slice_in_dim(selected_index, xy * 8, 8, 0)
+    group_index = lax.dynamic_slice_in_dim(selected_later, xy * 8, 8, 0)
     token = jnp.arange(span, dtype=jnp.int32)
     taken = jnp.any(group_index[:, :, None] == token[None, None, :], axis=1)
     kpos = jnp.concatenate(
@@ -330,37 +350,77 @@
         ],
         axis=1,
     )
-    query_index = lax.dynamic_slice_in_dim(
-        selected_index.reshape(4, 4, slot_local, count), mk, 1, 1
-    ).reshape(8, count)
-    tq = jnp.concatenate([query_index, query_index], axis=1).astype(F32)[:, :, None]
+    seq = lax.axis_index(SEQ)
+    query_index = jnp.concatenate(
+        [
+            lax.dynamic_slice_in_dim(
+                selected_later, jnp.bitwise_xor(seq, 2 * k) * slot_local, slot_local, 0
+            )
+            for k in (0,) + FAR_MASKS
+        ],
+        axis=0,
+    )
+
+    input_gain = input_gain.astype(F32).reshape(n, width)
+    post_gain = post_gain.astype(F32).reshape(n, width)
+    qg, kg = query_gain.astype(F32)[None], key_gain.astype(F32)[None]
+    pairs[0], input_gain, post_gain, qg, kg, qc, qs, ids, table, kpos, query_index = (
+        lax.optimization_barrier(
+            (pairs[0], input_gain, post_gain, qg, kg, qc, qs, ids, table, kpos, query_index)
+        )
+    )
+    queries, fresh = pl.pallas_call(
+        functools.partial(project_kernel, n),
+        in_specs=[SMEM] + [VMEM] * (n // 2 + 8),
+        out_specs=[VMEM, VMEM],
+        out_shape=[shaped(rows, query_weight.shape[1]), shaped(rows, 2 * hd)],
+        compiler_params=grant(10),
+        name="project",
+    )(
+        me,
+        *pairs,
+        input_gain,
+        query_weight,
+        key_weight,
+        value_weight,
+        qg,
+        kg,
+        qc,
+        qs,
+    )
+    cached_y = lax.optimization_barrier((cached_y, fresh))[0]
+    cached_set = [cached, swap(cached, "core", 1, 2), cached_y, swap(cached_y, "core", 1, 2)]
+    fresh_y = swap(fresh, "ylo", 1, 2)
+    fresh_set = [fresh, swap(fresh, "core", 1, 2), fresh_y, swap(fresh_y, "core", 1, 2)]
+    query_set = [queries] + [swap(queries, ROUND, k, 8) for k in FAR_MASKS]
 
     key_rows = span + 128
     parts = pl.pallas_call(
         functools.partial(attend_kernel, count),
-        in_specs=[SMEM, SMEM, VMEM, VMEM] + [VMEM] * 8 + [ANY] * 8,
+        in_specs=[SMEM, SMEM, VMEM, VMEM] + [VMEM] * 8 + [ANY] * 4,
         out_specs=[VMEM] * 4,
-        out_shape=[shaped(slot_local, 2 * count, 2 * hd)] * 4,
+        out_shape=[shaped(slot_local, 2 * count + 16, hd)] * 4,
         scratch_shapes=[
             pltpu.VMEM((8, key_rows, hd), BF16),
             pltpu.VMEM((8, key_rows, hd), BF16),
             pltpu.VMEM((8, 2 * count, hd), BF16),
+            pltpu.VMEM((8, 2 * count, 1), F32),
             pltpu.VMEM((2 * count, 1), F32),
             pltpu.VMEM((2 * count, 1), F32),
             pltpu.VMEM((2 * count, hd), F32),
             pltpu.SemaphoreType.DMA((2, 4)),
         ],
-        compiler_params=params,
+        compiler_params=grant(18),
         name="attend",
-    )(ids, table, kpos, tq, *query_set, *fresh_set, *key_set, *value_set)
-    parts = [parts[0]] + [swap(parts[k], ("xlo", "yhi"), k, 4) for k in (1, 2, 3)]
+    )(ids, table, kpos, query_index, *query_set, *fresh_set, *cached_set)
+    parts = [parts[0]] + [swap(part, ROUND, k, 8) for part, k in zip(parts[1:], FAR_MASKS)]
 
     projected = pl.pallas_call(
         functools.partial(merge_kernel, n, count),
         in_specs=[SMEM] + [VMEM] * 5,
         out_specs=[VMEM] * n,
         out_shape=[shaped(rows, width)] * n,
-        compiler_params=params,
+        compiler_params=grant(8),
         name="merge",
     )(me, *parts, output_weight)
     total = hidden.astype(F32) + projected[0].astype(F32)
@@ -374,12 +434,12 @@
         in_specs=[SMEM] + [VMEM] * (n + 4),
         out_specs=[VMEM] * n,
         out_shape=[shaped(rows, width)] * n,
-        compiler_params=params,
+        compiler_params=grant(18),
         name="feed",
     )(
         me,
         *pieces,
-        post_gain.astype(F32).reshape(n, width),
+        post_gain,
         gate_weight,
         up_weight,
         down_weight,

time: 173 us -> 140 us (0.81); the launches traced: 172 us -> 141 us
  starting transfers between devices: 82.2 us -> 71.3 us
  local copies, waits for them, and re-layouts: 14 us -> 5.75 us
  Pallas kernels: 24.9 us -> 17.1 us
  waiting for transfers between devices: 44.5 us -> 39.4 us
    ppermute x43 -> x37, starting transfers between devices: 82.2 us -> 71.3 us  [swap(): return lax.ppermute(x, axes, [(i, i ^ mask) for i in range(size)])]
    unnamed x34 -> x20, local copies, waits for them, and re-layouts: 9.62 us -> 4.2 us
    ppermute x43 -> x37, waiting for transfers between devices: 44.5 us -> 39.4 us  [swap(): return lax.ppermute(x, axes, [(i, i ^ mask) for i in range(size)])]
    pallas_call x1, Pallas kernels: 14.9 us -> 9.85 us  [on_device(): pl.pallas_call(functools.partial(attend_kernel, count), in_specs=[SMEM, S...]
    pallas_call x1, Pallas kernels: 5.59 us -> 2.48 us  [on_device(): pl.pallas_call(functools.partial(feed_kernel, n), in_specs=[SMEM] + [VMEM...]
  transfers between devices with their start and end apart: 43 -> 37, of which waited for: 19 -> 15; matrix products, arithmetic and copies ran while one was open for 6% -> 5% of each run, Pallas kernels for 2% -> 2%
where the time goes in v2:
time: 140 us; the launch traced here: 141 us
  starting transfers between devices  71.3 us (51%)
  waiting for transfers between devices  39.4 us (28%)
  Pallas kernels  17.1 us (12%)
  other arithmetic  7.58 us (5%)
  local copies, waits for them, and re-layouts  5.75 us (4%)
    ppermute x37, starting transfers between devices, swap(): return lax.ppermute(x, axes, [(i, i ^ mask) for i in range(size)])  71.3 us
    ppermute x37, waiting for transfers between devices, swap(): return lax.ppermute(x, axes, [(i, i ^ mask) for i in range(size)])  39.4 us
    pallas_call x1, Pallas kernels, on_device(): pl.pallas_call(functools.partial(attend_kernel, count), in_specs=[SMEM, S...  9.85 us
    unnamed x20, local copies, waits for them, and re-layouts  4.2 us
  transfers between devices with their start and end apart: 37, of which 15 were waited for; matrix products, arithmetic and copies ran while one was open for 5% of the time, Pallas kernels for 2%

profile of v2, /device:TPU:0, one launch (start us, length us, event | category | flops | bytes accessed | tf_op | source)
XLA Modules:
  0.0 141.4 jit_solution(15797266848461387589)
XLA Ops:
  5.5 3.0 %collective-permute-start = (bf16[208,256]{1,0:T(8,128)(2,1)}, bf16[208,256]{1,0:T(8,128)(2,1)S(1)}, u32[]{:S(2)}, u32[]{:S(2)}) collective-permute-start(bf16[208,256]{1,0:T(8,128)(2,1)} %bitcast.20), channel_id=1, source_target_pairs={{0,1},{1,0},{2,3},{3,2},{4,5},{5,4},{6,7},{7,6},{8,9},{9,8},{10,11... | collective-permute-start | bytes 319496 | tf_op jit(solution)/shard_map/ppermute | solution.py:43
  10.1 2.6 %collective-permute-done = bf16[208,256]{1,0:T(8,128)(2,1)S(1)} collective-permute-done((bf16[208,256]{1,0:T(8,128)(2,1)}, bf16[208,256]{1,0:T(8,128)(2,1)S(1)}, u32[]{:S(2)}, u32[]{:S(2)}) %collective-permute-start) | collective-permute-done | bytes 106528 | tf_op jit(solution)/shard_map/ppermute | solution.py:43
  13.6 4.1 %collective-permute-start.3 = (bf16[2,208,256]{2,1,0:T(8,128)(2,1)S(1)}, bf16[2,208,256]{2,1,0:T(8,128)(2,1)}, u32[]{:S(2)}, u32[]{:S(2)}) collective-permute-start(bf16[2,208,256]{2,1,0:T(8,128)(2,1)S(1)} %pad_maximum_fusion.refs_0_), channel_id=1, source_target_pairs={{0,6},{2,4},{4,2},{6,0},{1,7},{3,5},{5,3},{7,1},{8,14},{10,12},{12... | collective-permute-start | bytes 638984 | tf_op jit(solution)/shard_map/ppermute | solution.py:43
  23.2 4.3 %collective-permute-done.3.refs_3_ = bf16[2,208,256]{2,1,0:T(8,128)(2,1)} collective-permute-done((bf16[2,208,256]{2,1,0:T(8,128)(2,1)S(1)}, bf16[2,208,256]{2,1,0:T(8,128)(2,1)}, u32[]{:S(2)}, u32[]{:S(2)}) %collective-permute-start.3) | collective-permute-done | bytes 213024 | tf_op jit(solution)/shard_map/ppermute | solution.py:43
  30.3 2.7 %project.1 = (bf16[208,256]{1,0:T(8,128)(2,1)S(1)}, bf16[208,256]{1,0:T(8,128)(2,1)S(1)}) custom-call(s32[1]{0:T(128)} %bitcast.1.me_ref, bf16[2,208,256]{2,1,0:T(8,128)(2,1)S(1)} %pad_maximum_fusion.refs_0_, bf16[2,208,256]{2,1,0:T(8,128)(2,1)} %collective-permute-done.1.refs_1_, bf16[2,208,256]{2,1,0:T(8,128)(2,1)} %collective-permute-done.2.refs_2_, ...), custom_call_target="tpu_custom_call" | custom-call | tf_op jit(solution)/shard_map/project/pallas_call | solution.py:372
  33.1 3.2 %collective-permute-start.6 = (bf16[208,256]{1,0:T(8,128)(2,1)S(1)}, bf16[208,256]{1,0:T(8,128)(2,1)S(1)}, u32[]{:S(2)}, u32[]{:S(2)}) collective-permute-start(bf16[208,256]{1,0:T(8,128)(2,1)S(1)} %get-tuple-element.57.refs_0_), channel_id=1, source_target_pairs={{0,112},{16,96},{32,80},{48,64},{64,48},{80,32},{96,16},{112,0},{1... | collective-permute-start | bytes 319496 | tf_op jit(solution)/shard_map/ppermute | solution.py:43
  37.5 3.6 %collective-permute-done.6.refs_3_ = bf16[208,256]{1,0:T(8,128)(2,1)S(1)} collective-permute-done((bf16[208,256]{1,0:T(8,128)(2,1)S(1)}, bf16[208,256]{1,0:T(8,128)(2,1)S(1)}, u32[]{:S(2)}, u32[]{:S(2)}) %collective-permute-start.6) | collective-permute-done | bytes 106528 | tf_op jit(solution)/shard_map/ppermute | solution.py:43
  41.1 2.2 %collective-permute-start.4 = (bf16[208,256]{1,0:T(8,128)(2,1)S(1)}, bf16[208,256]{1,0:T(8,128)(2,1)S(1)}, u32[]{:S(2)}, u32[]{:S(2)}) collective-permute-start(bf16[208,256]{1,0:T(8,128)(2,1)S(1)} %get-tuple-element.57.refs_0_), channel_id=1, source_target_pairs={{0,48},{16,32},{32,16},{48,0},{64,112},{80,96},{96,80},{112,64},{1... | collective-permute-start | bytes 319496 | tf_op jit(solution)/shard_map/ppermute | solution.py:43
  43.8 3.2 %collective-permute-done.4.refs_1_ = bf16[208,256]{1,0:T(8,128)(2,1)S(1)} collective-permute-done((bf16[208,256]{1,0:T(8,128)(2,1)S(1)}, bf16[208,256]{1,0:T(8,128)(2,1)S(1)}, u32[]{:S(2)}, u32[]{:S(2)}) %collective-permute-start.4) | collective-permute-done | bytes 106528 | tf_op jit(solution)/shard_map/ppermute | solution.py:43
  47.1 9.8 %attend.1 = (bf16[2,224,128]{2,1,0:T(8,128)(2,1)S(1)}, bf16[2,224,128]{2,1,0:T(8,128)(2,1)S(1)}, bf16[2,224,128]{2,1,0:T(8,128)(2,1)S(1)}, bf16[2,224,128]{2,1,0:T(8,128)(2,1)S(1)}) custom-call(s32[2]{0:T(128)S(1)} %pad_add_fusion.1.ids, s32[64]{0:T(128)S(1)} %pad_add_fusion.2.tab, f32[8,1152]{1,0:T(8,128)S(1)} %concatenate.24.kpos, ...), custom_call_target="tpu_custom_call" | custom-call | tf_op jit(solution)/shard_map/attend/pallas_call | solution.py:398
  56.9 9.2 %collective-permute-start.13 = (bf16[2,224,128]{2,1,0:T(8,128)(2,1)S(1)}, bf16[2,224,128]{2,1,0:T(8,128)(2,1)S(1)}, u32[]{:S(2)}, u32[]{:S(2)}) collective-permute-start(bf16[2,224,128]{2,1,0:T(8,128)(2,1)S(1)} %get-tuple-element.61), channel_id=1, source_target_pairs={{0,48},{16,32},{32,16},{48,0},{64,112},{80,96},{96,80},{112,64},{1... | collective-permute-start | bytes 344072 | tf_op jit(solution)/shard_map/ppermute | solution.py:43
  66.1 2.4 %collective-permute-start.14 = (bf16[2,224,128]{2,1,0:T(8,128)(2,1)S(1)}, bf16[2,224,128]{2,1,0:T(8,128)(2,1)S(1)}, u32[]{:S(2)}, u32[]{:S(2)}) collective-permute-start(bf16[2,224,128]{2,1,0:T(8,128)(2,1)S(1)} %get-tuple-element.62), channel_id=1, source_target_pairs={{0,64},{16,80},{32,96},{48,112},{64,0},{80,16},{96,32},{112,48},{1... | collective-permute-start | bytes 344072 | tf_op jit(solution)/shard_map/ppermute | solution.py:43
  69.5 2.0 %collective-permute-done.14.refs_2_ = bf16[2,224,128]{2,1,0:T(8,128)(2,1)S(1)} collective-permute-done((bf16[2,224,128]{2,1,0:T(8,128)(2,1)S(1)}, bf16[2,224,128]{2,1,0:T(8,128)(2,1)S(1)}, u32[]{:S(2)}, u32[]{:S(2)}) %collective-permute-start.14) | collective-permute-done | bytes 114720 | tf_op jit(solution)/shard_map/ppermute | solution.py:43
  71.5 3.8 %collective-permute-done.15.refs_3_ = bf16[2,224,128]{2,1,0:T(8,128)(2,1)S(1)} collective-permute-done((bf16[2,224,128]{2,1,0:T(8,128)(2,1)S(1)}, bf16[2,224,128]{2,1,0:T(8,128)(2,1)S(1)}, u32[]{:S(2)}, u32[]{:S(2)}) %collective-permute-start.15) | collective-permute-done | bytes 114720 | tf_op jit(solution)/shard_map/ppermute | solution.py:43
  77.0 2.8 %collective-permute-start.16 = (bf16[208,256]{1,0:T(8,128)(2,1)S(1)}, bf16[208,256]{1,0:T(8,128)(2,1)S(1)}, u32[]{:S(2)}, u32[]{:S(2)}) collective-permute-start(bf16[208,256]{1,0:T(8,128)(2,1)S(1)} %get-tuple-element.65), channel_id=1, source_target_pairs={{0,1},{1,0},{2,3},{3,2},{4,5},{5,4},{6,7},{7,6},{8,9},{9,8},{10,11... | collective-permute-start | bytes 319496 | tf_op jit(solution)/shard_map/ppermute | solution.py:43
  82.1 2.7 %collective-permute-start.19 = (bf16[208,256]{1,0:T(8,128)(2,1)S(1)}, bf16[208,256]{1,0:T(8,128)(2,1)S(1)}, u32[]{:S(2)}, u32[]{:S(2)}) collective-permute-start(bf16[208,256]{1,0:T(8,128)(2,1)S(1)} %get-tuple-element.68), channel_id=1, source_target_pairs={{0,4},{1,5},{2,6},{3,7},{4,0},{5,1},{6,2},{7,3},{8,12},{9,13},{10,... | collective-permute-start | bytes 319496 | tf_op jit(solution)/shard_map/ppermute | solution.py:43
  84.8 3.0 %collective-permute-start.20 = (bf16[208,256]{1,0:T(8,128)(2,1)S(1)}, bf16[208,256]{1,0:T(8,128)(2,1)S(1)}, u32[]{:S(2)}, u32[]{:S(2)}) collective-permute-start(bf16[208,256]{1,0:T(8,128)(2,1)S(1)} %get-tuple-element.69), channel_id=1, source_target_pairs={{0,5},{1,4},{2,7},{3,6},{4,1},{5,0},{6,3},{7,2},{8,13},{9,12},{10,... | collective-permute-start | bytes 319496 | tf_op jit(solution)/shard_map/ppermute | solution.py:43
  87.8 2.9 %collective-permute-start.21 = (bf16[208,256]{1,0:T(8,128)(2,1)S(1)}, bf16[208,256]{1,0:T(8,128)(2,1)S(1)}, u32[]{:S(2)}, u32[]{:S(2)}) collective-permute-start(bf16[208,256]{1,0:T(8,128)(2,1)S(1)} %get-tuple-element.70), channel_id=1, source_target_pairs={{0,6},{1,7},{2,4},{3,5},{4,2},{5,3},{6,0},{7,1},{8,14},{9,15},{10,... | collective-permute-start | bytes 319496 | tf_op jit(solution)/shard_map/ppermute | solution.py:43
  91.3 2.2 %collective-permute-done.20 = bf16[208,256]{1,0:T(8,128)(2,1)S(1)} collective-permute-done((bf16[208,256]{1,0:T(8,128)(2,1)S(1)}, bf16[208,256]{1,0:T(8,128)(2,1)S(1)}, u32[]{:S(2)}, u32[]{:S(2)}) %collective-permute-start.20) | collective-permute-done | bytes 106528 | tf_op jit(solution)/shard_map/ppermute | solution.py:43
  94.6 5.6 %collective-permute-done.22 = bf16[208,256]{1,0:T(8,128)(2,1)S(1)} collective-permute-done((bf16[208,256]{1,0:T(8,128)(2,1)S(1)}, bf16[208,256]{1,0:T(8,128)(2,1)S(1)}, u32[]{:S(2)}, u32[]{:S(2)}) %collective-permute-start.22) | collective-permute-done | bytes 106528 | tf_op jit(solution)/shard_map/ppermute | solution.py:43
  100.9 2.7 %collective-permute-start.28 = (bf16[208,256]{1,0:T(8,128)(2,1)S(1)}, bf16[208,256]{1,0:T(8,128)(2,1)S(1)}, u32[]{:S(2)}, u32[]{:S(2)}) collective-permute-start(bf16[208,256]{1,0:T(8,128)(2,1)S(1)} %add_convert_fusion.1.refs_0_), channel_id=1, source_target_pairs={{0,6},{1,7},{2,4},{3,5},{4,2},{5,3},{6,0},{7,1},{8,14},{9,15},{10,... | collective-permute-start | bytes 319496 | tf_op jit(solution)/shard_map/ppermute | solution.py:43
  103.8 5.7 %collective-permute-start.26 = (bf16[208,256]{1,0:T(8,128)(2,1)S(1)}, bf16[208,256]{1,0:T(8,128)(2,1)S(1)}, u32[]{:S(2)}, u32[]{:S(2)}) collective-permute-start(bf16[208,256]{1,0:T(8,128)(2,1)S(1)} %add_convert_fusion.1.refs_0_), channel_id=1, source_target_pairs={{0,4},{1,5},{2,6},{3,7},{4,0},{5,1},{6,2},{7,3},{8,12},{9,13},{10,... | collective-permute-start | bytes 319496 | tf_op jit(solution)/shard_map/ppermute | solution.py:43
  109.5 2.1 %collective-permute-start.24 = (bf16[208,256]{1,0:T(8,128)(2,1)S(1)}, bf16[208,256]{1,0:T(8,128)(2,1)S(1)}, u32[]{:S(2)}, u32[]{:S(2)}) collective-permute-start(bf16[208,256]{1,0:T(8,128)(2,1)S(1)} %add_convert_fusion.1.refs_0_), channel_id=1, source_target_pairs={{0,2},{1,3},{2,0},{3,1},{4,6},{5,7},{6,4},{7,5},{8,10},{9,11},{10,... | collective-permute-start | bytes 319496 | tf_op jit(solution)/shard_map/ppermute | solution.py:43
  111.6 2.9 %collective-permute-start.23 = (bf16[208,256]{1,0:T(8,128)(2,1)S(1)}, bf16[208,256]{1,0:T(8,128)(2,1)S(1)}, u32[]{:S(2)}, u32[]{:S(2)}) collective-permute-start(bf16[208,256]{1,0:T(8,128)(2,1)S(1)} %add_convert_fusion.1.refs_0_), channel_id=1, source_target_pairs={{0,1},{1,0},{2,3},{3,2},{4,5},{5,4},{6,7},{7,6},{8,9},{9,8},{10,11... | collective-permute-start | bytes 319496 | tf_op jit(solution)/shard_map/ppermute | solution.py:43
  114.5 2.2 %collective-permute-done.25.refs_3_ = bf16[208,256]{1,0:T(8,128)(2,1)S(1)} collective-permute-done((bf16[208,256]{1,0:T(8,128)(2,1)S(1)}, bf16[208,256]{1,0:T(8,128)(2,1)S(1)}, u32[]{:S(2)}, u32[]{:S(2)}) %collective-permute-start.25) | collective-permute-done | bytes 106528 | tf_op jit(solution)/shard_map/ppermute | solution.py:43
  118.1 2.5 %feed.1 = (bf16[208,256]{1,0:T(8,128)(2,1)S(1)}, bf16[208,256]{1,0:T(8,128)(2,1)S(1)}, bf16[208,256]{1,0:T(8,128)(2,1)S(1)}, bf16[208,256]{1,0:T(8,128)(2,1)S(1)...) custom-call(s32[1]{0:T(128)} %bitcast.1.me_ref, ...), custom_call_target="tpu_custom_call" | custom-call | tf_op jit(solution)/shard_map/feed/pallas_call | solution.py:432
  120.5 2.8 %collective-permute-start.30 = (bf16[208,256]{1,0:T(8,128)(2,1)S(1)}, bf16[208,256]{1,0:T(8,128)(2,1)S(1)}, u32[]{:S(2)}, u32[]{:S(2)}) collective-permute-start(bf16[208,256]{1,0:T(8,128)(2,1)S(1)} %get-tuple-element.74), channel_id=1, source_target_pairs={{0,1},{1,0},{2,3},{3,2},{4,5},{5,4},{6,7},{7,6},{8,9},{9,8},{10,11... | collective-permute-start | bytes 319496 | tf_op jit(solution)/shard_map/ppermute | solution.py:43
  123.4 2.2 %collective-permute-start.32 = (bf16[208,256]{1,0:T(8,128)(2,1)S(1)}, bf16[208,256]{1,0:T(8,128)(2,1)S(1)}, u32[]{:S(2)}, u32[]{:S(2)}) collective-permute-start(bf16[208,256]{1,0:T(8,128)(2,1)S(1)} %get-tuple-element.76), channel_id=1, source_target_pairs={{0,3},{1,2},{2,1},{3,0},{4,7},{5,6},{6,5},{7,4},{8,11},{9,10},{10,... | collective-permute-start | bytes 319496 | tf_op jit(solution)/shard_map/ppermute | solution.py:43
  125.9 5.4 %collective-permute-start.34 = (bf16[208,256]{1,0:T(8,128)(2,1)S(1)}, bf16[208,256]{1,0:T(8,128)(2,1)S(1)}, u32[]{:S(2)}, u32[]{:S(2)}) collective-permute-start(bf16[208,256]{1,0:T(8,128)(2,1)S(1)} %get-tuple-element.78), channel_id=1, source_target_pairs={{0,5},{1,4},{2,7},{3,6},{4,1},{5,0},{6,3},{7,2},{8,13},{9,12},{10,... | collective-permute-start | bytes 319496 | tf_op jit(solution)/shard_map/ppermute | solution.py:43
  132.3 2.5 %collective-permute-start.36 = (bf16[208,256]{1,0:T(8,128)(2,1)S(1)}, bf16[208,256]{1,0:T(8,128)(2,1)S(1)}, u32[]{:S(2)}, u32[]{:S(2)}) collective-permute-start(bf16[208,256]{1,0:T(8,128)(2,1)S(1)} %get-tuple-element.80), channel_id=1, source_target_pairs={{0,7},{1,6},{2,5},{3,4},{4,3},{5,2},{6,1},{7,0},{8,15},{9,14},{10,... | collective-permute-start | bytes 319496 | tf_op jit(solution)/shard_map/ppermute | solution.py:43
  134.8 2.4 %collective-permute-done.35 = bf16[208,256]{1,0:T(8,128)(2,1)S(1)} collective-permute-done((bf16[208,256]{1,0:T(8,128)(2,1)S(1)}, bf16[208,256]{1,0:T(8,128)(2,1)S(1)}, u32[]{:S(2)}, u32[]{:S(2)}) %collective-permute-start.35) | collective-permute-done | bytes 106528 | tf_op jit(solution)/shard_map/ppermute | solution.py:43
  137.2 3.4 %collective-permute-done.36 = bf16[208,256]{1,0:T(8,128)(2,1)S(1)} collective-permute-done((bf16[208,256]{1,0:T(8,128)(2,1)S(1)}, bf16[208,256]{1,0:T(8,128)(2,1)S(1)}, u32[]{:S(2)}, u32[]{:S(2)}) %collective-permute-start.36) | collective-permute-done | bytes 106528 | tf_op jit(solution)/shard_map/ppermute | solution.py:43
  (95 shorter events, 29.2 us)
Async XLA Ops:
  3.8 29.2 %collective-permute-start.11 = (bf16[2,1024,256]{2,1,0:T(8,128)(2,1)S(1)}, bf16[2,1024,256]{2,1,0:T(8,128)(2,1)S(1)}, u32[]{:S(2)}, u32[]{:S(2)}) collective-permute-start(bf16[2,1024,256]{2,1,0:T(8,128)(2,1)S(1)} %rotate_keys.1.refs_8_), channel_id=1, source_target_pairs={{0,16},{16,0},{1,17},{17,1},{2,18},{18,2},{3,19},{19,3},{4,20},{20... | collective-permute-start | bytes 3145736 | tf_op jit(solution)/shard_map/ppermute | solution.py:43
  5.5 41.5 %collective-permute-start.10 = (bf16[2,1024,256]{2,1,0:T(8,128)(2,1)S(1)}, bf16[2,1024,256]{2,1,0:T(8,128)(2,1)}, u32[]{:S(2)}, u32[]{:S(2)}) collective-permute-start(bf16[2,1024,256]{2,1,0:T(8,128)(2,1)S(1)} %rotate_keys.1.refs_8_), channel_id=1, source_target_pairs={{0,8},{8,0},{1,9},{9,1},{2,10},{10,2},{3,11},{11,3},{4,12},{12,4},... | collective-permute-start | bytes 3145736 | tf_op jit(solution)/shard_map/ppermute | solution.py:43
  5.5 7.1 %collective-permute-start = (bf16[208,256]{1,0:T(8,128)(2,1)}, bf16[208,256]{1,0:T(8,128)(2,1)S(1)}, u32[]{:S(2)}, u32[]{:S(2)}) collective-permute-start(bf16[208,256]{1,0:T(8,128)(2,1)} %bitcast.20), channel_id=1, source_target_pairs={{0,1},{1,0},{2,3},{3,2},{4,5},{5,4},{6,7},{7,6},{8,9},{9,8},{10,11... | collective-permute-start | bytes 319496 | tf_op jit(solution)/shard_map/ppermute | solution.py:43
  13.6 13.9 %collective-permute-start.3 = (bf16[2,208,256]{2,1,0:T(8,128)(2,1)S(1)}, bf16[2,208,256]{2,1,0:T(8,128)(2,1)}, u32[]{:S(2)}, u32[]{:S(2)}) collective-permute-start(bf16[2,208,256]{2,1,0:T(8,128)(2,1)S(1)} %pad_maximum_fusion.refs_0_), channel_id=1, source_target_pairs={{0,6},{2,4},{4,2},{6,0},{1,7},{3,5},{5,3},{7,1},{8,14},{10,12},{12... | collective-permute-start | bytes 638984 | tf_op jit(solution)/shard_map/ppermute | solution.py:43
  17.7 9.8 %collective-permute-start.2 = (bf16[2,208,256]{2,1,0:T(8,128)(2,1)S(1)}, bf16[2,208,256]{2,1,0:T(8,128)(2,1)}, u32[]{:S(2)}, u32[]{:S(2)}) collective-permute-start(bf16[2,208,256]{2,1,0:T(8,128)(2,1)S(1)} %pad_maximum_fusion.refs_0_), channel_id=1, source_target_pairs={{0,4},{2,6},{4,0},{6,2},{1,5},{3,7},{5,1},{7,3},{8,12},{10,14},{12... | collective-permute-start | bytes 638984 | tf_op jit(solution)/shard_map/ppermute | solution.py:43
  17.7 10.5 %collective-permute-start.1 = (bf16[2,208,256]{2,1,0:T(8,128)(2,1)S(1)}, bf16[2,208,256]{2,1,0:T(8,128)(2,1)}, u32[]{:S(2)}, u32[]{:S(2)}) collective-permute-start(bf16[2,208,256]{2,1,0:T(8,128)(2,1)S(1)} %pad_maximum_fusion.refs_0_), channel_id=1, source_target_pairs={{0,2},{2,0},{4,6},{6,4},{1,3},{3,1},{5,7},{7,5},{8,10},{10,8},{12,... | collective-permute-start | bytes 638984 | tf_op jit(solution)/shard_map/ppermute | solution.py:43
  33.0 14.1 %collective-permute-start.12 = (bf16[2,1024,256]{2,1,0:T(8,128)(2,1)S(1)}, bf16[2,1024,256]{2,1,0:T(8,128)(2,1)S(1)}, u32[]{:S(2)}, u32[]{:S(2)}) collective-permute-start(bf16[2,1024,256]{2,1,0:T(8,128)(2,1)S(1)} %collective-permute-done.11.refs_10_), channel_id=1, source_target_pairs={{0,8},{8,0},{1,9},{9,1},{2,10},{10,2},{3,11},{11,3},{4,12},{12,4},... | collective-permute-start | bytes 3145736 | tf_op jit(solution)/shard_map/ppermute | solution.py:43
  33.1 8.0 %collective-permute-start.6 = (bf16[208,256]{1,0:T(8,128)(2,1)S(1)}, bf16[208,256]{1,0:T(8,128)(2,1)S(1)}, u32[]{:S(2)}, u32[]{:S(2)}) collective-permute-start(bf16[208,256]{1,0:T(8,128)(2,1)S(1)} %get-tuple-element.57.refs_0_), channel_id=1, source_target_pairs={{0,112},{16,96},{32,80},{48,64},{64,48},{80,32},{96,16},{112,0},{1... | collective-permute-start | bytes 319496 | tf_op jit(solution)/shard_map/ppermute | solution.py:43
  36.3 7.0 %collective-permute-start.5 = (bf16[208,256]{1,0:T(8,128)(2,1)S(1)}, bf16[208,256]{1,0:T(8,128)(2,1)S(1)}, u32[]{:S(2)}, u32[]{:S(2)}) collective-permute-start(bf16[208,256]{1,0:T(8,128)(2,1)S(1)} %get-tuple-element.57.refs_0_), channel_id=1, source_target_pairs={{0,64},{16,80},{32,96},{48,112},{64,0},{80,16},{96,32},{112,48},{1... | collective-permute-start | bytes 319496 | tf_op jit(solution)/shard_map/ppermute | solution.py:43
  36.9 6.4 %collective-permute-start.8 = (bf16[208,256]{1,0:T(8,128)(2,1)S(1)}, bf16[208,256]{1,0:T(8,128)(2,1)S(1)}, u32[]{:S(2)}, u32[]{:S(2)}) collective-permute-start(bf16[208,256]{1,0:T(8,128)(2,1)S(1)} %get-tuple-element.58.refs_4_), channel_id=1, source_target_pairs={{0,16},{16,0},{1,17},{17,1},{2,18},{18,2},{3,19},{19,3},{4,20},{20... | collective-permute-start | bytes 319496 | tf_op jit(solution)/shard_map/ppermute | solution.py:43
  56.9 12.6 %collective-permute-start.13 = (bf16[2,224,128]{2,1,0:T(8,128)(2,1)S(1)}, bf16[2,224,128]{2,1,0:T(8,128)(2,1)S(1)}, u32[]{:S(2)}, u32[]{:S(2)}) collective-permute-start(bf16[2,224,128]{2,1,0:T(8,128)(2,1)S(1)} %get-tuple-element.61), channel_id=1, source_target_pairs={{0,48},{16,32},{32,16},{48,0},{64,112},{80,96},{96,80},{112,64},{1... | collective-permute-start | bytes 344072 | tf_op jit(solution)/shard_map/ppermute | solution.py:43
  68.5 6.9 %collective-permute-start.15 = (bf16[2,224,128]{2,1,0:T(8,128)(2,1)S(1)}, bf16[2,224,128]{2,1,0:T(8,128)(2,1)S(1)}, u32[]{:S(2)}, u32[]{:S(2)}) collective-permute-start(bf16[2,224,128]{2,1,0:T(8,128)(2,1)S(1)} %get-tuple-element.63), channel_id=1, source_target_pairs={{0,112},{16,96},{32,80},{48,64},{64,48},{80,32},{96,16},{112,0},{1... | collective-permute-start | bytes 344072 | tf_op jit(solution)/shard_map/ppermute | solution.py:43
  77.0 10.8 %collective-permute-start.16 = (bf16[208,256]{1,0:T(8,128)(2,1)S(1)}, bf16[208,256]{1,0:T(8,128)(2,1)S(1)}, u32[]{:S(2)}, u32[]{:S(2)}) collective-permute-start(bf16[208,256]{1,0:T(8,128)(2,1)S(1)} %get-tuple-element.65), channel_id=1, source_target_pairs={{0,1},{1,0},{2,3},{3,2},{4,5},{5,4},{6,7},{7,6},{8,9},{9,8},{10,11... | collective-permute-start | bytes 319496 | tf_op jit(solution)/shard_map/ppermute | solution.py:43
  79.8 10.8 %collective-permute-start.17 = (bf16[208,256]{1,0:T(8,128)(2,1)S(1)}, bf16[208,256]{1,0:T(8,128)(2,1)S(1)}, u32[]{:S(2)}, u32[]{:S(2)}) collective-permute-start(bf16[208,256]{1,0:T(8,128)(2,1)S(1)} %get-tuple-element.66), channel_id=1, source_target_pairs={{0,2},{1,3},{2,0},{3,1},{4,6},{5,7},{6,4},{7,5},{8,10},{9,11},{10,... | collective-permute-start | bytes 319496 | tf_op jit(solution)/shard_map/ppermute | solution.py:43
  80.9 10.4 %collective-permute-start.18 = (bf16[208,256]{1,0:T(8,128)(2,1)S(1)}, bf16[208,256]{1,0:T(8,128)(2,1)S(1)}, u32[]{:S(2)}, u32[]{:S(2)}) collective-permute-start(bf16[208,256]{1,0:T(8,128)(2,1)S(1)} %get-tuple-element.67), channel_id=1, source_target_pairs={{0,3},{1,2},{2,1},{3,0},{4,7},{5,6},{6,5},{7,4},{8,11},{9,10},{10,... | collective-permute-start | bytes 319496 | tf_op jit(solution)/shard_map/ppermute | solution.py:43
  82.1 9.2 %collective-permute-start.19 = (bf16[208,256]{1,0:T(8,128)(2,1)S(1)}, bf16[208,256]{1,0:T(8,128)(2,1)S(1)}, u32[]{:S(2)}, u32[]{:S(2)}) collective-permute-start(bf16[208,256]{1,0:T(8,128)(2,1)S(1)} %get-tuple-element.68), channel_id=1, source_target_pairs={{0,4},{1,5},{2,6},{3,7},{4,0},{5,1},{6,2},{7,3},{8,12},{9,13},{10,... | collective-permute-start | bytes 319496 | tf_op jit(solution)/shard_map/ppermute | solution.py:43
  84.8 8.7 %collective-permute-start.20 = (bf16[208,256]{1,0:T(8,128)(2,1)S(1)}, bf16[208,256]{1,0:T(8,128)(2,1)S(1)}, u32[]{:S(2)}, u32[]{:S(2)}) collective-permute-start(bf16[208,256]{1,0:T(8,128)(2,1)S(1)} %get-tuple-element.69), channel_id=1, source_target_pairs={{0,5},{1,4},{2,7},{3,6},{4,1},{5,0},{6,3},{7,2},{8,13},{9,12},{10,... | collective-permute-start | bytes 319496 | tf_op jit(solution)/shard_map/ppermute | solution.py:43
  87.8 6.8 %collective-permute-start.21 = (bf16[208,256]{1,0:T(8,128)(2,1)S(1)}, bf16[208,256]{1,0:T(8,128)(2,1)S(1)}, u32[]{:S(2)}, u32[]{:S(2)}) collective-permute-start(bf16[208,256]{1,0:T(8,128)(2,1)S(1)} %get-tuple-element.70), channel_id=1, source_target_pairs={{0,6},{1,7},{2,4},{3,5},{4,2},{5,3},{6,0},{7,1},{8,14},{9,15},{10,... | collective-permute-start | bytes 319496 | tf_op jit(solution)/shard_map/ppermute | solution.py:43
  90.7 9.5 %collective-permute-start.22 = (bf16[208,256]{1,0:T(8,128)(2,1)S(1)}, bf16[208,256]{1,0:T(8,128)(2,1)S(1)}, u32[]{:S(2)}, u32[]{:S(2)}) collective-permute-start(bf16[208,256]{1,0:T(8,128)(2,1)S(1)} %get-tuple-element.71), channel_id=1, source_target_pairs={{0,7},{1,6},{2,5},{3,4},{4,3},{5,2},{6,1},{7,0},{8,15},{9,14},{10,... | collective-permute-start | bytes 319496 | tf_op jit(solution)/shard_map/ppermute | solution.py:43
  100.3 9.3 %collective-permute-start.29 = (bf16[208,256]{1,0:T(8,128)(2,1)S(1)}, bf16[208,256]{1,0:T(8,128)(2,1)S(1)}, u32[]{:S(2)}, u32[]{:S(2)}) collective-permute-start(bf16[208,256]{1,0:T(8,128)(2,1)S(1)} %add_convert_fusion.1.refs_0_), channel_id=1, source_target_pairs={{0,7},{1,6},{2,5},{3,4},{4,3},{5,2},{6,1},{7,0},{8,15},{9,14},{10,... | collective-permute-start | bytes 319496 | tf_op jit(solution)/shard_map/ppermute | solution.py:43
  100.9 10.7 %collective-permute-start.28 = (bf16[208,256]{1,0:T(8,128)(2,1)S(1)}, bf16[208,256]{1,0:T(8,128)(2,1)S(1)}, u32[]{:S(2)}, u32[]{:S(2)}) collective-permute-start(bf16[208,256]{1,0:T(8,128)(2,1)S(1)} %add_convert_fusion.1.refs_0_), channel_id=1, source_target_pairs={{0,6},{1,7},{2,4},{3,5},{4,2},{5,3},{6,0},{7,1},{8,14},{9,15},{10,... | collective-permute-start | bytes 319496 | tf_op jit(solution)/shard_map/ppermute | solution.py:43
  103.6 10.9 %collective-permute-start.27 = (bf16[208,256]{1,0:T(8,128)(2,1)S(1)}, bf16[208,256]{1,0:T(8,128)(2,1)S(1)}, u32[]{:S(2)}, u32[]{:S(2)}) collective-permute-start(bf16[208,256]{1,0:T(8,128)(2,1)S(1)} %add_convert_fusion.1.refs_0_), channel_id=1, source_target_pairs={{0,5},{1,4},{2,7},{3,6},{4,1},{5,0},{6,3},{7,2},{8,13},{9,12},{10,... | collective-permute-start | bytes 319496 | tf_op jit(solution)/shard_map/ppermute | solution.py:43
  103.8 10.7 %collective-permute-start.26 = (bf16[208,256]{1,0:T(8,128)(2,1)S(1)}, bf16[208,256]{1,0:T(8,128)(2,1)S(1)}, u32[]{:S(2)}, u32[]{:S(2)}) collective-permute-start(bf16[208,256]{1,0:T(8,128)(2,1)S(1)} %add_convert_fusion.1.refs_0_), channel_id=1, source_target_pairs={{0,4},{1,5},{2,6},{3,7},{4,0},{5,1},{6,2},{7,3},{8,12},{9,13},{10,... | collective-permute-start | bytes 319496 | tf_op jit(solution)/shard_map/ppermute | solution.py:43
  109.5 7.2 %collective-permute-start.25 = (bf16[208,256]{1,0:T(8,128)(2,1)S(1)}, bf16[208,256]{1,0:T(8,128)(2,1)S(1)}, u32[]{:S(2)}, u32[]{:S(2)}) collective-permute-start(bf16[208,256]{1,0:T(8,128)(2,1)S(1)} %add_convert_fusion.1.refs_0_), channel_id=1, source_target_pairs={{0,3},{1,2},{2,1},{3,0},{4,7},{5,6},{6,5},{7,4},{8,11},{9,10},{10,... | collective-permute-start | bytes 319496 | tf_op jit(solution)/shard_map/ppermute | solution.py:43
  109.5 7.2 %collective-permute-start.24 = (bf16[208,256]{1,0:T(8,128)(2,1)S(1)}, bf16[208,256]{1,0:T(8,128)(2,1)S(1)}, u32[]{:S(2)}, u32[]{:S(2)}) collective-permute-start(bf16[208,256]{1,0:T(8,128)(2,1)S(1)} %add_convert_fusion.1.refs_0_), channel_id=1, source_target_pairs={{0,2},{1,3},{2,0},{3,1},{4,6},{5,7},{6,4},{7,5},{8,10},{9,11},{10,... | collective-permute-start | bytes 319496 | tf_op jit(solution)/shard_map/ppermute | solution.py:43
  111.6 6.4 %collective-permute-start.23 = (bf16[208,256]{1,0:T(8,128)(2,1)S(1)}, bf16[208,256]{1,0:T(8,128)(2,1)S(1)}, u32[]{:S(2)}, u32[]{:S(2)}) collective-permute-start(bf16[208,256]{1,0:T(8,128)(2,1)S(1)} %add_convert_fusion.1.refs_0_), channel_id=1, source_target_pairs={{0,1},{1,0},{2,3},{3,2},{4,5},{5,4},{6,7},{7,6},{8,9},{9,8},{10,11... | collective-permute-start | bytes 319496 | tf_op jit(solution)/shard_map/ppermute | solution.py:43
  120.5 10.7 %collective-permute-start.30 = (bf16[208,256]{1,0:T(8,128)(2,1)S(1)}, bf16[208,256]{1,0:T(8,128)(2,1)S(1)}, u32[]{:S(2)}, u32[]{:S(2)}) collective-permute-start(bf16[208,256]{1,0:T(8,128)(2,1)S(1)} %get-tuple-element.74), channel_id=1, source_target_pairs={{0,1},{1,0},{2,3},{3,2},{4,5},{5,4},{6,7},{7,6},{8,9},{9,8},{10,11... | collective-permute-start | bytes 319496 | tf_op jit(solution)/shard_map/ppermute | solution.py:43
  123.3 9.0 %collective-permute-start.31 = (bf16[208,256]{1,0:T(8,128)(2,1)S(1)}, bf16[208,256]{1,0:T(8,128)(2,1)S(1)}, u32[]{:S(2)}, u32[]{:S(2)}) collective-permute-start(bf16[208,256]{1,0:T(8,128)(2,1)S(1)} %get-tuple-element.75), channel_id=1, source_target_pairs={{0,2},{1,3},{2,0},{3,1},{4,6},{5,7},{6,4},{7,5},{8,10},{9,11},{10,... | collective-permute-start | bytes 319496 | tf_op jit(solution)/shard_map/ppermute | solution.py:43
  123.4 11.4 %collective-permute-start.32 = (bf16[208,256]{1,0:T(8,128)(2,1)S(1)}, bf16[208,256]{1,0:T(8,128)(2,1)S(1)}, u32[]{:S(2)}, u32[]{:S(2)}) collective-permute-start(bf16[208,256]{1,0:T(8,128)(2,1)S(1)} %get-tuple-element.76), channel_id=1, source_target_pairs={{0,3},{1,2},{2,1},{3,0},{4,7},{5,6},{6,5},{7,4},{8,11},{9,10},{10,... | collective-permute-start | bytes 319496 | tf_op jit(solution)/shard_map/ppermute | solution.py:43
  125.6 9.2 %collective-permute-start.33 = (bf16[208,256]{1,0:T(8,128)(2,1)S(1)}, bf16[208,256]{1,0:T(8,128)(2,1)S(1)}, u32[]{:S(2)}, u32[]{:S(2)}) collective-permute-start(bf16[208,256]{1,0:T(8,128)(2,1)S(1)} %get-tuple-element.77), channel_id=1, source_target_pairs={{0,4},{1,5},{2,6},{3,7},{4,0},{5,1},{6,2},{7,3},{8,12},{9,13},{10,... | collective-permute-start | bytes 319496 | tf_op jit(solution)/shard_map/ppermute | solution.py:43
  125.9 8.9 %collective-permute-start.34 = (bf16[208,256]{1,0:T(8,128)(2,1)S(1)}, bf16[208,256]{1,0:T(8,128)(2,1)S(1)}, u32[]{:S(2)}, u32[]{:S(2)}) collective-permute-start(bf16[208,256]{1,0:T(8,128)(2,1)S(1)} %get-tuple-element.78), channel_id=1, source_target_pairs={{0,5},{1,4},{2,7},{3,6},{4,1},{5,0},{6,3},{7,2},{8,13},{9,12},{10,... | collective-permute-start | bytes 319496 | tf_op jit(solution)/shard_map/ppermute | solution.py:43
  132.3 8.3 %collective-permute-start.36 = (bf16[208,256]{1,0:T(8,128)(2,1)S(1)}, bf16[208,256]{1,0:T(8,128)(2,1)S(1)}, u32[]{:S(2)}, u32[]{:S(2)}) collective-permute-start(bf16[208,256]{1,0:T(8,128)(2,1)S(1)} %get-tuple-element.80), channel_id=1, source_target_pairs={{0,7},{1,6},{2,5},{3,4},{4,3},{5,2},{6,1},{7,0},{8,15},{9,14},{10,... | collective-permute-start | bytes 319496 | tf_op jit(solution)/shard_map/ppermute | solution.py:43
  (15 other events, 424.3 us)

commit v3 on v2

v3 whole, which is shorter than its diff:
```python
import functools
import math

import jax
import jax.numpy as jnp
from jax import lax
from jax.experimental import pallas as pl
from jax.experimental.pallas import tpu as pltpu
from jax.sharding import Mesh
from jax.sharding import PartitionSpec as P

theta_base = 1000000.0
norm_eps = 1e-06
NEG = -1e30
FAR = 1e9
TP = ("z", "xhi")
SEQ = ("xlo", "yhi", "ylo", "core")
ROUND = ("xlo", "yhi", "ylo")
FAR_MASKS = (3, 4, 7)
VMEM = pl.BlockSpec(memory_space=pltpu.VMEM)
SMEM = pl.BlockSpec(memory_space=pltpu.SMEM)
ANY = pl.BlockSpec(memory_space=pl.ANY)
HBM = pl.BlockSpec(memory_space=pltpu.HBM)
F32 = jnp.float32
BF16 = jnp.bfloat16


def rotation_tables(positions, head_dim):
    half = head_dim // 2
    frequency = jnp.exp(-jnp.log(theta_base) * jnp.arange(half, dtype=F32) * 2.0 / head_dim)
    angles = positions.astype(F32)[..., None] * frequency
    cosine, sine = jnp.cos(angles), jnp.sin(angles)
    return jnp.concatenate([cosine, cosine], -1), jnp.concatenate([-sine, sine], -1)


def rotate(values, cosine, sine):
    return values * cosine + pltpu.roll(values, values.shape[-1] // 2, values.ndim - 1) * sine


def grant(mib):
    return pltpu.CompilerParams(vmem_limit_bytes=mib << 20)


def swap(x, axes, mask, size):
    return lax.ppermute(x, axes, [(i, i ^ mask) for i in range(size)])


def scale_of(pieces, width):
    total = jnp.sum(pieces[0] * pieces[0], axis=-1, keepdims=True)
    for piece in pieces[1:]:
        total = total + jnp.sum(piece * piece, axis=-1, keepdims=True)
    return lax.rsqrt(total / width + norm_eps)


def head_norm(values):
    return values * lax.rsqrt(jnp.mean(values * values, axis=-1, keepdims=True) + norm_eps)


def project_kernel(n, me_ref, *refs):
    pairs = refs[: n // 2]
    gain, qg, kg, cos, sin = refs[n // 2 : n // 2 + 5]
    hbm, (q_out, kv_out) = refs[n // 2 + 5 : n // 2 + 8], refs[n // 2 + 8 : n // 2 + 10]
    (wq, wk, wv), sems = refs[n // 2 + 10 : -1], refs[-1]
    copies = [
        pltpu.make_async_copy(src, dst, sems.at[i])
        for i, (src, dst) in enumerate(zip(hbm, (wq, wk, wv)))
    ]
    for c in copies:
        c.start()
    me = me_ref[0]
    width = pairs[0].shape[2]
    hd = qg.shape[1]
    xs = [p[i].astype(F32) for p in pairs for i in range(2)]
    scale = scale_of(xs, n * width)
    for c in copies:
        c.wait()
    q = k = v = None
    for step in range(n):
        src = jnp.bitwise_xor(me, step)
        rows = pl.ds(pl.multiple_of(src * width, width), width)
        x = (xs[step] * scale * gain[rows].astype(F32)[None, :]).astype(BF16)
        dq = jnp.dot(x, wq[rows, :], preferred_element_type=F32)
        dk = jnp.dot(x, wk[rows, :], preferred_element_type=F32)
        dv = jnp.dot(x, wv[rows, :], preferred_element_type=F32)
        q, k, v = (dq, dk, dv) if q is None else (q + dq, k + dk, v + dv)
    c, s = cos[...], sin[...]
    for h in range(q.shape[1] // hd):
        part = q[:, h * hd : (h + 1) * hd]
        q_out[:, h * hd : (h + 1) * hd] = rotate(head_norm(part) * qg[...], c, s).astype(BF16)
    kv_out[:, :hd] = rotate(head_norm(k) * kg[...], c, s).astype(BF16)
    kv_out[:, hd:] = v.astype(BF16)


def identity(rows, cols, period):
    row = lax.broadcasted_iota(jnp.int32, (rows, cols), 0)
    col = lax.broadcasted_iota(jnp.int32, (rows, cols), 1)
    return jnp.where(lax.rem(row, period) == col, 1.0, 0.0).astype(BF16)


def attend_kernel(count, ids, tab, kpos, k_index, q_index, cos, sin, *refs):
    q_in, kv_in, cached = refs[0:4], refs[4:8], refs[8:12]
    outs = refs[12:16]
    keys, values, new_keys, queries, bounds, places, run_m, run_l, run_acc, todo, sems = refs[16:]
    hd = keys.shape[2]
    span = cached[0].shape[1]
    slots = keys.shape[0]
    place_at = tab.shape[0] // 2
    xy, mk = ids[0], ids[1]
    copies = []
    for p in range(4):
        for which, dst in enumerate((keys, values)):
            copies.append(
                pltpu.make_async_copy(
                    cached[p].at[pl.ds(2 * which, 2)],
                    dst.at[pl.ds(2 * p, 2), pl.ds(0, span), :],
                    sems.at[which, p],
                )
            )
    for c in copies:
        c.start()

    def scan_query(qi, n):
        p = qi // 2
        q_slot = jnp.bitwise_xor(xy, p) * 8 + jnp.bitwise_xor(mk, (p % 2) * 2) * 2 + qi % 2
        q_req, q_place = tab[q_slot], tab[place_at + q_slot]

        def scan_key(ki, n):
            k_nat = jnp.bitwise_xor(mk, ki // 2) * 2 + ki % 2
            k_slot = xy * 8 + k_nat
            k_req, k_place = tab[k_slot], tab[place_at + k_slot]
            seen = jnp.logical_and(k_req == q_req, k_place <= q_place)

            todo[0, n] = qi
            todo[1, n] = ki
            todo[2, n] = k_nat
            todo[3, n] = jnp.where(k_place < q_place, 65536, 0)
            return n + seen.astype(jnp.int32)

        return lax.fori_loop(0, slots, scan_key, n)

    found = lax.fori_loop(0, slots, scan_query, 0)
    todo[0, found] = 0
    todo[1, found] = 0
    todo[2, found] = 0
    todo[3, found] = -65536

    pad = values.shape[1] - span - count
    for p in range(4):
        for j in range(2):
            fresh = kv_in[p][j * count : (j + 1) * count, :]
            zero = jnp.zeros((pad, hd), BF16)
            new_keys[2 * p + j] = jnp.concatenate([fresh[:, :hd], zero], 0)
            values[2 * p + j, span:, :] = jnp.concatenate([fresh[:, hd:], zero], 0)
            rows = q_in[p][j * count : (j + 1) * count, :]
            queries[2 * p + j] = jnp.concatenate([rows[:, :hd], rows[:, hd:]], 0)
    places[:, :span] = kpos[...]
    places[:, span:] = jnp.concatenate(
        [k_index[...].astype(F32), jnp.full((slots, pad), FAR, F32)], axis=1
    )
    index = q_index[...].astype(F32)
    upper = jnp.floor(index * 0.125)
    digits = jnp.concatenate([upper, index - 8.0 * upper], 0).astype(BF16)
    columns = lax.dot_general(
        identity(2 * count, count, count),
        digits,
        (((1,), (1,)), ((), ())),
        preferred_element_type=F32,
    )
    for q in range(slots):
        bounds[q] = 8.0 * columns[:, q : q + 1] + columns[:, slots + q : slots + q + 1]
    run_m[...] = jnp.full(run_m.shape, NEG, F32)
    run_l[...] = jnp.zeros(run_l.shape, F32)
    run_acc[...] = jnp.zeros(run_acc.shape, F32)
    for c in copies:
        c.wait()
    factor = hd**-0.5 * math.log2(math.e)

    def score(at):
        qi, ki, row = todo[0, at], todo[1, at], pl.ds(todo[2, at], 1)
        query = queries[qi]
        turned = rotate(query.astype(F32), cos[row, :], sin[row, :]).astype(BF16)
        return jnp.concatenate(
            [
                lax.dot_general(
                    q, k[ki], (((1,), (1,)), ((), ())), preferred_element_type=F32
                )
                for q, k in ((turned, keys), (query, new_keys))
            ],
            axis=1,
        )

    def soften(at, scores):
        qi = todo[0, at]
        bound = bounds[qi] + todo[3, at].astype(F32)
        scores = jnp.where(places[pl.ds(todo[2, at], 1), :] <= bound, scores, NEG)
        old = run_m[qi]
        new = jnp.maximum(old, jnp.max(scores, axis=-1, keepdims=True))
        shrink = jnp.exp2((old - new) * factor)
        weights = jnp.exp2((scores - new) * factor)
        run_m[qi] = new
        run_l[qi] = run_l[qi] * shrink + jnp.sum(weights, axis=-1, keepdims=True)
        return shrink, weights.astype(BF16)

    def gather(at, shrink, weights):
        qi, ki = todo[0, at], todo[1, at]
        run_acc[qi] = run_acc[qi] * shrink + jnp.dot(
            weights, values[ki], preferred_element_type=F32
        )

    def two(i, _):
        first, second = 2 * i, 2 * i + 1
        s1 = score(first)
        s2 = score(second)
        soft1 = soften(first, s1)
        soft2 = soften(second, s2)
        gather(first, *soft1)
        gather(second, *soft2)
        return 0

    lax.fori_loop(0, (found + 1) // 2, two, 0)

    lane = lax.broadcasted_iota(jnp.int32, (2 * count, hd), 1)
    dest, entry, level = lane // 16, lane % 4, (lane % 16) // 4
    stats = jnp.zeros((2 * count, hd), F32)
    for p in range(4):
        for j in range(2):
            stats = jnp.where((dest == p) & (entry == j), run_m[2 * p + j], stats)
            stats = jnp.where((dest == p) & (entry == 2 + j), run_l[2 * p + j], stats)
    high = stats.astype(BF16).astype(F32)
    mid = (stats - high).astype(BF16).astype(F32)
    low = stats - high - mid
    stats = jnp.where(level == 0, high, jnp.where(level == 1, mid, low)).astype(BF16)
    flat = lax.dot_general(
        stats,
        identity(2 * count, 2 * hd, 4 * count),
        (((0,), (0,)), ((), ())),
        preferred_element_type=F32,
    ).astype(BF16)
    for p in range(4):
        for j in range(2):
            outs[p][j, : 2 * count, :] = run_acc[2 * p + j].astype(BF16)
            outs[p][j, 2 * count :, :] = flat[16 * p : 16 * p + 16, j * hd : (j + 1) * hd]


def attend(ids, table, kpos, key_index, query_index, cos, sin, queries, fresh, cached):
    count = query_index.shape[1]
    slot_local = cached[0].shape[0] // 2
    span, hd = cached[0].shape[1:]
    key_rows = span + 128
    return pl.pallas_call(
        functools.partial(attend_kernel, count),
        in_specs=[SMEM, SMEM] + [VMEM] * 13 + [ANY] * 4,
        out_specs=[VMEM] * 4,
        out_shape=[jax.ShapeDtypeStruct((slot_local, 2 * count + 16, hd), BF16)] * 4,
        scratch_shapes=[
            pltpu.VMEM((8, span, hd), BF16),
            pltpu.VMEM((8, key_rows, hd), BF16),
            pltpu.VMEM((8, key_rows - span, hd), BF16),
            pltpu.VMEM((8, 2 * count, hd), BF16),
            pltpu.VMEM((8, 2 * count, 1), F32),
            pltpu.VMEM((8, key_rows), F32),
            pltpu.VMEM((8, 2 * count, 1), F32),
            pltpu.VMEM((8, 2 * count, 1), F32),
            pltpu.VMEM((8, 2 * count, hd), F32),
            pltpu.SMEM((4, 72), jnp.int32),
            pltpu.SemaphoreType.DMA((2, 4)),
        ],
        compiler_params=grant(18),
        name="attend",
    )(ids, table, kpos, key_index, query_index, cos, sin, *queries, *fresh, *cached)


def merge_kernel(n, count, me_ref, *refs):
    parts, wo, outs = refs[:4], refs[4], refs[5:]
    me = me_ref[0]
    hd = parts[0].shape[2]
    width = outs[0].shape[1]
    turn = identity(2 * count, 2 * hd, 4 * count)
    tops, sums = [], []
    for part in parts:
        flat = jnp.concatenate([part[0, 2 * count :, :], part[1, 2 * count :, :]], axis=1)
        st = lax.dot_general(
            turn, flat, (((1,), (1,)), ((), ())), preferred_element_type=F32
        )
        st = st[:, 0:4] + st[:, 4:8] + st[:, 8:12]
        tops.append(st[:, 0:2])
        sums.append(st[:, 2:4])
    top = functools.reduce(jnp.maximum, tops)
    shares = [jnp.exp((m - top) * hd**-0.5) for m in tops]
    total = functools.reduce(jnp.add, [w * s for w, s in zip(shares, sums)])
    shares = [w / total for w in shares]
    rows = [[], []]
    for j in range(2):
        acc = functools.reduce(
            jnp.add,
            [
                w[:, j : j + 1] * part[j, : 2 * count, :].astype(F32)
                for w, part in zip(shares, parts)
            ],
        )
        for h in range(2):
            rows[h].append(acc[h * count : (h + 1) * count])
    att = jnp.concatenate([jnp.concatenate(r, 0) for r in rows], 1).astype(BF16)
    for step in range(n):
        src = jnp.bitwise_xor(me, step)
        cols = pl.ds(pl.multiple_of(src * width, width), width)
        outs[step][...] = jnp.dot(att, wo[:, cols], preferred_element_type=F32).astype(BF16)


def feed_kernel(n, me_ref, *refs):
    pieces = refs[:n]
    gain, wg, wu, wd = refs[n : n + 4]
    outs = refs[n + 4 :]
    me = me_ref[0]
    width = pieces[0].shape[1]
    xs = [p[...].astype(F32) for p in pieces]
    scale = scale_of(xs, n * width)
    g = u = None
    for step in range(n):
        src = jnp.bitwise_xor(me, step)
        rows = pl.ds(pl.multiple_of(src * width, width), width)
        x = (xs[step] * scale * gain[rows].astype(F32)[None, :]).astype(BF16)
        dg = jnp.dot(x, wg[rows, :], preferred_element_type=F32)
        du = jnp.dot(x, wu[rows, :], preferred_element_type=F32)
        g, u = (dg, du) if g is None else (g + dg, u + du)
    active = (g / (1.0 + jnp.exp(-g)) * u).astype(BF16)
    for step in range(n):
        src = jnp.bitwise_xor(me, step)
        cols = pl.ds(pl.multiple_of(src * width, width), width)
        outs[step][...] = jnp.dot(active, wd[:, cols], preferred_element_type=F32).astype(BF16)


def on_device(
    selected_hidden,
    cached_keys,
    cached_values,
    slot_spans,
    span_order,
    cache_start,
    selected_index,
    input_gain,
    query_weight,
    key_weight,
    value_weight,
    query_gain,
    key_gain,
    output_weight,
    post_gain,
    gate_weight,
    up_weight,
    down_weight,
):
    slot_local, count, width = selected_hidden.shape
    span = cached_keys.shape[1]
    hd = query_gain.shape[0]
    rows = slot_local * count
    spans = span_order.shape[1]
    n = 8

    def shaped(*shape, dtype=BF16):
        return jax.ShapeDtypeStruct(shape, dtype)

    xy = lax.axis_index(("xlo", "yhi"))
    mk = lax.axis_index(("ylo", "core"))
    me = lax.axis_index(TP).reshape(1)
    first_slot = lax.axis_index(SEQ) * slot_local

    number = lax.broadcasted_iota(jnp.int32, span_order.shape, 0) * spans
    number = number + lax.broadcasted_iota(jnp.int32, span_order.shape, 1)
    hit = slot_spans[:, None, None] == number[None]
    place = jnp.sum(jnp.where(hit, span_order[None], 0), axis=(1, 2))
    start = jnp.sum(jnp.where(hit, cache_start[None], 0), axis=(1, 2))
    table = jnp.concatenate([slot_spans // spans, place])
    ids = jnp.stack([xy, mk])
    base_here = lax.dynamic_slice_in_dim(place * span, first_slot, slot_local, 0)

    hidden = selected_hidden.reshape(rows, width)
    pair = jnp.stack([hidden, swap(hidden, "xhi", 1, 2)])

    pair, selected_later = lax.optimization_barrier((pair, selected_index))
    pairs = [pair] + [swap(pair, "z", k, 4) for k in (1, 2, 3)]

    cached = jnp.concatenate([cached_keys, cached_values], axis=0)
    cached_y = swap(cached, "ylo", 1, 2)
    cached_core = swap(cached, "core", 1, 2)

    index_here = lax.dynamic_slice_in_dim(selected_later, first_slot, slot_local, 0)
    qc, qs = rotation_tables(base_here[:, None] + index_here, hd)
    qc, qs = qc.reshape(rows, hd), qs.reshape(rows, hd)
    qg, kg = query_gain.astype(F32)[None], key_gain.astype(F32)[None]
    pairs[0], qg, kg, qc, qs, ids, table, cached_core = lax.optimization_barrier(
        (pairs[0], qg, kg, qc, qs, ids, table, cached_core)
    )
    queries, fresh = pl.pallas_call(
        functools.partial(project_kernel, n),
        in_specs=[SMEM] + [VMEM] * (n // 2 + 5) + [HBM] * 3,
        out_specs=[VMEM, VMEM],
        scratch_shapes=[
            pltpu.VMEM(w.shape, BF16) for w in (query_weight, key_weight, value_weight)
        ]
        + [pltpu.SemaphoreType.DMA((3,))],
        out_shape=[shaped(rows, query_weight.shape[1]), shaped(rows, 2 * hd)],
        compiler_params=grant(10),
        name="project",
    )(
        me,
        *pairs,
        input_gain,
        qg,
        kg,
        qc,
        qs,
        query_weight,
        key_weight,
        value_weight,
    )
    cached_y, selected_last, start, _ = lax.optimization_barrier(
        (cached_y, selected_later, start, fresh)
    )
    cached_set = [cached, cached_core, cached_y, swap(cached_y, "core", 1, 2)]
    fresh_y = swap(fresh, "ylo", 1, 2)
    fresh_set = [fresh, swap(fresh, "core", 1, 2), fresh_y, swap(fresh_y, "core", 1, 2)]
    query_set = [queries] + [swap(queries, ROUND, k, 8) for k in FAR_MASKS]

    group_index = lax.dynamic_slice_in_dim(selected_last, xy * 8, 8, 0)
    token = jnp.arange(span, dtype=jnp.int32)
    taken = jnp.any(group_index[:, :, None] == token[None, None, :], axis=1)
    kpos = jnp.where(taken, FAR, token[None, :].astype(F32))
    seq = lax.axis_index(SEQ)
    query_index = jnp.concatenate(
        [
            lax.dynamic_slice_in_dim(
                selected_last, jnp.bitwise_xor(seq, 2 * k) * slot_local, slot_local, 0
            )
            for k in (0,) + FAR_MASKS
        ],
        axis=0,
    )

    shift = lax.dynamic_slice_in_dim(place * span - start, xy * 8, 8, 0)
    kc, ks = rotation_tables(-shift, hd)
    parts = attend(
        ids,
        table,
        kpos,
        group_index,
        query_index,
        kc,
        ks,
        query_set,
        fresh_set,
        cached_set,
    )
    parts = [parts[0]] + [swap(part, ROUND, k, 8) for part, k in zip(parts[1:], FAR_MASKS)]

    projected = pl.pallas_call(
        functools.partial(merge_kernel, n, count),
        in_specs=[SMEM] + [VMEM] * 5,
        out_specs=[VMEM] * n,
        out_shape=[shaped(rows, width)] * n,
        compiler_params=grant(8),
        name="merge",
    )(me, *parts, output_weight)
    total = hidden.astype(F32) + projected[0].astype(F32)
    for k in range(1, n):
        total = total + swap(projected[k], TP, k, n).astype(F32)
    stream = total.astype(BF16)

    pieces = [stream] + [swap(stream, TP, k, n) for k in range(1, n)]
    downs = pl.pallas_call(
        functools.partial(feed_kernel, n),
        in_specs=[SMEM] + [VMEM] * (n + 4),
        out_specs=[VMEM] * n,
        out_shape=[shaped(rows, width)] * n,
        compiler_params=grant(18),
        name="feed",
    )(
        me,
        *pieces,
        post_gain,
        gate_weight,
        up_weight,
        down_weight,
    )
    total = stream.astype(F32) + downs[0].astype(F32)
    for k in range(1, n):
        total = total + swap(downs[k], TP, k, n).astype(F32)
    return total.astype(BF16).reshape(slot_local, count, width)


def solution(mesh):
    fine = Mesh(
        mesh.devices.reshape(2, 2, 2, 2, 4, 2), ("xlo", "yhi", "ylo", "core", "z", "xhi")
    )
    in_specs = (
        P(SEQ, None, TP),
        P(SEQ, None, TP),
        P(SEQ, None, TP),
        P(),
        P(),
        P(),
        P(),
        P(),
        P(None, TP),
        P(None, TP),
        P(None, TP),
        P(),
        P(),
        P(TP, None),
        P(),
        P(None, TP),
        P(None, TP),
        P(TP, None),
    )
    return jax.shard_map(
        on_device, mesh=fine, in_specs=in_specs, out_specs=P(SEQ, None, TP), check_vma=False
    )
```

time: 140 us -> 130 us (0.929); the launches traced: 141 us -> 129 us
  starting transfers between devices: 71.3 us -> 67.1 us
  Pallas kernels: 17.1 us -> 13.4 us
  waiting for transfers between devices: 39.4 us -> 37.1 us
    ppermute x37, starting transfers between devices: 71.3 us -> 67.1 us  [swap(): return lax.ppermute(x, axes, [(i, i ^ mask) for i in range(size)])]
    pallas_call x2 -> x1, Pallas kernels: 10.3 us -> 6.98 us  [attend(): pl.pallas_call(functools.partial(attend_kernel, count), in_specs=[SMEM, S...]
    ppermute x37, waiting for transfers between devices: 39.4 us -> 37.1 us  [swap(): return lax.ppermute(x, axes, [(i, i ^ mask) for i in range(size)])]
    unnamed x20 -> x23, local copies, waits for them, and re-layouts: 4.2 us -> 3.29 us
  transfers between devices with their start and end apart: 37 -> 37, of which waited for: 15 -> 17; matrix products, arithmetic and copies ran while one was open for 5% -> 5% of each run, Pallas kernels for 2% -> 2%
where the time goes in v3:
time: 130 us; the launch traced here: 129 us
  starting transfers between devices  67.1 us (52%)
  waiting for transfers between devices  37.1 us (29%)
  Pallas kernels  13.4 us (10%)
  other arithmetic  6.85 us (5%)
  local copies, waits for them, and re-layouts  4.58 us (4%)
    ppermute x37, starting transfers between devices, swap(): return lax.ppermute(x, axes, [(i, i ^ mask) for i in range(size)])  67.1 us
    ppermute x37, waiting for transfers between devices, swap(): return lax.ppermute(x, axes, [(i, i ^ mask) for i in range(size)])  37.1 us
    pallas_call x1, Pallas kernels, attend(): pl.pallas_call(functools.partial(attend_kernel, count), in_specs=[SMEM, S...  6.98 us
    unnamed x23, local copies, waits for them, and re-layouts  3.29 us
    pallas_call x1, Pallas kernels, on_device(): pl.pallas_call(functools.partial(project_kernel, n), in_specs=[SMEM] + [V...  2.79 us
  transfers between devices with their start and end apart: 37, of which 17 were waited for; matrix products, arithmetic and copies ran while one was open for 5% of the time, Pallas kernels for 2%

profile of v3, /device:TPU:0, one launch (start us, length us, event | category | flops | bytes accessed | tf_op | source)
XLA Modules:
  0.0 129.3 jit_solution(15871093815644904655)
XLA Ops:
  2.3 1.7 %collective-permute-start.2 = (bf16[4,1024,128]{2,1,0:T(8,128)(2,1)S(1)}, bf16[4,1024,128]{2,1,0:T(8,128)(2,1)S(1)}, u32[]{:S(2)}, u32[]{:S(2)}) collective-permute-start(bf16[4,1024,128]{2,1,0:T(8,128)(2,1)S(1)} %constant_dynamic-update-slice_fusion.refs_8_), channel_id=1, source_target_pairs={{0,16},{16,0},{1,17},{17,1},{2,18},{18,2},{3,19},{19,3},{4,20},{20... | collective-permute-start | bytes 3145736 | tf_op jit(solution)/shard_map/ppermute | solution.py:45
  4.0 3.0 %collective-permute-start = (bf16[208,256]{1,0:T(8,128)(2,1)}, bf16[208,256]{1,0:T(8,128)(2,1)S(1)}, u32[]{:S(2)}, u32[]{:S(2)}) collective-permute-start(bf16[208,256]{1,0:T(8,128)(2,1)} %bitcast.14), channel_id=1, source_target_pairs={{0,1},{1,0},{2,3},{3,2},{4,5},{5,4},{6,7},{7,6},{8,9},{9,8},{10,11... | collective-permute-start | bytes 319496 | tf_op jit(solution)/shard_map/ppermute | solution.py:45
  9.5 1.6 %collective-permute-done = bf16[208,256]{1,0:T(8,128)(2,1)S(1)} collective-permute-done((bf16[208,256]{1,0:T(8,128)(2,1)}, bf16[208,256]{1,0:T(8,128)(2,1)S(1)}, u32[]{:S(2)}, u32[]{:S(2)}) %collective-permute-start) | collective-permute-done | bytes 106528 | tf_op jit(solution)/shard_map/ppermute | solution.py:45
  12.1 4.1 %collective-permute-start.5 = (bf16[2,208,256]{2,1,0:T(8,128)(2,1)S(1)}, bf16[2,208,256]{2,1,0:T(8,128)(2,1)}, u32[]{:S(2)}, u32[]{:S(2)}) collective-permute-start(bf16[2,208,256]{2,1,0:T(8,128)(2,1)S(1)} %pad_maximum_fusion.refs_0_), channel_id=1, source_target_pairs={{0,6},{2,4},{4,2},{6,0},{1,7},{3,5},{5,3},{7,1},{8,14},{10,12},{12... | collective-permute-start | bytes 638984 | tf_op jit(solution)/shard_map/ppermute | solution.py:45
  18.6 7.4 %collective-permute-done.5.refs_3_ = bf16[2,208,256]{2,1,0:T(8,128)(2,1)} collective-permute-done((bf16[2,208,256]{2,1,0:T(8,128)(2,1)S(1)}, bf16[2,208,256]{2,1,0:T(8,128)(2,1)}, u32[]{:S(2)}, u32[]{:S(2)}) %collective-permute-start.5) | collective-permute-done | bytes 213024 | tf_op jit(solution)/shard_map/ppermute | solution.py:45
  28.8 2.8 %project.1 = (bf16[208,256]{1,0:T(8,128)(2,1)S(1)}, bf16[208,256]{1,0:T(8,128)(2,1)S(1)}) custom-call(s32[1]{0:T(128)} %bitcast.1.me_ref, bf16[2,208,256]{2,1,0:T(8,128)(2,1)S(1)} %pad_maximum_fusion.refs_0_, bf16[2,208,256]{2,1,0:T(8,128)(2,1)} %collective-permute-done.3.refs_1_, bf16[2,208,256]{2,1,0:T(8,128)(2,1)} %collective-permute-done.4.refs_2_, ...), custom_call_target="tpu_custom_call" | custom-call | tf_op jit(solution)/shard_map/project/pallas_call | solution.py:394
  32.1 3.9 %collective-permute-start.8 = (bf16[208,256]{1,0:T(8,128)(2,1)S(1)}, bf16[208,256]{1,0:T(8,128)(2,1)S(1)}, u32[]{:S(2)}, u32[]{:S(2)}) collective-permute-start(bf16[208,256]{1,0:T(8,128)(2,1)S(1)} %get-tuple-element.52.refs_0_), channel_id=1, source_target_pairs={{0,112},{16,96},{32,80},{48,64},{64,48},{80,32},{96,16},{112,0},{1... | collective-permute-start | bytes 319496 | tf_op jit(solution)/shard_map/ppermute | solution.py:45
  40.0 2.3 %collective-permute-done.7.refs_2_ = bf16[208,256]{1,0:T(8,128)(2,1)S(1)} collective-permute-done((bf16[208,256]{1,0:T(8,128)(2,1)S(1)}, bf16[208,256]{1,0:T(8,128)(2,1)S(1)}, u32[]{:S(2)}, u32[]{:S(2)}) %collective-permute-start.7) | collective-permute-done | bytes 106528 | tf_op jit(solution)/shard_map/ppermute | solution.py:45
  42.3 2.4 %collective-permute-done.6.refs_1_ = bf16[208,256]{1,0:T(8,128)(2,1)S(1)} collective-permute-done((bf16[208,256]{1,0:T(8,128)(2,1)S(1)}, bf16[208,256]{1,0:T(8,128)(2,1)S(1)}, u32[]{:S(2)}, u32[]{:S(2)}) %collective-permute-start.6) | collective-permute-done | bytes 106528 | tf_op jit(solution)/shard_map/ppermute | solution.py:45
  44.7 7.0 %attend.1 = (bf16[2,224,128]{2,1,0:T(8,128)(2,1)S(1)}, bf16[2,224,128]{2,1,0:T(8,128)(2,1)S(1)}, bf16[2,224,128]{2,1,0:T(8,128)(2,1)S(1)}, bf16[2,224,128]{2,1,0:T(8,128)(2,1)S(1)}) custom-call(s32[2]{0:T(128)S(1)} %pad_add_fusion.1.ids, s32[64]{0:T(128)S(1)} %pad_add_fusion.2.tab, f32[8,1024]{1,0:T(8,128)S(1)} %broadcast_select_fusion.kpos, ...), custom_call_target="tpu_custom_call" | custom-call | tf_op jit(solution)/shard_map/attend/pallas_call | solution.py:250
  51.6 2.9 %collective-permute-start.13 = (bf16[2,224,128]{2,1,0:T(8,128)(2,1)S(1)}, bf16[2,224,128]{2,1,0:T(8,128)(2,1)S(1)}, u32[]{:S(2)}, u32[]{:S(2)}) collective-permute-start(bf16[2,224,128]{2,1,0:T(8,128)(2,1)S(1)} %get-tuple-element.56), channel_id=1, source_target_pairs={{0,48},{16,32},{32,16},{48,0},{64,112},{80,96},{96,80},{112,64},{1... | collective-permute-start | bytes 344072 | tf_op jit(solution)/shard_map/ppermute | solution.py:45
  54.5 3.4 %collective-permute-start.14 = (bf16[2,224,128]{2,1,0:T(8,128)(2,1)S(1)}, bf16[2,224,128]{2,1,0:T(8,128)(2,1)S(1)}, u32[]{:S(2)}, u32[]{:S(2)}) collective-permute-start(bf16[2,224,128]{2,1,0:T(8,128)(2,1)S(1)} %get-tuple-element.57), channel_id=1, source_target_pairs={{0,64},{16,80},{32,96},{48,112},{64,0},{80,16},{96,32},{112,48},{1... | collective-permute-start | bytes 344072 | tf_op jit(solution)/shard_map/ppermute | solution.py:45
  58.0 2.6 %collective-permute-start.15 = (bf16[2,224,128]{2,1,0:T(8,128)(2,1)S(1)}, bf16[2,224,128]{2,1,0:T(8,128)(2,1)S(1)}, u32[]{:S(2)}, u32[]{:S(2)}) collective-permute-start(bf16[2,224,128]{2,1,0:T(8,128)(2,1)S(1)} %get-tuple-element.58), channel_id=1, source_target_pairs={{0,112},{16,96},{32,80},{48,64},{64,48},{80,32},{96,16},{112,0},{1... | collective-permute-start | bytes 344072 | tf_op jit(solution)/shard_map/ppermute | solution.py:45
  61.6 3.3 %collective-permute-done.15.refs_3_ = bf16[2,224,128]{2,1,0:T(8,128)(2,1)S(1)} collective-permute-done((bf16[2,224,128]{2,1,0:T(8,128)(2,1)S(1)}, bf16[2,224,128]{2,1,0:T(8,128)(2,1)S(1)}, u32[]{:S(2)}, u32[]{:S(2)}) %collective-permute-start.15) | collective-permute-done | bytes 114720 | tf_op jit(solution)/shard_map/ppermute | solution.py:45
  66.0 2.8 %collective-permute-start.16 = (bf16[208,256]{1,0:T(8,128)(2,1)S(1)}, bf16[208,256]{1,0:T(8,128)(2,1)S(1)}, u32[]{:S(2)}, u32[]{:S(2)}) collective-permute-start(bf16[208,256]{1,0:T(8,128)(2,1)S(1)} %get-tuple-element.60), channel_id=1, source_target_pairs={{0,1},{1,0},{2,3},{3,2},{4,5},{5,4},{6,7},{7,6},{8,9},{9,8},{10,11... | collective-permute-start | bytes 319496 | tf_op jit(solution)/shard_map/ppermute | solution.py:45
  71.1 2.7 %collective-permute-start.19 = (bf16[208,256]{1,0:T(8,128)(2,1)S(1)}, bf16[208,256]{1,0:T(8,128)(2,1)S(1)}, u32[]{:S(2)}, u32[]{:S(2)}) collective-permute-start(bf16[208,256]{1,0:T(8,128)(2,1)S(1)} %get-tuple-element.63), channel_id=1, source_target_pairs={{0,4},{1,5},{2,6},{3,7},{4,0},{5,1},{6,2},{7,3},{8,12},{9,13},{10,... | collective-permute-start | bytes 319496 | tf_op jit(solution)/shard_map/ppermute | solution.py:45
  73.8 3.0 %collective-permute-start.20 = (bf16[208,256]{1,0:T(8,128)(2,1)S(1)}, bf16[208,256]{1,0:T(8,128)(2,1)S(1)}, u32[]{:S(2)}, u32[]{:S(2)}) collective-permute-start(bf16[208,256]{1,0:T(8,128)(2,1)S(1)} %get-tuple-element.64), channel_id=1, source_target_pairs={{0,5},{1,4},{2,7},{3,6},{4,1},{5,0},{6,3},{7,2},{8,13},{9,12},{10,... | collective-permute-start | bytes 319496 | tf_op jit(solution)/shard_map/ppermute | solution.py:45
  76.8 2.9 %collective-permute-start.21 = (bf16[208,256]{1,0:T(8,128)(2,1)S(1)}, bf16[208,256]{1,0:T(8,128)(2,1)S(1)}, u32[]{:S(2)}, u32[]{:S(2)}) collective-permute-start(bf16[208,256]{1,0:T(8,128)(2,1)S(1)} %get-tuple-element.65), channel_id=1, source_target_pairs={{0,6},{1,7},{2,4},{3,5},{4,2},{5,3},{6,0},{7,1},{8,14},{9,15},{10,... | collective-permute-start | bytes 319496 | tf_op jit(solution)/shard_map/ppermute | solution.py:45
  80.3 2.3 %collective-permute-done.20 = bf16[208,256]{1,0:T(8,128)(2,1)S(1)} collective-permute-done((bf16[208,256]{1,0:T(8,128)(2,1)S(1)}, bf16[208,256]{1,0:T(8,128)(2,1)S(1)}, u32[]{:S(2)}, u32[]{:S(2)}) %collective-permute-start.20) | collective-permute-done | bytes 106528 | tf_op jit(solution)/shard_map/ppermute | solution.py:45
  83.6 4.6 %collective-permute-done.22 = bf16[208,256]{1,0:T(8,128)(2,1)S(1)} collective-permute-done((bf16[208,256]{1,0:T(8,128)(2,1)S(1)}, bf16[208,256]{1,0:T(8,128)(2,1)S(1)}, u32[]{:S(2)}, u32[]{:S(2)}) %collective-permute-start.22) | collective-permute-done | bytes 106528 | tf_op jit(solution)/shard_map/ppermute | solution.py:45
  88.8 2.9 %collective-permute-start.28 = (bf16[208,256]{1,0:T(8,128)(2,1)S(1)}, bf16[208,256]{1,0:T(8,128)(2,1)S(1)}, u32[]{:S(2)}, u32[]{:S(2)}) collective-permute-start(bf16[208,256]{1,0:T(8,128)(2,1)S(1)} %add_convert_fusion.1.refs_0_), channel_id=1, source_target_pairs={{0,6},{1,7},{2,4},{3,5},{4,2},{5,3},{6,0},{7,1},{8,14},{9,15},{10,... | collective-permute-start | bytes 319496 | tf_op jit(solution)/shard_map/ppermute | solution.py:45
  92.6 5.0 %collective-permute-start.26 = (bf16[208,256]{1,0:T(8,128)(2,1)S(1)}, bf16[208,256]{1,0:T(8,128)(2,1)S(1)}, u32[]{:S(2)}, u32[]{:S(2)}) collective-permute-start(bf16[208,256]{1,0:T(8,128)(2,1)S(1)} %add_convert_fusion.1.refs_0_), channel_id=1, source_target_pairs={{0,4},{1,5},{2,6},{3,7},{4,0},{5,1},{6,2},{7,3},{8,12},{9,13},{10,... | collective-permute-start | bytes 319496 | tf_op jit(solution)/shard_map/ppermute | solution.py:45
  97.7 2.0 %collective-permute-start.24 = (bf16[208,256]{1,0:T(8,128)(2,1)S(1)}, bf16[208,256]{1,0:T(8,128)(2,1)S(1)}, u32[]{:S(2)}, u32[]{:S(2)}) collective-permute-start(bf16[208,256]{1,0:T(8,128)(2,1)S(1)} %add_convert_fusion.1.refs_0_), channel_id=1, source_target_pairs={{0,2},{1,3},{2,0},{3,1},{4,6},{5,7},{6,4},{7,5},{8,10},{9,11},{10,... | collective-permute-start | bytes 319496 | tf_op jit(solution)/shard_map/ppermute | solution.py:45
  99.7 2.9 %collective-permute-start.23 = (bf16[208,256]{1,0:T(8,128)(2,1)S(1)}, bf16[208,256]{1,0:T(8,128)(2,1)S(1)}, u32[]{:S(2)}, u32[]{:S(2)}) collective-permute-start(bf16[208,256]{1,0:T(8,128)(2,1)S(1)} %add_convert_fusion.1.refs_0_), channel_id=1, source_target_pairs={{0,1},{1,0},{2,3},{3,2},{4,5},{5,4},{6,7},{7,6},{8,9},{9,8},{10,11... | collective-permute-start | bytes 319496 | tf_op jit(solution)/shard_map/ppermute | solution.py:45
  102.6 3.2 %collective-permute-done.25.refs_3_ = bf16[208,256]{1,0:T(8,128)(2,1)S(1)} collective-permute-done((bf16[208,256]{1,0:T(8,128)(2,1)S(1)}, bf16[208,256]{1,0:T(8,128)(2,1)S(1)}, u32[]{:S(2)}, u32[]{:S(2)}) %collective-permute-start.25) | collective-permute-done | bytes 106528 | tf_op jit(solution)/shard_map/ppermute | solution.py:45
  106.5 2.5 %feed.1 = (bf16[208,256]{1,0:T(8,128)(2,1)S(1)}, bf16[208,256]{1,0:T(8,128)(2,1)S(1)}, bf16[208,256]{1,0:T(8,128)(2,1)S(1)}, bf16[208,256]{1,0:T(8,128)(2,1)S(1)...) custom-call(s32[1]{0:T(128)} %bitcast.1.me_ref, ...), custom_call_target="tpu_custom_call" | custom-call | tf_op jit(solution)/shard_map/feed/pallas_call | solution.py:470
  109.0 3.1 %collective-permute-start.30 = (bf16[208,256]{1,0:T(8,128)(2,1)S(1)}, bf16[208,256]{1,0:T(8,128)(2,1)S(1)}, u32[]{:S(2)}, u32[]{:S(2)}) collective-permute-start(bf16[208,256]{1,0:T(8,128)(2,1)S(1)} %get-tuple-element.68), channel_id=1, source_target_pairs={{0,1},{1,0},{2,3},{3,2},{4,5},{5,4},{6,7},{7,6},{8,9},{9,8},{10,11... | collective-permute-start | bytes 319496 | tf_op jit(solution)/shard_map/ppermute | solution.py:45
  112.1 2.0 %collective-permute-start.32 = (bf16[208,256]{1,0:T(8,128)(2,1)S(1)}, bf16[208,256]{1,0:T(8,128)(2,1)S(1)}, u32[]{:S(2)}, u32[]{:S(2)}) collective-permute-start(bf16[208,256]{1,0:T(8,128)(2,1)S(1)} %get-tuple-element.70), channel_id=1, source_target_pairs={{0,3},{1,2},{2,1},{3,0},{4,7},{5,6},{6,5},{7,4},{8,11},{9,10},{10,... | collective-permute-start | bytes 319496 | tf_op jit(solution)/shard_map/ppermute | solution.py:45
  114.9 5.2 %collective-permute-start.34 = (bf16[208,256]{1,0:T(8,128)(2,1)S(1)}, bf16[208,256]{1,0:T(8,128)(2,1)S(1)}, u32[]{:S(2)}, u32[]{:S(2)}) collective-permute-start(bf16[208,256]{1,0:T(8,128)(2,1)S(1)} %get-tuple-element.72), channel_id=1, source_target_pairs={{0,5},{1,4},{2,7},{3,6},{4,1},{5,0},{6,3},{7,2},{8,13},{9,12},{10,... | collective-permute-start | bytes 319496 | tf_op jit(solution)/shard_map/ppermute | solution.py:45
  120.1 3.2 %collective-permute-start.36 = (bf16[208,256]{1,0:T(8,128)(2,1)S(1)}, bf16[208,256]{1,0:T(8,128)(2,1)S(1)}, u32[]{:S(2)}, u32[]{:S(2)}) collective-permute-start(bf16[208,256]{1,0:T(8,128)(2,1)S(1)} %get-tuple-element.74), channel_id=1, source_target_pairs={{0,7},{1,6},{2,5},{3,4},{4,3},{5,2},{6,1},{7,0},{8,15},{9,14},{10,... | collective-permute-start | bytes 319496 | tf_op jit(solution)/shard_map/ppermute | solution.py:45
  123.5 2.5 %collective-permute-done.35 = bf16[208,256]{1,0:T(8,128)(2,1)S(1)} collective-permute-done((bf16[208,256]{1,0:T(8,128)(2,1)S(1)}, bf16[208,256]{1,0:T(8,128)(2,1)S(1)}, u32[]{:S(2)}, u32[]{:S(2)}) %collective-permute-start.35) | collective-permute-done | bytes 106528 | tf_op jit(solution)/shard_map/ppermute | solution.py:45
  126.0 2.5 %collective-permute-done.36 = bf16[208,256]{1,0:T(8,128)(2,1)S(1)} collective-permute-done((bf16[208,256]{1,0:T(8,128)(2,1)S(1)}, bf16[208,256]{1,0:T(8,128)(2,1)S(1)}, u32[]{:S(2)}, u32[]{:S(2)}) %collective-permute-start.36) | collective-permute-done | bytes 106528 | tf_op jit(solution)/shard_map/ppermute | solution.py:45
  (98 shorter events, 25.4 us)
Async XLA Ops:
  2.3 34.3 %collective-permute-start.2 = (bf16[4,1024,128]{2,1,0:T(8,128)(2,1)S(1)}, bf16[4,1024,128]{2,1,0:T(8,128)(2,1)S(1)}, u32[]{:S(2)}, u32[]{:S(2)}) collective-permute-start(bf16[4,1024,128]{2,1,0:T(8,128)(2,1)S(1)} %constant_dynamic-update-slice_fusion.refs_8_), channel_id=1, source_target_pairs={{0,16},{16,0},{1,17},{17,1},{2,18},{18,2},{3,19},{19,3},{4,20},{20... | collective-permute-start | bytes 3145736 | tf_op jit(solution)/shard_map/ppermute | solution.py:45
  4.0 14.5 %collective-permute-start.1 = (bf16[4,1024,128]{2,1,0:T(8,128)(2,1)S(1)}, bf16[4,1024,128]{2,1,0:T(8,128)(2,1)}, u32[]{:S(2)}, u32[]{:S(2)}) collective-permute-start(bf16[4,1024,128]{2,1,0:T(8,128)(2,1)S(1)} %constant_dynamic-update-slice_fusion.refs_8_), channel_id=1, source_target_pairs={{0,8},{8,0},{1,9},{9,1},{2,10},{10,2},{3,11},{11,3},{4,12},{12,4},... | collective-permute-start | bytes 3145736 | tf_op jit(solution)/shard_map/ppermute | solution.py:45
  4.0 7.1 %collective-permute-start = (bf16[208,256]{1,0:T(8,128)(2,1)}, bf16[208,256]{1,0:T(8,128)(2,1)S(1)}, u32[]{:S(2)}, u32[]{:S(2)}) collective-permute-start(bf16[208,256]{1,0:T(8,128)(2,1)} %bitcast.14), channel_id=1, source_target_pairs={{0,1},{1,0},{2,3},{3,2},{4,5},{5,4},{6,7},{7,6},{8,9},{9,8},{10,11... | collective-permute-start | bytes 319496 | tf_op jit(solution)/shard_map/ppermute | solution.py:45
  12.1 13.9 %collective-permute-start.5 = (bf16[2,208,256]{2,1,0:T(8,128)(2,1)S(1)}, bf16[2,208,256]{2,1,0:T(8,128)(2,1)}, u32[]{:S(2)}, u32[]{:S(2)}) collective-permute-start(bf16[2,208,256]{2,1,0:T(8,128)(2,1)S(1)} %pad_maximum_fusion.refs_0_), channel_id=1, source_target_pairs={{0,6},{2,4},{4,2},{6,0},{1,7},{3,5},{5,3},{7,1},{8,14},{10,12},{12... | collective-permute-start | bytes 638984 | tf_op jit(solution)/shard_map/ppermute | solution.py:45
  16.2 9.8 %collective-permute-start.4 = (bf16[2,208,256]{2,1,0:T(8,128)(2,1)S(1)}, bf16[2,208,256]{2,1,0:T(8,128)(2,1)}, u32[]{:S(2)}, u32[]{:S(2)}) collective-permute-start(bf16[2,208,256]{2,1,0:T(8,128)(2,1)S(1)} %pad_maximum_fusion.refs_0_), channel_id=1, source_target_pairs={{0,4},{2,6},{4,0},{6,2},{1,5},{3,7},{5,1},{7,3},{8,12},{10,14},{12... | collective-permute-start | bytes 638984 | tf_op jit(solution)/shard_map/ppermute | solution.py:45
  16.2 10.5 %collective-permute-start.3 = (bf16[2,208,256]{2,1,0:T(8,128)(2,1)S(1)}, bf16[2,208,256]{2,1,0:T(8,128)(2,1)}, u32[]{:S(2)}, u32[]{:S(2)}) collective-permute-start(bf16[2,208,256]{2,1,0:T(8,128)(2,1)S(1)} %pad_maximum_fusion.refs_0_), channel_id=1, source_target_pairs={{0,2},{2,0},{4,6},{6,4},{1,3},{3,1},{5,7},{7,5},{8,10},{10,8},{12,... | collective-permute-start | bytes 638984 | tf_op jit(solution)/shard_map/ppermute | solution.py:45
  32.1 7.9 %collective-permute-start.8 = (bf16[208,256]{1,0:T(8,128)(2,1)S(1)}, bf16[208,256]{1,0:T(8,128)(2,1)S(1)}, u32[]{:S(2)}, u32[]{:S(2)}) collective-permute-start(bf16[208,256]{1,0:T(8,128)(2,1)S(1)} %get-tuple-element.52.refs_0_), channel_id=1, source_target_pairs={{0,112},{16,96},{32,80},{48,64},{64,48},{80,32},{96,16},{112,0},{1... | collective-permute-start | bytes 319496 | tf_op jit(solution)/shard_map/ppermute | solution.py:45
  36.7 8.0 %collective-permute-start.12 = (bf16[4,1024,128]{2,1,0:T(8,128)(2,1)S(1)}, bf16[4,1024,128]{2,1,0:T(8,128)(2,1)S(1)}, u32[]{:S(2)}, u32[]{:S(2)}) collective-permute-start(bf16[4,1024,128]{2,1,0:T(8,128)(2,1)S(1)} %collective-permute-done.2.refs_10_), channel_id=1, source_target_pairs={{0,8},{8,0},{1,9},{9,1},{2,10},{10,2},{3,11},{11,3},{4,12},{12,4},... | collective-permute-start | bytes 3145736 | tf_op jit(solution)/shard_map/ppermute | solution.py:45
  38.0 6.7 %collective-permute-start.6 = (bf16[208,256]{1,0:T(8,128)(2,1)S(1)}, bf16[208,256]{1,0:T(8,128)(2,1)S(1)}, u32[]{:S(2)}, u32[]{:S(2)}) collective-permute-start(bf16[208,256]{1,0:T(8,128)(2,1)S(1)} %get-tuple-element.52.refs_0_), channel_id=1, source_target_pairs={{0,48},{16,32},{32,16},{48,0},{64,112},{80,96},{96,80},{112,64},{1... | collective-permute-start | bytes 319496 | tf_op jit(solution)/shard_map/ppermute | solution.py:45
  51.6 8.9 %collective-permute-start.13 = (bf16[2,224,128]{2,1,0:T(8,128)(2,1)S(1)}, bf16[2,224,128]{2,1,0:T(8,128)(2,1)S(1)}, u32[]{:S(2)}, u32[]{:S(2)}) collective-permute-start(bf16[2,224,128]{2,1,0:T(8,128)(2,1)S(1)} %get-tuple-element.56), channel_id=1, source_target_pairs={{0,48},{16,32},{32,16},{48,0},{64,112},{80,96},{96,80},{112,64},{1... | collective-permute-start | bytes 344072 | tf_op jit(solution)/shard_map/ppermute | solution.py:45
  54.5 7.1 %collective-permute-start.14 = (bf16[2,224,128]{2,1,0:T(8,128)(2,1)S(1)}, bf16[2,224,128]{2,1,0:T(8,128)(2,1)S(1)}, u32[]{:S(2)}, u32[]{:S(2)}) collective-permute-start(bf16[2,224,128]{2,1,0:T(8,128)(2,1)S(1)} %get-tuple-element.57), channel_id=1, source_target_pairs={{0,64},{16,80},{32,96},{48,112},{64,0},{80,16},{96,32},{112,48},{1... | collective-permute-start | bytes 344072 | tf_op jit(solution)/shard_map/ppermute | solution.py:45
  58.0 6.9 %collective-permute-start.15 = (bf16[2,224,128]{2,1,0:T(8,128)(2,1)S(1)}, bf16[2,224,128]{2,1,0:T(8,128)(2,1)S(1)}, u32[]{:S(2)}, u32[]{:S(2)}) collective-permute-start(bf16[2,224,128]{2,1,0:T(8,128)(2,1)S(1)} %get-tuple-element.58), channel_id=1, source_target_pairs={{0,112},{16,96},{32,80},{48,64},{64,48},{80,32},{96,16},{112,0},{1... | collective-permute-start | bytes 344072 | tf_op jit(solution)/shard_map/ppermute | solution.py:45
  66.0 10.8 %collective-permute-start.16 = (bf16[208,256]{1,0:T(8,128)(2,1)S(1)}, bf16[208,256]{1,0:T(8,128)(2,1)S(1)}, u32[]{:S(2)}, u32[]{:S(2)}) collective-permute-start(bf16[208,256]{1,0:T(8,128)(2,1)S(1)} %get-tuple-element.60), channel_id=1, source_target_pairs={{0,1},{1,0},{2,3},{3,2},{4,5},{5,4},{6,7},{7,6},{8,9},{9,8},{10,11... | collective-permute-start | bytes 319496 | tf_op jit(solution)/shard_map/ppermute | solution.py:45
  68.8 10.8 %collective-permute-start.17 = (bf16[208,256]{1,0:T(8,128)(2,1)S(1)}, bf16[208,256]{1,0:T(8,128)(2,1)S(1)}, u32[]{:S(2)}, u32[]{:S(2)}) collective-permute-start(bf16[208,256]{1,0:T(8,128)(2,1)S(1)} %get-tuple-element.61), channel_id=1, source_target_pairs={{0,2},{1,3},{2,0},{3,1},{4,6},{5,7},{6,4},{7,5},{8,10},{9,11},{10,... | collective-permute-start | bytes 319496 | tf_op jit(solution)/shard_map/ppermute | solution.py:45
  69.9 10.4 %collective-permute-start.18 = (bf16[208,256]{1,0:T(8,128)(2,1)S(1)}, bf16[208,256]{1,0:T(8,128)(2,1)S(1)}, u32[]{:S(2)}, u32[]{:S(2)}) collective-permute-start(bf16[208,256]{1,0:T(8,128)(2,1)S(1)} %get-tuple-element.62), channel_id=1, source_target_pairs={{0,3},{1,2},{2,1},{3,0},{4,7},{5,6},{6,5},{7,4},{8,11},{9,10},{10,... | collective-permute-start | bytes 319496 | tf_op jit(solution)/shard_map/ppermute | solution.py:45
  71.1 9.2 %collective-permute-start.19 = (bf16[208,256]{1,0:T(8,128)(2,1)S(1)}, bf16[208,256]{1,0:T(8,128)(2,1)S(1)}, u32[]{:S(2)}, u32[]{:S(2)}) collective-permute-start(bf16[208,256]{1,0:T(8,128)(2,1)S(1)} %get-tuple-element.63), channel_id=1, source_target_pairs={{0,4},{1,5},{2,6},{3,7},{4,0},{5,1},{6,2},{7,3},{8,12},{9,13},{10,... | collective-permute-start | bytes 319496 | tf_op jit(solution)/shard_map/ppermute | solution.py:45
  73.8 8.8 %collective-permute-start.20 = (bf16[208,256]{1,0:T(8,128)(2,1)S(1)}, bf16[208,256]{1,0:T(8,128)(2,1)S(1)}, u32[]{:S(2)}, u32[]{:S(2)}) collective-permute-start(bf16[208,256]{1,0:T(8,128)(2,1)S(1)} %get-tuple-element.64), channel_id=1, source_target_pairs={{0,5},{1,4},{2,7},{3,6},{4,1},{5,0},{6,3},{7,2},{8,13},{9,12},{10,... | collective-permute-start | bytes 319496 | tf_op jit(solution)/shard_map/ppermute | solution.py:45
  76.8 6.8 %collective-permute-start.21 = (bf16[208,256]{1,0:T(8,128)(2,1)S(1)}, bf16[208,256]{1,0:T(8,128)(2,1)S(1)}, u32[]{:S(2)}, u32[]{:S(2)}) collective-permute-start(bf16[208,256]{1,0:T(8,128)(2,1)S(1)} %get-tuple-element.65), channel_id=1, source_target_pairs={{0,6},{1,7},{2,4},{3,5},{4,2},{5,3},{6,0},{7,1},{8,14},{9,15},{10,... | collective-permute-start | bytes 319496 | tf_op jit(solution)/shard_map/ppermute | solution.py:45
  79.7 8.5 %collective-permute-start.22 = (bf16[208,256]{1,0:T(8,128)(2,1)S(1)}, bf16[208,256]{1,0:T(8,128)(2,1)S(1)}, u32[]{:S(2)}, u32[]{:S(2)}) collective-permute-start(bf16[208,256]{1,0:T(8,128)(2,1)S(1)} %get-tuple-element.66), channel_id=1, source_target_pairs={{0,7},{1,6},{2,5},{3,4},{4,3},{5,2},{6,1},{7,0},{8,15},{9,14},{10,... | collective-permute-start | bytes 319496 | tf_op jit(solution)/shard_map/ppermute | solution.py:45
  88.4 9.4 %collective-permute-start.29 = (bf16[208,256]{1,0:T(8,128)(2,1)S(1)}, bf16[208,256]{1,0:T(8,128)(2,1)S(1)}, u32[]{:S(2)}, u32[]{:S(2)}) collective-permute-start(bf16[208,256]{1,0:T(8,128)(2,1)S(1)} %add_convert_fusion.1.refs_0_), channel_id=1, source_target_pairs={{0,7},{1,6},{2,5},{3,4},{4,3},{5,2},{6,1},{7,0},{8,15},{9,14},{10,... | collective-permute-start | bytes 319496 | tf_op jit(solution)/shard_map/ppermute | solution.py:45
  88.8 10.9 %collective-permute-start.28 = (bf16[208,256]{1,0:T(8,128)(2,1)S(1)}, bf16[208,256]{1,0:T(8,128)(2,1)S(1)}, u32[]{:S(2)}, u32[]{:S(2)}) collective-permute-start(bf16[208,256]{1,0:T(8,128)(2,1)S(1)} %add_convert_fusion.1.refs_0_), channel_id=1, source_target_pairs={{0,6},{1,7},{2,4},{3,5},{4,2},{5,3},{6,0},{7,1},{8,14},{9,15},{10,... | collective-permute-start | bytes 319496 | tf_op jit(solution)/shard_map/ppermute | solution.py:45
  91.7 10.9 %collective-permute-start.27 = (bf16[208,256]{1,0:T(8,128)(2,1)S(1)}, bf16[208,256]{1,0:T(8,128)(2,1)S(1)}, u32[]{:S(2)}, u32[]{:S(2)}) collective-permute-start(bf16[208,256]{1,0:T(8,128)(2,1)S(1)} %add_convert_fusion.1.refs_0_), channel_id=1, source_target_pairs={{0,5},{1,4},{2,7},{3,6},{4,1},{5,0},{6,3},{7,2},{8,13},{9,12},{10,... | collective-permute-start | bytes 319496 | tf_op jit(solution)/shard_map/ppermute | solution.py:45
  92.6 10.0 %collective-permute-start.26 = (bf16[208,256]{1,0:T(8,128)(2,1)S(1)}, bf16[208,256]{1,0:T(8,128)(2,1)S(1)}, u32[]{:S(2)}, u32[]{:S(2)}) collective-permute-start(bf16[208,256]{1,0:T(8,128)(2,1)S(1)} %add_convert_fusion.1.refs_0_), channel_id=1, source_target_pairs={{0,4},{1,5},{2,6},{3,7},{4,0},{5,1},{6,2},{7,3},{8,12},{9,13},{10,... | collective-permute-start | bytes 319496 | tf_op jit(solution)/shard_map/ppermute | solution.py:45
  97.6 8.2 %collective-permute-start.25 = (bf16[208,256]{1,0:T(8,128)(2,1)S(1)}, bf16[208,256]{1,0:T(8,128)(2,1)S(1)}, u32[]{:S(2)}, u32[]{:S(2)}) collective-permute-start(bf16[208,256]{1,0:T(8,128)(2,1)S(1)} %add_convert_fusion.1.refs_0_), channel_id=1, source_target_pairs={{0,3},{1,2},{2,1},{3,0},{4,7},{5,6},{6,5},{7,4},{8,11},{9,10},{10,... | collective-permute-start | bytes 319496 | tf_op jit(solution)/shard_map/ppermute | solution.py:45
  97.7 8.1 %collective-permute-start.24 = (bf16[208,256]{1,0:T(8,128)(2,1)S(1)}, bf16[208,256]{1,0:T(8,128)(2,1)S(1)}, u32[]{:S(2)}, u32[]{:S(2)}) collective-permute-start(bf16[208,256]{1,0:T(8,128)(2,1)S(1)} %add_convert_fusion.1.refs_0_), channel_id=1, source_target_pairs={{0,2},{1,3},{2,0},{3,1},{4,6},{5,7},{6,4},{7,5},{8,10},{9,11},{10,... | collective-permute-start | bytes 319496 | tf_op jit(solution)/shard_map/ppermute | solution.py:45
  99.7 6.8 %collective-permute-start.23 = (bf16[208,256]{1,0:T(8,128)(2,1)S(1)}, bf16[208,256]{1,0:T(8,128)(2,1)S(1)}, u32[]{:S(2)}, u32[]{:S(2)}) collective-permute-start(bf16[208,256]{1,0:T(8,128)(2,1)S(1)} %add_convert_fusion.1.refs_0_), channel_id=1, source_target_pairs={{0,1},{1,0},{2,3},{3,2},{4,5},{5,4},{6,7},{7,6},{8,9},{9,8},{10,11... | collective-permute-start | bytes 319496 | tf_op jit(solution)/shard_map/ppermute | solution.py:45
  109.0 11.1 %collective-permute-start.30 = (bf16[208,256]{1,0:T(8,128)(2,1)S(1)}, bf16[208,256]{1,0:T(8,128)(2,1)S(1)}, u32[]{:S(2)}, u32[]{:S(2)}) collective-permute-start(bf16[208,256]{1,0:T(8,128)(2,1)S(1)} %get-tuple-element.68), channel_id=1, source_target_pairs={{0,1},{1,0},{2,3},{3,2},{4,5},{5,4},{6,7},{7,6},{8,9},{9,8},{10,11... | collective-permute-start | bytes 319496 | tf_op jit(solution)/shard_map/ppermute | solution.py:45
  112.1 8.0 %collective-permute-start.31 = (bf16[208,256]{1,0:T(8,128)(2,1)S(1)}, bf16[208,256]{1,0:T(8,128)(2,1)S(1)}, u32[]{:S(2)}, u32[]{:S(2)}) collective-permute-start(bf16[208,256]{1,0:T(8,128)(2,1)S(1)} %get-tuple-element.69), channel_id=1, source_target_pairs={{0,2},{1,3},{2,0},{3,1},{4,6},{5,7},{6,4},{7,5},{8,10},{9,11},{10,... | collective-permute-start | bytes 319496 | tf_op jit(solution)/shard_map/ppermute | solution.py:45
  112.1 11.2 %collective-permute-start.32 = (bf16[208,256]{1,0:T(8,128)(2,1)S(1)}, bf16[208,256]{1,0:T(8,128)(2,1)S(1)}, u32[]{:S(2)}, u32[]{:S(2)}) collective-permute-start(bf16[208,256]{1,0:T(8,128)(2,1)S(1)} %get-tuple-element.70), channel_id=1, source_target_pairs={{0,3},{1,2},{2,1},{3,0},{4,7},{5,6},{6,5},{7,4},{8,11},{9,10},{10,... | collective-permute-start | bytes 319496 | tf_op jit(solution)/shard_map/ppermute | solution.py:45
  114.1 9.2 %collective-permute-start.33 = (bf16[208,256]{1,0:T(8,128)(2,1)S(1)}, bf16[208,256]{1,0:T(8,128)(2,1)S(1)}, u32[]{:S(2)}, u32[]{:S(2)}) collective-permute-start(bf16[208,256]{1,0:T(8,128)(2,1)S(1)} %get-tuple-element.71), channel_id=1, source_target_pairs={{0,4},{1,5},{2,6},{3,7},{4,0},{5,1},{6,2},{7,3},{8,12},{9,13},{10,... | collective-permute-start | bytes 319496 | tf_op jit(solution)/shard_map/ppermute | solution.py:45
  114.9 8.6 %collective-permute-start.34 = (bf16[208,256]{1,0:T(8,128)(2,1)S(1)}, bf16[208,256]{1,0:T(8,128)(2,1)S(1)}, u32[]{:S(2)}, u32[]{:S(2)}) collective-permute-start(bf16[208,256]{1,0:T(8,128)(2,1)S(1)} %get-tuple-element.72), channel_id=1, source_target_pairs={{0,5},{1,4},{2,7},{3,6},{4,1},{5,0},{6,3},{7,2},{8,13},{9,12},{10,... | collective-permute-start | bytes 319496 | tf_op jit(solution)/shard_map/ppermute | solution.py:45
  120.1 8.4 %collective-permute-start.36 = (bf16[208,256]{1,0:T(8,128)(2,1)S(1)}, bf16[208,256]{1,0:T(8,128)(2,1)S(1)}, u32[]{:S(2)}, u32[]{:S(2)}) collective-permute-start(bf16[208,256]{1,0:T(8,128)(2,1)S(1)} %get-tuple-element.74), channel_id=1, source_target_pairs={{0,7},{1,6},{2,5},{3,4},{4,3},{5,2},{6,1},{7,0},{8,15},{9,14},{10,... | collective-permute-start | bytes 319496 | tf_op jit(solution)/shard_map/ppermute | solution.py:45
  (16 other events, 487.1 us)

commit v4 on v3

--- a/solution.py
+++ b/solution.py
@@ -45,6 +45,17 @@
     return lax.ppermute(x, axes, [(i, i ^ mask) for i in range(size)])
 
 
+def cross(x, kind, flip):
+    masks = {0: (0, 0), 1: (1, 3), 2: (3, 1), 3: (2, 2)}[kind]
+    perm = []
+    for core in range(2):
+        for z in range(4):
+            for hi in range(2):
+                there = (core * 4 + (z ^ masks[core])) * 2 + (hi ^ flip)
+                perm.append(((core * 4 + z) * 2 + hi, there))
+    return lax.ppermute(x, ("core", "z", "xhi"), perm)
+
+
 def scale_of(pieces, width):
     total = jnp.sum(pieces[0] * pieces[0], axis=-1, keepdims=True)
     for piece in pieces[1:]:
@@ -67,7 +78,7 @@
     ]
     for c in copies:
         c.start()
-    me = me_ref[0]
+    me = me_ref[2]
     width = pairs[0].shape[2]
     hd = qg.shape[1]
     xs = [p[i].astype(F32) for p in pairs for i in range(2)]
@@ -83,7 +94,8 @@
         dk = jnp.dot(x, wk[rows, :], preferred_element_type=F32)
         dv = jnp.dot(x, wv[rows, :], preferred_element_type=F32)
         q, k, v = (dq, dk, dv) if q is None else (q + dq, k + dk, v + dv)
-    c, s = cos[...], sin[...]
+    c = cos[...].reshape(q.shape[0], hd)
+    s = sin[...].reshape(q.shape[0], hd)
     for h in range(q.shape[1] // hd):
         part = q[:, h * hd : (h + 1) * hd]
         q_out[:, h * hd : (h + 1) * hd] = rotate(head_norm(part) * qg[...], c, s).astype(BF16)
@@ -270,11 +282,9 @@
     )(ids, table, kpos, key_index, query_index, cos, sin, *queries, *fresh, *cached)
 
 
-def merge_kernel(n, count, me_ref, *refs):
-    parts, wo, outs = refs[:4], refs[4], refs[5:]
-    me = me_ref[0]
+def merge_kernel(count, *refs):
+    parts, out = refs[:4], refs[4]
     hd = parts[0].shape[2]
-    width = outs[0].shape[1]
     turn = identity(2 * count, 2 * hd, 4 * count)
     tops, sums = [], []
     for part in parts:
@@ -300,29 +310,38 @@
         )
         for h in range(2):
             rows[h].append(acc[h * count : (h + 1) * count])
-    att = jnp.concatenate([jnp.concatenate(r, 0) for r in rows], 1).astype(BF16)
+    out[...] = jnp.concatenate([jnp.concatenate(r, 0) for r in rows], 1).astype(BF16)
+
+
+def feed_kernel(n, ids, *refs):
+    pieces, pairs = refs[:n], refs[n : n + n // 2]
+    wo_own = refs[n + n // 2 : 2 * n]
+    wo_sibling = refs[2 * n : 2 * n + n // 2]
+    gain, wg, wu, wd = refs[2 * n + n // 2 : 2 * n + n // 2 + 4]
+    outs, mine = refs[2 * n + n // 2 + 4 : -2], refs[-2]
+    stream = refs[-1]
+    me, core = ids[2], ids[3]
+    width = pieces[0].shape[1]
+    half = width // 2
+    total = None
+    for weights, which in ((wo_own, core), (wo_sibling, 1 - core)):
+        cols = pl.ds(pl.multiple_of(which * half, half), half)
+        for i, weight in enumerate(weights):
+            x = jnp.concatenate([pieces[2 * i][:, cols], pieces[2 * i + 1][:, cols]], axis=1)
+            part = jnp.dot(x, weight[...], preferred_element_type=F32)
+            total = part if total is None else total + part
+    stream[...] = total
     for step in range(n):
         src = jnp.bitwise_xor(me, step)
         cols = pl.ds(pl.multiple_of(src * width, width), width)
-        outs[step][...] = jnp.dot(att, wo[:, cols], preferred_element_type=F32).astype(BF16)
-
-
-def feed_kernel(n, me_ref, *refs):
-    pieces = refs[:n]
-    gain, wg, wu, wd = refs[n : n + 4]
-    outs = refs[n + 4 :]
-    me = me_ref[0]
-    width = pieces[0].shape[1]
-    xs = [p[...].astype(F32) for p in pieces]
-    scale = scale_of(xs, n * width)
-    g = u = None
-    for step in range(n):
-        src = jnp.bitwise_xor(me, step)
-        rows = pl.ds(pl.multiple_of(src * width, width), width)
-        x = (xs[step] * scale * gain[rows].astype(F32)[None, :]).astype(BF16)
-        dg = jnp.dot(x, wg[rows, :], preferred_element_type=F32)
-        du = jnp.dot(x, wu[rows, :], preferred_element_type=F32)
-        g, u = (dg, du) if g is None else (g + dg, u + du)
+        stream[:, cols] = stream[:, cols] + pairs[step // 2][step % 2].astype(F32)
+        if step == 0:
+            mine[...] = stream[:, cols].astype(BF16)
+    xs = stream[...].astype(BF16).astype(F32)
+    scale = scale_of([xs], n * width)
+    x = (xs * scale * gain[...].astype(F32)[None, :]).astype(BF16)
+    g = jnp.dot(x, wg[...], preferred_element_type=F32)
+    u = jnp.dot(x, wu[...], preferred_element_type=F32)
     active = (g / (1.0 + jnp.exp(-g)) * u).astype(BF16)
     for step in range(n):
         src = jnp.bitwise_xor(me, step)
@@ -360,10 +379,15 @@
     def shaped(*shape, dtype=BF16):
         return jax.ShapeDtypeStruct(shape, dtype)
 
+    def rows_at(array, start, size):
+        return lax.dynamic_slice(array, (start, 0), (size, array.shape[1]), allow_negative_indices=False)
+
+    hidden = selected_hidden.reshape(rows, width)
+    half = output_weight.shape[0] // 2
     xy = lax.axis_index(("xlo", "yhi"))
-    mk = lax.axis_index(("ylo", "core"))
-    me = lax.axis_index(TP).reshape(1)
-    first_slot = lax.axis_index(SEQ) * slot_local
+    core = lax.axis_index("core")
+    seq = lax.axis_index(SEQ)
+    ids = jnp.stack([xy, lax.axis_index(("ylo", "core")), lax.axis_index(TP), core])
 
     number = lax.broadcasted_iota(jnp.int32, span_order.shape, 0) * spans
     number = number + lax.broadcasted_iota(jnp.int32, span_order.shape, 1)
@@ -371,23 +395,30 @@
     place = jnp.sum(jnp.where(hit, span_order[None], 0), axis=(1, 2))
     start = jnp.sum(jnp.where(hit, cache_start[None], 0), axis=(1, 2))
     table = jnp.concatenate([slot_spans // spans, place])
-    ids = jnp.stack([xy, mk])
-    base_here = lax.dynamic_slice_in_dim(place * span, first_slot, slot_local, 0)
-
-    hidden = selected_hidden.reshape(rows, width)
+
     pair = jnp.stack([hidden, swap(hidden, "xhi", 1, 2)])
 
-    pair, selected_later = lax.optimization_barrier((pair, selected_index))
+    output_half = rows_at(output_weight, core * half, half)
+    pair, selected_later, place, start, ids, at_group, *at_slots = lax.optimization_barrier(
+        (pair, selected_index, place, start, ids, xy * 8)
+        + tuple(jnp.bitwise_xor(seq, 2 * k) * slot_local for k in (0,) + FAR_MASKS)
+    )
+    output_x = swap(output_half, "xhi", 1, 2)
     pairs = [pair] + [swap(pair, "z", k, 4) for k in (1, 2, 3)]
 
     cached = jnp.concatenate([cached_keys, cached_values], axis=0)
     cached_y = swap(cached, "ylo", 1, 2)
     cached_core = swap(cached, "core", 1, 2)
 
-    index_here = lax.dynamic_slice_in_dim(selected_later, first_slot, slot_local, 0)
-    qc, qs = rotation_tables(base_here[:, None] + index_here, hd)
-    qc, qs = qc.reshape(rows, hd), qs.reshape(rows, hd)
+    base_here = rows_at((place * span)[:, None], at_slots[0], slot_local)
+    index_here = rows_at(selected_later, at_slots[0], slot_local)
+    qc, qs = rotation_tables(base_here + index_here, hd)
     qg, kg = query_gain.astype(F32)[None], key_gain.astype(F32)[None]
+    output_half, output_x, pairs[1] = lax.optimization_barrier(
+        (output_half, output_x, pairs[1])
+    )
+    wo_0 = jnp.concatenate([output_half, output_x], axis=0)
+    wo_1 = cross(wo_0, 1, 0)
     pairs[0], qg, kg, qc, qs, ids, table, cached_core = lax.optimization_barrier(
         (pairs[0], qg, kg, qc, qs, ids, table, cached_core)
     )
@@ -403,7 +434,7 @@
         compiler_params=grant(10),
         name="project",
     )(
-        me,
+        ids,
         *pairs,
         input_gain,
         qg,
@@ -422,22 +453,20 @@
     fresh_set = [fresh, swap(fresh, "core", 1, 2), fresh_y, swap(fresh_y, "core", 1, 2)]
     query_set = [queries] + [swap(queries, ROUND, k, 8) for k in FAR_MASKS]
 
-    group_index = lax.dynamic_slice_in_dim(selected_last, xy * 8, 8, 0)
+    group_index = rows_at(selected_last, at_group, 8)
     token = jnp.arange(span, dtype=jnp.int32)
     taken = jnp.any(group_index[:, :, None] == token[None, None, :], axis=1)
     kpos = jnp.where(taken, FAR, token[None, :].astype(F32))
-    seq = lax.axis_index(SEQ)
     query_index = jnp.concatenate(
-        [
-            lax.dynamic_slice_in_dim(
-                selected_last, jnp.bitwise_xor(seq, 2 * k) * slot_local, slot_local, 0
-            )
-            for k in (0,) + FAR_MASKS
-        ],
-        axis=0,
-    )
-
-    shift = lax.dynamic_slice_in_dim(place * span - start, xy * 8, 8, 0)
+        [rows_at(selected_last, at, slot_local) for at in at_slots], axis=0
+    )
+    query_set[1], wo_1 = lax.optimization_barrier((query_set[1], wo_1))
+    wo_2 = cross(wo_0, 2, 0)
+    wo_3 = cross(wo_1, 2, 0)
+    wo_0, wo_1, query_set[3] = lax.optimization_barrier((wo_0, wo_1, query_set[3]))
+    wo_0c, wo_1c = swap(wo_0, "core", 1, 2), swap(wo_1, "core", 1, 2)
+
+    shift = rows_at((place * span - start)[:, None], at_group, 8)[:, 0]
     kc, ks = rotation_tables(-shift, hd)
     parts = attend(
         ids,
@@ -451,32 +480,43 @@
         fresh_set,
         cached_set,
     )
+    *parts, wo_0c, wo_1c = lax.optimization_barrier((*parts, wo_0c, wo_1c))
     parts = [parts[0]] + [swap(part, ROUND, k, 8) for part, k in zip(parts[1:], FAR_MASKS)]
 
-    projected = pl.pallas_call(
-        functools.partial(merge_kernel, n, count),
-        in_specs=[SMEM] + [VMEM] * 5,
-        out_specs=[VMEM] * n,
-        out_shape=[shaped(rows, width)] * n,
+    attended = pl.pallas_call(
+        functools.partial(merge_kernel, count),
+        in_specs=[VMEM] * 4,
+        out_specs=VMEM,
+        out_shape=shaped(rows, width),
         compiler_params=grant(8),
         name="merge",
-    )(me, *parts, output_weight)
-    total = hidden.astype(F32) + projected[0].astype(F32)
-    for k in range(1, n):
-        total = total + swap(projected[k], TP, k, n).astype(F32)
-    stream = total.astype(BF16)
-
-    pieces = [stream] + [swap(stream, TP, k, n) for k in range(1, n)]
-    downs = pl.pallas_call(
+    )(*parts)
+    order = [(kind, flip) for kind in range(4) for flip in range(2)]
+    wo_2, wo_3, attended = lax.optimization_barrier((wo_2, wo_3, attended))
+    wo_2c, wo_3c = swap(wo_2, "core", 1, 2), swap(wo_3, "core", 1, 2)
+    wo_own = [wo_0, wo_1, wo_2, wo_3]
+    wo_2c, wo_3c, later = lax.optimization_barrier((wo_2c, wo_3c, attended))
+    pieces = [attended] + [
+        cross(attended if i < 3 else later, kind, flip)
+        for i, (kind, flip) in enumerate(order[1:])
+    ]
+    *downs, stream = pl.pallas_call(
         functools.partial(feed_kernel, n),
-        in_specs=[SMEM] + [VMEM] * (n + 4),
-        out_specs=[VMEM] * n,
-        out_shape=[shaped(rows, width)] * n,
-        compiler_params=grant(18),
+        in_specs=[SMEM] + [VMEM] * (2 * n + n // 2 + 4),
+        out_specs=[VMEM] * (n + 1),
+        out_shape=[shaped(rows, width)] * (n + 1),
+        scratch_shapes=[pltpu.VMEM((rows, n * width), F32)],
+        compiler_params=grant(20),
         name="feed",
     )(
-        me,
+        ids,
         *pieces,
+        *pairs,
+        *wo_own,
+        wo_0c,
+        wo_2c,
+        wo_1c,
+        wo_3c,
         post_gain,
         gate_weight,
         up_weight,

time: 130 us -> 117 us (0.900)
  starting transfers between devices: 67.1 us -> 61.1 us
  waiting for transfers between devices: 37.1 us -> 31.5 us
  other arithmetic: 6.85 us -> 3.09 us
  Pallas kernels: 13.4 us -> 15 us
    ppermute x37 -> x28, starting transfers between devices: 67.1 us -> 41.5 us  [swap(): return lax.ppermute(x, axes, [(i, i ^ mask) for i in range(size)])]
    ppermute x0 -> x10, starting transfers between devices: none -> 19.6 us  [cross(): return lax.ppermute(x, ('core', 'z', 'xhi'), perm)]
    ppermute x37 -> x28, waiting for transfers between devices: 37.1 us -> 23.7 us  [swap(): return lax.ppermute(x, axes, [(i, i ^ mask) for i in range(size)])]
    ppermute x0 -> x10, waiting for transfers between devices: none -> 7.81 us  [cross(): return lax.ppermute(x, ('core', 'z', 'xhi'), perm)]
    pallas_call x1, Pallas kernels: 2.5 us -> 5.2 us  [on_device(): pl.pallas_call(functools.partial(feed_kernel, n), in_specs=[SMEM] + [VMEM...]
    unnamed x23 -> x34, local copies, waits for them, and re-layouts: 3.29 us -> 2.37 us
  transfers between devices with their start and end apart: 37 -> 38, of which waited for: 17 -> 16; matrix products, arithmetic and copies ran while one was open for 5% -> 5% of each run, Pallas kernels for 2% -> 8%
where the time goes in v4:
time: 117 us
  starting transfers between devices  61.1 us (52%)
  waiting for transfers between devices  31.5 us (27%)
  Pallas kernels  15 us (13%)
  local copies, waits for them, and re-layouts  5.49 us (5%)
  other arithmetic  3.09 us (3%)
    ppermute x28, starting transfers between devices, swap(): return lax.ppermute(x, axes, [(i, i ^ mask) for i in range(size)])  41.5 us
    ppermute x28, waiting for transfers between devices, swap(): return lax.ppermute(x, axes, [(i, i ^ mask) for i in range(size)])  23.7 us
    ppermute x10, starting transfers between devices, cross(): return lax.ppermute(x, ('core', 'z', 'xhi'), perm)  19.6 us
    ppermute x10, waiting for transfers between devices, cross(): return lax.ppermute(x, ('core', 'z', 'xhi'), perm)  7.81 us
    pallas_call x1, Pallas kernels, attend(): pl.pallas_call(functools.partial(attend_kernel, count), in_specs=[SMEM, S...  6.92 us
    pallas_call x1, Pallas kernels, on_device(): pl.pallas_call(functools.partial(feed_kernel, n), in_specs=[SMEM] + [VMEM...  5.2 us
    unnamed x34, local copies, waits for them, and re-layouts  2.37 us
  transfers between devices with their start and end apart: 38, of which 16 were waited for; matrix products, arithmetic and copies ran while one was open for 5% of the time, Pallas kernels for 8%

profile of v4, /device:TPU:0, one launch (start us, length us, event | category | flops | bytes accessed | tf_op | source)
XLA Modules:
  0.0 116.6 jit_solution(1442128818107032958)
XLA Ops:
  2.4 1.7 %collective-permute-start.10 = (bf16[4,1024,128]{2,1,0:T(8,128)(2,1)S(1)}, bf16[4,1024,128]{2,1,0:T(8,128)(2,1)}, u32[]{:S(2)}, u32[]{:S(2)}) collective-permute-start(bf16[4,1024,128]{2,1,0:T(8,128)(2,1)S(1)} %constant_dynamic-update-slice_fusion.refs_8_), channel_id=1, source_target_pairs={{0,16},{16,0},{1,17},{17,1},{2,18},{18,2},{3,19},{19,3},{4,20},{20... | collective-permute-start | bytes 3145736 | tf_op jit(solution)/shard_map/ppermute | solution.py:45
  4.2 3.0 %collective-permute-start = (bf16[208,256]{1,0:T(8,128)(2,1)}, bf16[208,256]{1,0:T(8,128)(2,1)S(1)}, u32[]{:S(2)}, u32[]{:S(2)}) collective-permute-start(bf16[208,256]{1,0:T(8,128)(2,1)} %bitcast.14), channel_id=1, source_target_pairs={{0,1},{1,0},{2,3},{3,2},{4,5},{5,4},{6,7},{7,6},{8,9},{9,8},{10,11... | collective-permute-start | bytes 319496 | tf_op jit(solution)/shard_map/ppermute | solution.py:45
  8.9 2.3 %collective-permute-done = bf16[208,256]{1,0:T(8,128)(2,1)S(1)} collective-permute-done((bf16[208,256]{1,0:T(8,128)(2,1)}, bf16[208,256]{1,0:T(8,128)(2,1)S(1)}, u32[]{:S(2)}, u32[]{:S(2)}) %collective-permute-start) | collective-permute-done | bytes 106528 | tf_op jit(solution)/shard_map/ppermute | solution.py:45
  11.3 2.0 %collective-permute-start.3 = (bf16[2,208,256]{2,1,0:T(8,128)(2,1)S(1)}, bf16[2,208,256]{2,1,0:T(8,128)(2,1)S(1)}, u32[]{:S(2)}, u32[]{:S(2)}) collective-permute-start(bf16[2,208,256]{2,1,0:T(8,128)(2,1)S(1)} %pad_maximum_fusion.refs_0_.refs_8_), channel_id=1, source_target_pairs={{0,2},{2,0},{4,6},{6,4},{1,3},{3,1},{5,7},{7,5},{8,10},{10,8},{12,... | collective-permute-start | bytes 638984 | tf_op jit(solution)/shard_map/ppermute | solution.py:45
  13.3 2.6 %collective-permute-start.6 = (bf16[2,208,256]{2,1,0:T(8,128)(2,1)S(1)}, bf16[2,208,256]{2,1,0:T(8,128)(2,1)S(1)}, u32[]{:S(2)}, u32[]{:S(2)}) collective-permute-start(bf16[2,208,256]{2,1,0:T(8,128)(2,1)S(1)} %pad_maximum_fusion.refs_0_.refs_8_), channel_id=1, source_target_pairs={{0,6},{2,4},{4,2},{6,0},{1,7},{3,5},{5,3},{7,1},{8,14},{10,12},{12... | collective-permute-start | bytes 638984 | tf_op jit(solution)/shard_map/ppermute | solution.py:45
  15.9 2.5 %collective-permute-done.3.refs_1_.refs_9_ = bf16[2,208,256]{2,1,0:T(8,128)(2,1)S(1)} collective-permute-done((bf16[2,208,256]{2,1,0:T(8,128)(2,1)S(1)}, bf16[2,208,256]{2,1,0:T(8,128)(2,1)S(1)}, u32[]{:S(2)}, u32[]{:S(2)}) %collective-permute-start.3) | collective-permute-done | bytes 213024 | tf_op jit(solution)/shard_map/ppermute | solution.py:45
  18.4 3.7 %collective-permute-start.5 = (bf16[2,208,256]{2,1,0:T(8,128)(2,1)S(1)}, bf16[2,208,256]{2,1,0:T(8,128)(2,1)S(1)}, u32[]{:S(2)}, u32[]{:S(2)}) collective-permute-start(bf16[2,208,256]{2,1,0:T(8,128)(2,1)S(1)} %pad_maximum_fusion.refs_0_.refs_8_), channel_id=1, source_target_pairs={{0,4},{2,6},{4,0},{6,2},{1,5},{3,7},{5,1},{7,3},{8,12},{10,14},{12... | collective-permute-start | bytes 638984 | tf_op jit(solution)/shard_map/ppermute | solution.py:45
  22.1 1.8 %collective-permute-done.2 = bf16[128,2048]{1,0:T(8,128)(2,1)} collective-permute-done((bf16[128,2048]{1,0:T(8,128)(2,1)}, bf16[128,2048]{1,0:T(8,128)(2,1)}, u32[]{:S(2)}, u32[]{:S(2)}) %collective-permute-start.2) | collective-permute-done | bytes 524320 | tf_op jit(solution)/shard_map/ppermute | solution.py:45
  26.1 2.0 %collective-permute-start.8 = (bf16[256,2048]{1,0:T(8,128)(2,1)S(1)}, bf16[256,2048]{1,0:T(8,128)(2,1)S(1)}, u32[]{:S(2)}, u32[]{:S(2)}) collective-permute-start(bf16[256,2048]{1,0:T(8,128)(2,1)S(1)} %constant_dynamic-update-slice_fusion.2.refs_12_), channel_id=1, source_target_pairs={{0,2},{1,3},{2,0},{3,1},{4,6},{5,7},{6,4},{7,5},{8,14},{9,15},{10,... | collective-permute-start | bytes 3145736 | tf_op jit(solution)/shard_map/ppermute | solution.py:56
  28.9 2.1 %project.1 = (bf16[208,256]{1,0:T(8,128)(2,1)S(1)}, bf16[208,256]{1,0:T(8,128)(2,1)S(1)}) custom-call(s32[4]{0:T(128)S(1)} %pad_add_fusion.1.me_ref.ids, bf16[2,208,256]{2,1,0:T(8,128)(2,1)S(1)} %pad_maximum_fusion.refs_0_.refs_8_, bf16[2,208,256]{2,1,0:T(8,128)(2,1)S(1)} %collective-permute-done.3.refs_1_.refs_9_, ...), custom_call_target="tpu_custom_call" | custom-call | tf_op jit(solution)/shard_map/project/pallas_call | solution.py:425
  31.0 2.3 %collective-permute-start.12 = (bf16[208,256]{1,0:T(8,128)(2,1)S(1)}, bf16[208,256]{1,0:T(8,128)(2,1)S(1)}, u32[]{:S(2)}, u32[]{:S(2)}) collective-permute-start(bf16[208,256]{1,0:T(8,128)(2,1)S(1)} %get-tuple-element.75.refs_0_), channel_id=1, source_target_pairs={{0,112},{16,96},{32,80},{48,64},{64,48},{80,32},{96,16},{112,0},{1... | collective-permute-start | bytes 319496 | tf_op jit(solution)/shard_map/ppermute | solution.py:45
  35.9 5.7 %collective-permute-done.7.refs_1_ = bf16[208,256]{1,0:T(8,128)(2,1)S(1)} collective-permute-done((bf16[208,256]{1,0:T(8,128)(2,1)S(1)}, bf16[208,256]{1,0:T(8,128)(2,1)S(1)}, u32[]{:S(2)}, u32[]{:S(2)}) %collective-permute-start.7) | collective-permute-done | bytes 106528 | tf_op jit(solution)/shard_map/ppermute | solution.py:45
  42.9 2.9 %collective-permute-start.4 = (bf16[256,2048]{1,0:T(8,128)(2,1)S(1)}, bf16[256,2048]{1,0:T(8,128)(2,1)S(1)}, u32[]{:S(2)}, u32[]{:S(2)}) collective-permute-start(bf16[256,2048]{1,0:T(8,128)(2,1)S(1)} %constant_dynamic-update-slice_fusion.2.refs_12_), channel_id=1, source_target_pairs={{0,6},{1,7},{2,4},{3,5},{4,2},{5,3},{6,0},{7,1},{8,10},{9,11},{10,... | collective-permute-start | bytes 3145736 | tf_op jit(solution)/shard_map/ppermute | solution.py:56
  47.4 6.9 %attend.1 = (bf16[2,224,128]{2,1,0:T(8,128)(2,1)S(1)}, bf16[2,224,128]{2,1,0:T(8,128)(2,1)S(1)}, bf16[2,224,128]{2,1,0:T(8,128)(2,1)S(1)}, bf16[2,224,128]{2,1,0:T(8,128)(2,1)S(1)}) custom-call(s32[4]{0:T(128)S(1)} %pad_add_fusion.1.me_ref.ids, s32[64]{0:T(128)S(1)} %pad_add_fusion.2.tab, f32[8,1024]{1,0:T(8,128)S(1)} %broadcast_select_fusion.kpos, ...), custom_call_target="tpu_custom_call" | custom-call | tf_op jit(solution)/shard_map/attend/pallas_call | solution.py:262
  54.4 5.8 %collective-permute-start.19 = (bf16[2,224,128]{2,1,0:T(8,128)(2,1)S(1)}, bf16[2,224,128]{2,1,0:T(8,128)(2,1)S(1)}, u32[]{:S(2)}, u32[]{:S(2)}) collective-permute-start(bf16[2,224,128]{2,1,0:T(8,128)(2,1)S(1)} %get-tuple-element.97), channel_id=1, source_target_pairs={{0,48},{16,32},{32,16},{48,0},{64,112},{80,96},{96,80},{112,64},{1... | collective-permute-start | bytes 344072 | tf_op jit(solution)/shard_map/ppermute | solution.py:45
  60.2 1.6 %collective-permute-start.21 = (bf16[2,224,128]{2,1,0:T(8,128)(2,1)S(1)}, bf16[2,224,128]{2,1,0:T(8,128)(2,1)S(1)}, u32[]{:S(2)}, u32[]{:S(2)}) collective-permute-start(bf16[2,224,128]{2,1,0:T(8,128)(2,1)S(1)} %get-tuple-element.99), channel_id=1, source_target_pairs={{0,112},{16,96},{32,80},{48,64},{64,48},{80,32},{96,16},{112,0},{1... | collective-permute-start | bytes 344072 | tf_op jit(solution)/shard_map/ppermute | solution.py:45
  61.7 1.7 %collective-permute-done.19.refs_1_ = bf16[2,224,128]{2,1,0:T(8,128)(2,1)S(1)} collective-permute-done((bf16[2,224,128]{2,1,0:T(8,128)(2,1)S(1)}, bf16[2,224,128]{2,1,0:T(8,128)(2,1)S(1)}, u32[]{:S(2)}, u32[]{:S(2)}) %collective-permute-start.19) | collective-permute-done | bytes 114720 | tf_op jit(solution)/shard_map/ppermute | solution.py:45
  64.9 2.1 %collective-permute-done.21.refs_3_ = bf16[2,224,128]{2,1,0:T(8,128)(2,1)S(1)} collective-permute-done((bf16[2,224,128]{2,1,0:T(8,128)(2,1)S(1)}, bf16[2,224,128]{2,1,0:T(8,128)(2,1)S(1)}, u32[]{:S(2)}, u32[]{:S(2)}) %collective-permute-start.21) | collective-permute-done | bytes 114720 | tf_op jit(solution)/shard_map/ppermute | solution.py:45
  67.9 2.3 %collective-permute-done.9.refs_15_ = bf16[256,2048]{1,0:T(8,128)(2,1)S(1)} collective-permute-done((bf16[256,2048]{1,0:T(8,128)(2,1)S(1)}, bf16[256,2048]{1,0:T(8,128)(2,1)S(1)}, u32[]{:S(2)}, u32[]{:S(2)}) %collective-permute-start.9) | collective-permute-done | bytes 1048608 | tf_op jit(solution)/shard_map/ppermute | solution.py:56
  71.4 2.7 %collective-permute-start.23 = (bf16[208,256]{1,0:T(8,128)(2,1)S(1)}, bf16[208,256]{1,0:T(8,128)(2,1)S(1)}, u32[]{:S(2)}, u32[]{:S(2)}) collective-permute-start(bf16[208,256]{1,0:T(8,128)(2,1)S(1)} %merge.1.refs_0_), channel_id=1, source_target_pairs={{0,2},{1,3},{2,0},{3,1},{4,6},{5,7},{6,4},{7,5},{8,14},{9,15},{10,... | collective-permute-start | bytes 319496 | tf_op jit(solution)/shard_map/ppermute | solution.py:56
  74.1 1.6 %collective-permute-start.22 = (bf16[208,256]{1,0:T(8,128)(2,1)S(1)}, bf16[208,256]{1,0:T(8,128)(2,1)S(1)}, u32[]{:S(2)}, u32[]{:S(2)}) collective-permute-start(bf16[208,256]{1,0:T(8,128)(2,1)S(1)} %merge.1.refs_0_), channel_id=1, source_target_pairs={{0,1},{1,0},{2,3},{3,2},{4,5},{5,4},{6,7},{7,6},{8,9},{9,8},{10,11... | collective-permute-start | bytes 319496 | tf_op jit(solution)/shard_map/ppermute | solution.py:56
  75.7 3.5 %collective-permute-start.30 = (bf16[208,256]{1,0:T(8,128)(2,1)S(1)}, bf16[208,256]{1,0:T(8,128)(2,1)S(1)}, u32[]{:S(2)}, u32[]{:S(2)}) collective-permute-start(bf16[208,256]{1,0:T(8,128)(2,1)S(1)} %merge.1.refs_0_), channel_id=1, source_target_pairs={{0,5},{1,4},{2,7},{3,6},{4,1},{5,0},{6,3},{7,2},{8,13},{9,12},{10,... | collective-permute-start | bytes 319496 | tf_op jit(solution)/shard_map/ppermute | solution.py:56
  80.6 3.9 %collective-permute-start.28 = (bf16[208,256]{1,0:T(8,128)(2,1)S(1)}, bf16[208,256]{1,0:T(8,128)(2,1)S(1)}, u32[]{:S(2)}, u32[]{:S(2)}) collective-permute-start(bf16[208,256]{1,0:T(8,128)(2,1)S(1)} %merge.1.refs_0_), channel_id=1, source_target_pairs={{0,7},{1,6},{2,5},{3,4},{4,3},{5,2},{6,1},{7,0},{8,11},{9,10},{10,... | collective-permute-start | bytes 319496 | tf_op jit(solution)/shard_map/ppermute | solution.py:56
  86.1 2.8 %collective-permute-done.28.refs_5_ = bf16[208,256]{1,0:T(8,128)(2,1)S(1)} collective-permute-done((bf16[208,256]{1,0:T(8,128)(2,1)S(1)}, bf16[208,256]{1,0:T(8,128)(2,1)S(1)}, u32[]{:S(2)}, u32[]{:S(2)}) %collective-permute-start.28) | collective-permute-done | bytes 106528 | tf_op jit(solution)/shard_map/ppermute | solution.py:56
  90.4 5.2 %feed.1 = (bf16[208,256]{1,0:T(8,128)(2,1)S(1)}, bf16[208,256]{1,0:T(8,128)(2,1)S(1)}, bf16[208,256]{1,0:T(8,128)(2,1)S(1)}, bf16[208,256]{1,0:T(8,128)(2,1)S(1)...) custom-call(s32[4]{0:T(128)S(1)} %pad_add_fusion.1.me_ref.ids, ...), custom_call_target="tpu_custom_call" | custom-call | tf_op jit(solution)/shard_map/feed/pallas_call | solution.py:503
  95.6 1.8 %collective-permute-start.31 = (bf16[208,256]{1,0:T(8,128)(2,1)S(1)}, bf16[208,256]{1,0:T(8,128)(2,1)S(1)}, u32[]{:S(2)}, u32[]{:S(2)}) collective-permute-start(bf16[208,256]{1,0:T(8,128)(2,1)S(1)} %get-tuple-element.110), channel_id=1, source_target_pairs={{0,1},{1,0},{2,3},{3,2},{4,5},{5,4},{6,7},{7,6},{8,9},{9,8},{10,11... | collective-permute-start | bytes 319496 | tf_op jit(solution)/shard_map/ppermute | solution.py:45
  98.2 2.5 %collective-permute-start.33 = (bf16[208,256]{1,0:T(8,128)(2,1)S(1)}, bf16[208,256]{1,0:T(8,128)(2,1)S(1)}, u32[]{:S(2)}, u32[]{:S(2)}) collective-permute-start(bf16[208,256]{1,0:T(8,128)(2,1)S(1)} %get-tuple-element.112), channel_id=1, source_target_pairs={{0,3},{1,2},{2,1},{3,0},{4,7},{5,6},{6,5},{7,4},{8,11},{9,10},{10,... | collective-permute-start | bytes 319496 | tf_op jit(solution)/shard_map/ppermute | solution.py:45
  102.1 3.3 %collective-permute-start.35 = (bf16[208,256]{1,0:T(8,128)(2,1)S(1)}, bf16[208,256]{1,0:T(8,128)(2,1)S(1)}, u32[]{:S(2)}, u32[]{:S(2)}) collective-permute-start(bf16[208,256]{1,0:T(8,128)(2,1)S(1)} %get-tuple-element.114), channel_id=1, source_target_pairs={{0,5},{1,4},{2,7},{3,6},{4,1},{5,0},{6,3},{7,2},{8,13},{9,12},{10,... | collective-permute-start | bytes 319496 | tf_op jit(solution)/shard_map/ppermute | solution.py:45
  105.4 2.1 %collective-permute-start.36 = (bf16[208,256]{1,0:T(8,128)(2,1)S(1)}, bf16[208,256]{1,0:T(8,128)(2,1)S(1)}, u32[]{:S(2)}, u32[]{:S(2)}) collective-permute-start(bf16[208,256]{1,0:T(8,128)(2,1)S(1)} %get-tuple-element.115), channel_id=1, source_target_pairs={{0,6},{1,7},{2,4},{3,5},{4,2},{5,3},{6,0},{7,1},{8,14},{9,15},{10,... | collective-permute-start | bytes 319496 | tf_op jit(solution)/shard_map/ppermute | solution.py:45
  107.5 2.4 %collective-permute-start.37 = (bf16[208,256]{1,0:T(8,128)(2,1)S(1)}, bf16[208,256]{1,0:T(8,128)(2,1)S(1)}, u32[]{:S(2)}, u32[]{:S(2)}) collective-permute-start(bf16[208,256]{1,0:T(8,128)(2,1)S(1)} %get-tuple-element.116), channel_id=1, source_target_pairs={{0,7},{1,6},{2,5},{3,4},{4,3},{5,2},{6,1},{7,0},{8,15},{9,14},{10,... | collective-permute-start | bytes 319496 | tf_op jit(solution)/shard_map/ppermute | solution.py:45
  109.9 1.6 %collective-permute-done.35 = bf16[208,256]{1,0:T(8,128)(2,1)S(1)} collective-permute-done((bf16[208,256]{1,0:T(8,128)(2,1)S(1)}, bf16[208,256]{1,0:T(8,128)(2,1)S(1)}, u32[]{:S(2)}, u32[]{:S(2)}) %collective-permute-start.35) | collective-permute-done | bytes 106528 | tf_op jit(solution)/shard_map/ppermute | solution.py:45
  113.0 2.8 %collective-permute-done.37 = bf16[208,256]{1,0:T(8,128)(2,1)S(1)} collective-permute-done((bf16[208,256]{1,0:T(8,128)(2,1)S(1)}, bf16[208,256]{1,0:T(8,128)(2,1)S(1)}, u32[]{:S(2)}, u32[]{:S(2)}) %collective-permute-start.37) | collective-permute-done | bytes 106528 | tf_op jit(solution)/shard_map/ppermute | solution.py:45
  (111 shorter events, 25.1 us)
Async XLA Ops:
  2.4 33.3 %collective-permute-start.10 = (bf16[4,1024,128]{2,1,0:T(8,128)(2,1)S(1)}, bf16[4,1024,128]{2,1,0:T(8,128)(2,1)}, u32[]{:S(2)}, u32[]{:S(2)}) collective-permute-start(bf16[4,1024,128]{2,1,0:T(8,128)(2,1)S(1)} %constant_dynamic-update-slice_fusion.refs_8_), channel_id=1, source_target_pairs={{0,16},{16,0},{1,17},{17,1},{2,18},{18,2},{3,19},{19,3},{4,20},{20... | collective-permute-start | bytes 3145736 | tf_op jit(solution)/shard_map/ppermute | solution.py:45
  4.2 24.7 %collective-permute-start.1 = (bf16[4,1024,128]{2,1,0:T(8,128)(2,1)S(1)}, bf16[4,1024,128]{2,1,0:T(8,128)(2,1)}, u32[]{:S(2)}, u32[]{:S(2)}) collective-permute-start(bf16[4,1024,128]{2,1,0:T(8,128)(2,1)S(1)} %constant_dynamic-update-slice_fusion.refs_8_), channel_id=1, source_target_pairs={{0,8},{8,0},{1,9},{9,1},{2,10},{10,2},{3,11},{11,3},{4,12},{12,4},... | collective-permute-start | bytes 3145736 | tf_op jit(solution)/shard_map/ppermute | solution.py:45
  4.2 7.1 %collective-permute-start = (bf16[208,256]{1,0:T(8,128)(2,1)}, bf16[208,256]{1,0:T(8,128)(2,1)S(1)}, u32[]{:S(2)}, u32[]{:S(2)}) collective-permute-start(bf16[208,256]{1,0:T(8,128)(2,1)} %bitcast.14), channel_id=1, source_target_pairs={{0,1},{1,0},{2,3},{3,2},{4,5},{5,4},{6,7},{7,6},{8,9},{9,8},{10,11... | collective-permute-start | bytes 319496 | tf_op jit(solution)/shard_map/ppermute | solution.py:45
  8.0 15.9 %collective-permute-start.2 = (bf16[128,2048]{1,0:T(8,128)(2,1)}, bf16[128,2048]{1,0:T(8,128)(2,1)}, u32[]{:S(2)}, u32[]{:S(2)}) collective-permute-start(bf16[128,2048]{1,0:T(8,128)(2,1)} %constant_dynamic-slice_fusion.5), channel_id=1, source_target_pairs={{0,1},{1,0},{2,3},{3,2},{4,5},{5,4},{6,7},{7,6},{8,9},{9,8},{10,11... | collective-permute-start | bytes 1572872 | tf_op jit(solution)/shard_map/ppermute | solution.py:45
  11.3 7.1 %collective-permute-start.3 = (bf16[2,208,256]{2,1,0:T(8,128)(2,1)S(1)}, bf16[2,208,256]{2,1,0:T(8,128)(2,1)S(1)}, u32[]{:S(2)}, u32[]{:S(2)}) collective-permute-start(bf16[2,208,256]{2,1,0:T(8,128)(2,1)S(1)} %pad_maximum_fusion.refs_0_.refs_8_), channel_id=1, source_target_pairs={{0,2},{2,0},{4,6},{6,4},{1,3},{3,1},{5,7},{7,5},{8,10},{10,8},{12,... | collective-permute-start | bytes 638984 | tf_op jit(solution)/shard_map/ppermute | solution.py:45
  13.3 15.5 %collective-permute-start.6 = (bf16[2,208,256]{2,1,0:T(8,128)(2,1)S(1)}, bf16[2,208,256]{2,1,0:T(8,128)(2,1)S(1)}, u32[]{:S(2)}, u32[]{:S(2)}) collective-permute-start(bf16[2,208,256]{2,1,0:T(8,128)(2,1)S(1)} %pad_maximum_fusion.refs_0_.refs_8_), channel_id=1, source_target_pairs={{0,6},{2,4},{4,2},{6,0},{1,7},{3,5},{5,3},{7,1},{8,14},{10,12},{12... | collective-permute-start | bytes 638984 | tf_op jit(solution)/shard_map/ppermute | solution.py:45
  18.4 10.4 %collective-permute-start.5 = (bf16[2,208,256]{2,1,0:T(8,128)(2,1)S(1)}, bf16[2,208,256]{2,1,0:T(8,128)(2,1)S(1)}, u32[]{:S(2)}, u32[]{:S(2)}) collective-permute-start(bf16[2,208,256]{2,1,0:T(8,128)(2,1)S(1)} %pad_maximum_fusion.refs_0_.refs_8_), channel_id=1, source_target_pairs={{0,4},{2,6},{4,0},{6,2},{1,5},{3,7},{5,1},{7,3},{8,12},{10,14},{12... | collective-permute-start | bytes 638984 | tf_op jit(solution)/shard_map/ppermute | solution.py:45
  26.1 16.0 %collective-permute-start.8 = (bf16[256,2048]{1,0:T(8,128)(2,1)S(1)}, bf16[256,2048]{1,0:T(8,128)(2,1)S(1)}, u32[]{:S(2)}, u32[]{:S(2)}) collective-permute-start(bf16[256,2048]{1,0:T(8,128)(2,1)S(1)} %constant_dynamic-update-slice_fusion.2.refs_12_), channel_id=1, source_target_pairs={{0,2},{1,3},{2,0},{3,1},{4,6},{5,7},{6,4},{7,5},{8,14},{9,15},{10,... | collective-permute-start | bytes 3145736 | tf_op jit(solution)/shard_map/ppermute | solution.py:56
  31.0 11.2 %collective-permute-start.12 = (bf16[208,256]{1,0:T(8,128)(2,1)S(1)}, bf16[208,256]{1,0:T(8,128)(2,1)S(1)}, u32[]{:S(2)}, u32[]{:S(2)}) collective-permute-start(bf16[208,256]{1,0:T(8,128)(2,1)S(1)} %get-tuple-element.75.refs_0_), channel_id=1, source_target_pairs={{0,112},{16,96},{32,80},{48,64},{64,48},{80,32},{96,16},{112,0},{1... | collective-permute-start | bytes 319496 | tf_op jit(solution)/shard_map/ppermute | solution.py:45
  33.3 9.3 %collective-permute-start.11 = (bf16[208,256]{1,0:T(8,128)(2,1)S(1)}, bf16[208,256]{1,0:T(8,128)(2,1)S(1)}, u32[]{:S(2)}, u32[]{:S(2)}) collective-permute-start(bf16[208,256]{1,0:T(8,128)(2,1)S(1)} %get-tuple-element.75.refs_0_), channel_id=1, source_target_pairs={{0,64},{16,80},{32,96},{48,112},{64,0},{80,16},{96,32},{112,48},{1... | collective-permute-start | bytes 319496 | tf_op jit(solution)/shard_map/ppermute | solution.py:45
  34.7 6.8 %collective-permute-start.7 = (bf16[208,256]{1,0:T(8,128)(2,1)S(1)}, bf16[208,256]{1,0:T(8,128)(2,1)S(1)}, u32[]{:S(2)}, u32[]{:S(2)}) collective-permute-start(bf16[208,256]{1,0:T(8,128)(2,1)S(1)} %get-tuple-element.75.refs_0_), channel_id=1, source_target_pairs={{0,48},{16,32},{32,16},{48,0},{64,112},{80,96},{96,80},{112,64},{1... | collective-permute-start | bytes 319496 | tf_op jit(solution)/shard_map/ppermute | solution.py:45
  41.5 5.9 %collective-permute-start.16 = (bf16[4,1024,128]{2,1,0:T(8,128)(2,1)}, bf16[4,1024,128]{2,1,0:T(8,128)(2,1)S(1)}, u32[]{:S(2)}, u32[]{:S(2)}) collective-permute-start(bf16[4,1024,128]{2,1,0:T(8,128)(2,1)} %collective-permute-done.10.refs_10_), channel_id=1, source_target_pairs={{0,8},{8,0},{1,9},{9,1},{2,10},{10,2},{3,11},{11,3},{4,12},{12,4},... | collective-permute-start | bytes 3145736 | tf_op jit(solution)/shard_map/ppermute | solution.py:45
  42.1 12.2 %collective-permute-start.17 = (bf16[256,2048]{1,0:T(8,128)(2,1)S(1)}, bf16[256,2048]{1,0:T(8,128)(2,1)S(1)}, u32[]{:S(2)}, u32[]{:S(2)}) collective-permute-start(bf16[256,2048]{1,0:T(8,128)(2,1)S(1)} %constant_dynamic-update-slice_fusion.2.refs_12_), channel_id=1, source_target_pairs={{0,8},{8,0},{1,9},{9,1},{2,10},{10,2},{3,11},{11,3},{4,12},{12,4},... | collective-permute-start | bytes 3145736 | tf_op jit(solution)/shard_map/ppermute | solution.py:45
  42.6 11.8 %collective-permute-start.18 = (bf16[256,2048]{1,0:T(8,128)(2,1)S(1)}, bf16[256,2048]{1,0:T(8,128)(2,1)S(1)}, u32[]{:S(2)}, u32[]{:S(2)}) collective-permute-start(bf16[256,2048]{1,0:T(8,128)(2,1)S(1)} %collective-permute-done.8.refs_13_), channel_id=1, source_target_pairs={{0,8},{8,0},{1,9},{9,1},{2,10},{10,2},{3,11},{11,3},{4,12},{12,4},... | collective-permute-start | bytes 3145736 | tf_op jit(solution)/shard_map/ppermute | solution.py:45
  42.9 25.0 %collective-permute-start.4 = (bf16[256,2048]{1,0:T(8,128)(2,1)S(1)}, bf16[256,2048]{1,0:T(8,128)(2,1)S(1)}, u32[]{:S(2)}, u32[]{:S(2)}) collective-permute-start(bf16[256,2048]{1,0:T(8,128)(2,1)S(1)} %constant_dynamic-update-slice_fusion.2.refs_12_), channel_id=1, source_target_pairs={{0,6},{1,7},{2,4},{3,5},{4,2},{5,3},{6,0},{7,1},{8,10},{9,11},{10,... | collective-permute-start | bytes 3145736 | tf_op jit(solution)/shard_map/ppermute | solution.py:56
  45.8 24.4 %collective-permute-start.9 = (bf16[256,2048]{1,0:T(8,128)(2,1)S(1)}, bf16[256,2048]{1,0:T(8,128)(2,1)S(1)}, u32[]{:S(2)}, u32[]{:S(2)}) collective-permute-start(bf16[256,2048]{1,0:T(8,128)(2,1)S(1)} %collective-permute-done.8.refs_13_), channel_id=1, source_target_pairs={{0,6},{1,7},{2,4},{3,5},{4,2},{5,3},{6,0},{7,1},{8,10},{9,11},{10,... | collective-permute-start | bytes 3145736 | tf_op jit(solution)/shard_map/ppermute | solution.py:56
  54.4 9.1 %collective-permute-start.19 = (bf16[2,224,128]{2,1,0:T(8,128)(2,1)S(1)}, bf16[2,224,128]{2,1,0:T(8,128)(2,1)S(1)}, u32[]{:S(2)}, u32[]{:S(2)}) collective-permute-start(bf16[2,224,128]{2,1,0:T(8,128)(2,1)S(1)} %get-tuple-element.97), channel_id=1, source_target_pairs={{0,48},{16,32},{32,16},{48,0},{64,112},{80,96},{96,80},{112,64},{1... | collective-permute-start | bytes 344072 | tf_op jit(solution)/shard_map/ppermute | solution.py:45
  60.2 6.9 %collective-permute-start.21 = (bf16[2,224,128]{2,1,0:T(8,128)(2,1)S(1)}, bf16[2,224,128]{2,1,0:T(8,128)(2,1)S(1)}, u32[]{:S(2)}, u32[]{:S(2)}) collective-permute-start(bf16[2,224,128]{2,1,0:T(8,128)(2,1)S(1)} %get-tuple-element.99), channel_id=1, source_target_pairs={{0,112},{16,96},{32,80},{48,64},{64,48},{80,32},{96,16},{112,0},{1... | collective-permute-start | bytes 344072 | tf_op jit(solution)/shard_map/ppermute | solution.py:45
  70.7 9.9 %collective-permute-start.24 = (bf16[208,256]{1,0:T(8,128)(2,1)S(1)}, bf16[208,256]{1,0:T(8,128)(2,1)S(1)}, u32[]{:S(2)}, u32[]{:S(2)}) collective-permute-start(bf16[208,256]{1,0:T(8,128)(2,1)S(1)} %merge.1.refs_0_), channel_id=1, source_target_pairs={{0,3},{1,2},{2,1},{3,0},{4,7},{5,6},{6,5},{7,4},{8,15},{9,14},{10,... | collective-permute-start | bytes 319496 | tf_op jit(solution)/shard_map/ppermute | solution.py:56
  71.4 13.1 %collective-permute-start.23 = (bf16[208,256]{1,0:T(8,128)(2,1)S(1)}, bf16[208,256]{1,0:T(8,128)(2,1)S(1)}, u32[]{:S(2)}, u32[]{:S(2)}) collective-permute-start(bf16[208,256]{1,0:T(8,128)(2,1)S(1)} %merge.1.refs_0_), channel_id=1, source_target_pairs={{0,2},{1,3},{2,0},{3,1},{4,6},{5,7},{6,4},{7,5},{8,14},{9,15},{10,... | collective-permute-start | bytes 319496 | tf_op jit(solution)/shard_map/ppermute | solution.py:56
  74.1 10.8 %collective-permute-start.22 = (bf16[208,256]{1,0:T(8,128)(2,1)S(1)}, bf16[208,256]{1,0:T(8,128)(2,1)S(1)}, u32[]{:S(2)}, u32[]{:S(2)}) collective-permute-start(bf16[208,256]{1,0:T(8,128)(2,1)S(1)} %merge.1.refs_0_), channel_id=1, source_target_pairs={{0,1},{1,0},{2,3},{3,2},{4,5},{5,4},{6,7},{7,6},{8,9},{9,8},{10,11... | collective-permute-start | bytes 319496 | tf_op jit(solution)/shard_map/ppermute | solution.py:56
  75.7 9.3 %collective-permute-start.30 = (bf16[208,256]{1,0:T(8,128)(2,1)S(1)}, bf16[208,256]{1,0:T(8,128)(2,1)S(1)}, u32[]{:S(2)}, u32[]{:S(2)}) collective-permute-start(bf16[208,256]{1,0:T(8,128)(2,1)S(1)} %merge.1.refs_0_), channel_id=1, source_target_pairs={{0,5},{1,4},{2,7},{3,6},{4,1},{5,0},{6,3},{7,2},{8,13},{9,12},{10,... | collective-permute-start | bytes 319496 | tf_op jit(solution)/shard_map/ppermute | solution.py:56
  79.1 6.9 %collective-permute-start.29 = (bf16[208,256]{1,0:T(8,128)(2,1)S(1)}, bf16[208,256]{1,0:T(8,128)(2,1)S(1)}, u32[]{:S(2)}, u32[]{:S(2)}) collective-permute-start(bf16[208,256]{1,0:T(8,128)(2,1)S(1)} %merge.1.refs_0_), channel_id=1, source_target_pairs={{0,4},{1,5},{2,6},{3,7},{4,0},{5,1},{6,2},{7,3},{8,12},{9,13},{10,... | collective-permute-start | bytes 319496 | tf_op jit(solution)/shard_map/ppermute | solution.py:56
  80.6 8.3 %collective-permute-start.28 = (bf16[208,256]{1,0:T(8,128)(2,1)S(1)}, bf16[208,256]{1,0:T(8,128)(2,1)S(1)}, u32[]{:S(2)}, u32[]{:S(2)}) collective-permute-start(bf16[208,256]{1,0:T(8,128)(2,1)S(1)} %merge.1.refs_0_), channel_id=1, source_target_pairs={{0,7},{1,6},{2,5},{3,4},{4,3},{5,2},{6,1},{7,0},{8,11},{9,10},{10,... | collective-permute-start | bytes 319496 | tf_op jit(solution)/shard_map/ppermute | solution.py:56
  84.5 5.9 %collective-permute-start.27 = (bf16[208,256]{1,0:T(8,128)(2,1)S(1)}, bf16[208,256]{1,0:T(8,128)(2,1)S(1)}, u32[]{:S(2)}, u32[]{:S(2)}) collective-permute-start(bf16[208,256]{1,0:T(8,128)(2,1)S(1)} %merge.1.refs_0_), channel_id=1, source_target_pairs={{0,6},{1,7},{2,4},{3,5},{4,2},{5,3},{6,0},{7,1},{8,10},{9,11},{10,... | collective-permute-start | bytes 319496 | tf_op jit(solution)/shard_map/ppermute | solution.py:56
  95.6 9.8 %collective-permute-start.31 = (bf16[208,256]{1,0:T(8,128)(2,1)S(1)}, bf16[208,256]{1,0:T(8,128)(2,1)S(1)}, u32[]{:S(2)}, u32[]{:S(2)}) collective-permute-start(bf16[208,256]{1,0:T(8,128)(2,1)S(1)} %get-tuple-element.110), channel_id=1, source_target_pairs={{0,1},{1,0},{2,3},{3,2},{4,5},{5,4},{6,7},{7,6},{8,9},{9,8},{10,11... | collective-permute-start | bytes 319496 | tf_op jit(solution)/shard_map/ppermute | solution.py:45
  97.4 10.0 %collective-permute-start.32 = (bf16[208,256]{1,0:T(8,128)(2,1)S(1)}, bf16[208,256]{1,0:T(8,128)(2,1)S(1)}, u32[]{:S(2)}, u32[]{:S(2)}) collective-permute-start(bf16[208,256]{1,0:T(8,128)(2,1)S(1)} %get-tuple-element.111), channel_id=1, source_target_pairs={{0,2},{1,3},{2,0},{3,1},{4,6},{5,7},{6,4},{7,5},{8,10},{9,11},{10,... | collective-permute-start | bytes 319496 | tf_op jit(solution)/shard_map/ppermute | solution.py:45
  98.2 11.7 %collective-permute-start.33 = (bf16[208,256]{1,0:T(8,128)(2,1)S(1)}, bf16[208,256]{1,0:T(8,128)(2,1)S(1)}, u32[]{:S(2)}, u32[]{:S(2)}) collective-permute-start(bf16[208,256]{1,0:T(8,128)(2,1)S(1)} %get-tuple-element.112), channel_id=1, source_target_pairs={{0,3},{1,2},{2,1},{3,0},{4,7},{5,6},{6,5},{7,4},{8,11},{9,10},{10,... | collective-permute-start | bytes 319496 | tf_op jit(solution)/shard_map/ppermute | solution.py:45
  100.7 9.2 %collective-permute-start.34 = (bf16[208,256]{1,0:T(8,128)(2,1)S(1)}, bf16[208,256]{1,0:T(8,128)(2,1)S(1)}, u32[]{:S(2)}, u32[]{:S(2)}) collective-permute-start(bf16[208,256]{1,0:T(8,128)(2,1)S(1)} %get-tuple-element.113), channel_id=1, source_target_pairs={{0,4},{1,5},{2,6},{3,7},{4,0},{5,1},{6,2},{7,3},{8,12},{9,13},{10,... | collective-permute-start | bytes 319496 | tf_op jit(solution)/shard_map/ppermute | solution.py:45
  102.1 9.4 %collective-permute-start.35 = (bf16[208,256]{1,0:T(8,128)(2,1)S(1)}, bf16[208,256]{1,0:T(8,128)(2,1)S(1)}, u32[]{:S(2)}, u32[]{:S(2)}) collective-permute-start(bf16[208,256]{1,0:T(8,128)(2,1)S(1)} %get-tuple-element.114), channel_id=1, source_target_pairs={{0,5},{1,4},{2,7},{3,6},{4,1},{5,0},{6,3},{7,2},{8,13},{9,12},{10,... | collective-permute-start | bytes 319496 | tf_op jit(solution)/shard_map/ppermute | solution.py:45
  105.4 7.6 %collective-permute-start.36 = (bf16[208,256]{1,0:T(8,128)(2,1)S(1)}, bf16[208,256]{1,0:T(8,128)(2,1)S(1)}, u32[]{:S(2)}, u32[]{:S(2)}) collective-permute-start(bf16[208,256]{1,0:T(8,128)(2,1)S(1)} %get-tuple-element.115), channel_id=1, source_target_pairs={{0,6},{1,7},{2,4},{3,5},{4,2},{5,3},{6,0},{7,1},{8,14},{9,15},{10,... | collective-permute-start | bytes 319496 | tf_op jit(solution)/shard_map/ppermute | solution.py:45
  107.5 8.3 %collective-permute-start.37 = (bf16[208,256]{1,0:T(8,128)(2,1)S(1)}, bf16[208,256]{1,0:T(8,128)(2,1)S(1)}, u32[]{:S(2)}, u32[]{:S(2)}) collective-permute-start(bf16[208,256]{1,0:T(8,128)(2,1)S(1)} %get-tuple-element.116), channel_id=1, source_target_pairs={{0,7},{1,6},{2,5},{3,4},{4,3},{5,2},{6,1},{7,0},{8,15},{9,14},{10,... | collective-permute-start | bytes 319496 | tf_op jit(solution)/shard_map/ppermute | solution.py:45
  (22 other events, 465.8 us)

commit v5 on v4

--- a/solution.py
+++ b/solution.py
@@ -54,6 +54,30 @@
                 there = (core * 4 + (z ^ masks[core])) * 2 + (hi ^ flip)
                 perm.append(((core * 4 + z) * 2 + hi, there))
     return lax.ppermute(x, ("core", "z", "xhi"), perm)
+
+
+def join_kernel(a_ref, b_ref, out_ref, sems):
+    rows = a_ref.shape[0]
+    copies = [
+        pltpu.make_async_copy(ref, out_ref.at[pl.ds(i * rows, rows)], sems.at[i])
+        for i, ref in enumerate((a_ref, b_ref))
+    ]
+    for c in copies:
+        c.start()
+    for c in copies:
+        c.wait()
+
+
+def join(a, b):
+    return pl.pallas_call(
+        join_kernel,
+        in_specs=[ANY, ANY],
+        out_specs=ANY,
+        out_shape=jax.ShapeDtypeStruct((2 * a.shape[0],) + a.shape[1:], a.dtype),
+        scratch_shapes=[pltpu.SemaphoreType.DMA((2,))],
+        compiler_params=grant(2),
+        name="join",
+    )(a, b)
 
 
 def scale_of(pieces, width):
@@ -131,30 +155,25 @@
     for c in copies:
         c.start()
 
-    def scan_query(qi, n):
+    key_rows = []
+    for ki in range(slots):
+        k_nat = jnp.bitwise_xor(mk, ki // 2) * 2 + ki % 2
+        k_slot = xy * 8 + k_nat
+        key_rows.append((tab[k_slot], tab[place_at + k_slot], ki * 8 + k_nat * 64))
+    found = jnp.int32(0)
+    for qi in range(slots):
         p = qi // 2
         q_slot = jnp.bitwise_xor(xy, p) * 8 + jnp.bitwise_xor(mk, (p % 2) * 2) * 2 + qi % 2
         q_req, q_place = tab[q_slot], tab[place_at + q_slot]
-
-        def scan_key(ki, n):
-            k_nat = jnp.bitwise_xor(mk, ki // 2) * 2 + ki % 2
-            k_slot = xy * 8 + k_nat
-            k_req, k_place = tab[k_slot], tab[place_at + k_slot]
+        for k_req, k_place, word in key_rows:
+            todo[found] = word + qi + jnp.where(k_place < q_place, 512, 0)
             seen = jnp.logical_and(k_req == q_req, k_place <= q_place)
-
-            todo[0, n] = qi
-            todo[1, n] = ki
-            todo[2, n] = k_nat
-            todo[3, n] = jnp.where(k_place < q_place, 65536, 0)
-            return n + seen.astype(jnp.int32)
-
-        return lax.fori_loop(0, slots, scan_key, n)
-
-    found = lax.fori_loop(0, slots, scan_query, 0)
-    todo[0, found] = 0
-    todo[1, found] = 0
-    todo[2, found] = 0
-    todo[3, found] = -65536
+            found = found + seen.astype(jnp.int32)
+    todo[found] = 1024
+
+    def entry(at):
+        word = todo[at]
+        return word % 8, word // 8 % 8, word // 64 % 8, word // 512
 
     pad = values.shape[1] - span - count
     for p in range(4):
@@ -188,7 +207,8 @@
     factor = hd**-0.5 * math.log2(math.e)
 
     def score(at):
-        qi, ki, row = todo[0, at], todo[1, at], pl.ds(todo[2, at], 1)
+        qi, ki, k_nat, _ = entry(at)
+        row = pl.ds(k_nat, 1)
         query = queries[qi]
         turned = rotate(query.astype(F32), cos[row, :], sin[row, :]).astype(BF16)
         return jnp.concatenate(
@@ -202,9 +222,10 @@
         )
 
     def soften(at, scores):
-        qi = todo[0, at]
-        bound = bounds[qi] + todo[3, at].astype(F32)
-        scores = jnp.where(places[pl.ds(todo[2, at], 1), :] <= bound, scores, NEG)
+        qi, _, k_nat, level = entry(at)
+        offset = jnp.where(level == 1, 65536.0, jnp.where(level == 2, -65536.0, 0.0))
+        bound = bounds[qi] + offset
+        scores = jnp.where(places[pl.ds(k_nat, 1), :] <= bound, scores, NEG)
         old = run_m[qi]
         new = jnp.maximum(old, jnp.max(scores, axis=-1, keepdims=True))
         shrink = jnp.exp2((old - new) * factor)
@@ -214,7 +235,7 @@
         return shrink, weights.astype(BF16)
 
     def gather(at, shrink, weights):
-        qi, ki = todo[0, at], todo[1, at]
+        qi, ki, _, _ = entry(at)
         run_acc[qi] = run_acc[qi] * shrink + jnp.dot(
             weights, values[ki], preferred_element_type=F32
         )
@@ -274,7 +295,7 @@
             pltpu.VMEM((8, 2 * count, 1), F32),
             pltpu.VMEM((8, 2 * count, 1), F32),
             pltpu.VMEM((8, 2 * count, hd), F32),
-            pltpu.SMEM((4, 72), jnp.int32),
+            pltpu.SMEM((72,), jnp.int32),
             pltpu.SemaphoreType.DMA((2, 4)),
         ],
         compiler_params=grant(18),
@@ -399,16 +420,26 @@
     pair = jnp.stack([hidden, swap(hidden, "xhi", 1, 2)])
 
     output_half = rows_at(output_weight, core * half, half)
-    pair, selected_later, place, start, ids, at_group, *at_slots = lax.optimization_barrier(
-        (pair, selected_index, place, start, ids, xy * 8)
+    cached_keys, place = lax.optimization_barrier((cached_keys, place))
+    cached = join(cached_keys, cached_values)
+    cached_y = swap(cached, "ylo", 1, 2)
+    cached_core = swap(cached, "core", 1, 2)
+
+    (
+        pair,
+        cached_core,
+        selected_later,
+        place,
+        start,
+        ids,
+        at_group,
+        *at_slots,
+    ) = lax.optimization_barrier(
+        (pair, cached_core, selected_index, place, start, ids, xy * 8)
         + tuple(jnp.bitwise_xor(seq, 2 * k) * slot_local for k in (0,) + FAR_MASKS)
     )
     output_x = swap(output_half, "xhi", 1, 2)
     pairs = [pair] + [swap(pair, "z", k, 4) for k in (1, 2, 3)]
-
-    cached = jnp.concatenate([cached_keys, cached_values], axis=0)
-    cached_y = swap(cached, "ylo", 1, 2)
-    cached_core = swap(cached, "core", 1, 2)
 
     base_here = rows_at((place * span)[:, None], at_slots[0], slot_local)
     index_here = rows_at(selected_later, at_slots[0], slot_local)
@@ -417,10 +448,10 @@
     output_half, output_x, pairs[1] = lax.optimization_barrier(
         (output_half, output_x, pairs[1])
     )
-    wo_0 = jnp.concatenate([output_half, output_x], axis=0)
+    wo_0 = join(output_half, output_x)
     wo_1 = cross(wo_0, 1, 0)
-    pairs[0], qg, kg, qc, qs, ids, table, cached_core = lax.optimization_barrier(
-        (pairs[0], qg, kg, qc, qs, ids, table, cached_core)
+    pairs[0], qg, kg, qc, qs, ids, table = lax.optimization_barrier(
+        (pairs[0], qg, kg, qc, qs, ids, table)
     )
     queries, fresh = pl.pallas_call(
         functools.partial(project_kernel, n),
@@ -491,15 +522,14 @@
         compiler_params=grant(8),
         name="merge",
     )(*parts)
-    order = [(kind, flip) for kind in range(4) for flip in range(2)]
+    order = [(3, 1), (1, 1), (2, 1), (3, 0), (0, 1), (1, 0), (2, 0)]
     wo_2, wo_3, attended = lax.optimization_barrier((wo_2, wo_3, attended))
     wo_2c, wo_3c = swap(wo_2, "core", 1, 2), swap(wo_3, "core", 1, 2)
     wo_own = [wo_0, wo_1, wo_2, wo_3]
     wo_2c, wo_3c, later = lax.optimization_barrier((wo_2c, wo_3c, attended))
-    pieces = [attended] + [
-        cross(attended if i < 3 else later, kind, flip)
-        for i, (kind, flip) in enumerate(order[1:])
-    ]
+    pieces = [attended] + [None] * (n - 1)
+    for i, (kind, flip) in enumerate(order):
+        pieces[2 * kind + flip] = cross(attended if i < 3 else later, kind, flip)
     *downs, stream = pl.pallas_call(
         functools.partial(feed_kernel, n),
         in_specs=[SMEM] + [VMEM] * (2 * n + n // 2 + 4),
@@ -523,7 +553,7 @@
         down_weight,
     )
     total = stream.astype(F32) + downs[0].astype(F32)
-    for k in range(1, n):
+    for k in (5, 3, 7, 4, 1, 2, 6):
         total = total + swap(downs[k], TP, k, n).astype(F32)
     return total.astype(BF16).reshape(slot_local, count, width)
 

time: 117 us -> 113 us (0.966)
  Pallas kernels: 15 us -> 21.6 us
  starting transfers between devices: 61.1 us -> 55.9 us
  local copies, waits for them, and re-layouts: 5.49 us -> 2.28 us
  waiting for transfers between devices: 31.5 us -> 28.4 us
    pallas_call x1, Pallas kernels: 6.92 us -> 12.3 us  [attend(): pl.pallas_call(functools.partial(attend_kernel, count), in_specs=[SMEM, S...]
    ppermute x28, starting transfers between devices: 41.5 us -> 36.4 us  [swap(): return lax.ppermute(x, axes, [(i, i ^ mask) for i in range(size)])]
    ppermute x10, waiting for transfers between devices: 7.81 us -> 5.43 us  [cross(): return lax.ppermute(x, ('core', 'z', 'xhi'), perm)]
    concatenate x2 -> x0, local copies, waits for them, and re-layouts: 2.19 us -> none  [the longest x1 1.11 us: on_device(): cached = jnp.concatenate([cached_keys, cached_values], axis=0)]
    pallas_call x0 -> x2, Pallas kernels: none -> 1.19 us  [join(): pl.pallas_call(join_kernel, in_specs=[ANY, ANY], out_specs=ANY, out_shape...]
    unnamed x34 -> x32, local copies, waits for them, and re-layouts: 2.37 us -> 2.14 us
  transfers between devices with their start and end apart: 38 -> 38, of which waited for: 16 -> 15; matrix products, arithmetic and copies ran while one was open for 5% -> 2% of each run, Pallas kernels for 8% -> 14%
where the time goes in v5:
time: 113 us; the launch traced here: 112 us
  starting transfers between devices  55.9 us (49%)
  waiting for transfers between devices  28.4 us (25%)
  Pallas kernels  21.6 us (19%)
  other arithmetic  3.87 us (3%)
  local copies, waits for them, and re-layouts  2.28 us (2%)
    ppermute x28, starting transfers between devices, swap(): return lax.ppermute(x, axes, [(i, i ^ mask) for i in range(size)])  36.4 us
    ppermute x28, waiting for transfers between devices, swap(): return lax.ppermute(x, axes, [(i, i ^ mask) for i in range(size)])  22.9 us
    ppermute x10, starting transfers between devices, cross(): return lax.ppermute(x, ('core', 'z', 'xhi'), perm)  19.5 us
    pallas_call x1, Pallas kernels, attend(): pl.pallas_call(functools.partial(attend_kernel, count), in_specs=[SMEM, S...  12.3 us
    ppermute x10, waiting for transfers between devices, cross(): return lax.ppermute(x, ('core', 'z', 'xhi'), perm)  5.43 us
    pallas_call x1, Pallas kernels, on_device(): pl.pallas_call(functools.partial(feed_kernel, n), in_specs=[SMEM] + [VMEM...  5.21 us
  transfers between devices with their start and end apart: 38, of which 15 were waited for; matrix products, arithmetic and copies ran while one was open for 2% of the time, Pallas kernels for 14%

profile of v5, /device:TPU:0, one launch (start us, length us, event | category | flops | bytes accessed | tf_op | source)
XLA Modules:
  0.0 112.4 jit_solution(10214439267384193320)
XLA Ops:
  3.3 1.7 %collective-permute-start.10 = (bf16[4,1024,128]{2,1,0:T(8,128)(2,1)S(1)}, bf16[4,1024,128]{2,1,0:T(8,128)(2,1)}, u32[]{:S(2)}, u32[]{:S(2)}) collective-permute-start(bf16[4,1024,128]{2,1,0:T(8,128)(2,1)S(1)} %join.2.refs_8_), channel_id=1, source_target_pairs={{0,16},{16,0},{1,17},{17,1},{2,18},{18,2},{3,19},{19,3},{4,20},{20... | collective-permute-start | bytes 3145736 | tf_op jit(solution)/shard_map/ppermute | solution.py:45
  5.0 3.0 %collective-permute-start = (bf16[208,256]{1,0:T(8,128)(2,1)}, bf16[208,256]{1,0:T(8,128)(2,1)S(1)}, u32[]{:S(2)}, u32[]{:S(2)}) collective-permute-start(bf16[208,256]{1,0:T(8,128)(2,1)} %bitcast.14), channel_id=1, source_target_pairs={{0,1},{1,0},{2,3},{3,2},{4,5},{5,4},{6,7},{7,6},{8,9},{9,8},{10,11... | collective-permute-start | bytes 319496 | tf_op jit(solution)/shard_map/ppermute | solution.py:45
  8.9 2.9 %collective-permute-done = bf16[208,256]{1,0:T(8,128)(2,1)S(1)} collective-permute-done((bf16[208,256]{1,0:T(8,128)(2,1)}, bf16[208,256]{1,0:T(8,128)(2,1)S(1)}, u32[]{:S(2)}, u32[]{:S(2)}) %collective-permute-start) | collective-permute-done | bytes 106528 | tf_op jit(solution)/shard_map/ppermute | solution.py:45
  11.8 2.0 %collective-permute-start.3 = (bf16[2,208,256]{2,1,0:T(8,128)(2,1)S(1)}, bf16[2,208,256]{2,1,0:T(8,128)(2,1)S(1)}, u32[]{:S(2)}, u32[]{:S(2)}) collective-permute-start(bf16[2,208,256]{2,1,0:T(8,128)(2,1)S(1)} %pad_maximum_fusion.refs_0_.refs_8_), channel_id=1, source_target_pairs={{0,2},{2,0},{4,6},{6,4},{1,3},{3,1},{5,7},{7,5},{8,10},{10,8},{12,... | collective-permute-start | bytes 638984 | tf_op jit(solution)/shard_map/ppermute | solution.py:45
  13.8 2.6 %collective-permute-start.6 = (bf16[2,208,256]{2,1,0:T(8,128)(2,1)S(1)}, bf16[2,208,256]{2,1,0:T(8,128)(2,1)S(1)}, u32[]{:S(2)}, u32[]{:S(2)}) collective-permute-start(bf16[2,208,256]{2,1,0:T(8,128)(2,1)S(1)} %pad_maximum_fusion.refs_0_.refs_8_), channel_id=1, source_target_pairs={{0,6},{2,4},{4,2},{6,0},{1,7},{3,5},{5,3},{7,1},{8,14},{10,12},{12... | collective-permute-start | bytes 638984 | tf_op jit(solution)/shard_map/ppermute | solution.py:45
  16.4 1.2 %collective-permute-start.5 = (bf16[2,208,256]{2,1,0:T(8,128)(2,1)S(1)}, bf16[2,208,256]{2,1,0:T(8,128)(2,1)S(1)}, u32[]{:S(2)}, u32[]{:S(2)}) collective-permute-start(bf16[2,208,256]{2,1,0:T(8,128)(2,1)S(1)} %pad_maximum_fusion.refs_0_.refs_8_), channel_id=1, source_target_pairs={{0,4},{2,6},{4,0},{6,2},{1,5},{3,7},{5,1},{7,3},{8,12},{10,14},{12... | collective-permute-start | bytes 638984 | tf_op jit(solution)/shard_map/ppermute | solution.py:45
  17.6 5.9 %collective-permute-done.2.b_ref = bf16[128,2048]{1,0:T(8,128)(2,1)} collective-permute-done((bf16[128,2048]{1,0:T(8,128)(2,1)S(1)}, bf16[128,2048]{1,0:T(8,128)(2,1)}, u32[]{:S(2)}, u32[]{:S(2)}) %collective-permute-start.2) | collective-permute-done | bytes 524320 | tf_op jit(solution)/shard_map/ppermute | solution.py:45
  23.5 1.1 join.3.refs_12_
  24.6 2.0 %collective-permute-start.8 = (bf16[256,2048]{1,0:T(8,128)(2,1)S(1)}, bf16[256,2048]{1,0:T(8,128)(2,1)S(1)}, u32[]{:S(2)}, u32[]{:S(2)}) collective-permute-start(bf16[256,2048]{1,0:T(8,128)(2,1)S(1)} %join.3.refs_12_), channel_id=1, source_target_pairs={{0,2},{1,3},{2,0},{3,1},{4,6},{5,7},{6,4},{7,5},{8,14},{9,15},{10,... | collective-permute-start | bytes 3145736 | tf_op jit(solution)/shard_map/ppermute | solution.py:56
  27.4 2.0 %project.1 = (bf16[208,256]{1,0:T(8,128)(2,1)S(1)}, bf16[208,256]{1,0:T(8,128)(2,1)S(1)}) custom-call(s32[4]{0:T(128)S(1)} %pad_add_fusion.1.me_ref.ids, bf16[2,208,256]{2,1,0:T(8,128)(2,1)S(1)} %pad_maximum_fusion.refs_0_.refs_8_, bf16[2,208,256]{2,1,0:T(8,128)(2,1)S(1)} %collective-permute-done.3.refs_1_.refs_9_, ...), custom_call_target="tpu_custom_call" | custom-call | tf_op jit(solution)/shard_map/project/pallas_call | solution.py:456
  29.5 2.8 %collective-permute-start.12 = (bf16[208,256]{1,0:T(8,128)(2,1)S(1)}, bf16[208,256]{1,0:T(8,128)(2,1)S(1)}, u32[]{:S(2)}, u32[]{:S(2)}) collective-permute-start(bf16[208,256]{1,0:T(8,128)(2,1)S(1)} %get-tuple-element.79.refs_0_), channel_id=1, source_target_pairs={{0,112},{16,96},{32,80},{48,64},{64,48},{80,32},{96,16},{112,0},{1... | collective-permute-start | bytes 319496 | tf_op jit(solution)/shard_map/ppermute | solution.py:45
  33.2 1.1 collective-permute-start.7
  34.4 5.3 %collective-permute-done.7.refs_1_ = bf16[208,256]{1,0:T(8,128)(2,1)S(1)} collective-permute-done((bf16[208,256]{1,0:T(8,128)(2,1)S(1)}, bf16[208,256]{1,0:T(8,128)(2,1)S(1)}, u32[]{:S(2)}, u32[]{:S(2)}) %collective-permute-start.7) | collective-permute-done | bytes 106528 | tf_op jit(solution)/shard_map/ppermute | solution.py:45
  41.1 3.2 %collective-permute-start.4 = (bf16[256,2048]{1,0:T(8,128)(2,1)S(1)}, bf16[256,2048]{1,0:T(8,128)(2,1)S(1)}, u32[]{:S(2)}, u32[]{:S(2)}) collective-permute-start(bf16[256,2048]{1,0:T(8,128)(2,1)S(1)} %join.3.refs_12_), channel_id=1, source_target_pairs={{0,6},{1,7},{2,4},{3,5},{4,2},{5,3},{6,0},{7,1},{8,10},{9,11},{10,... | collective-permute-start | bytes 3145736 | tf_op jit(solution)/shard_map/ppermute | solution.py:56
  46.0 12.3 %attend.1 = (bf16[2,224,128]{2,1,0:T(8,128)(2,1)S(1)}, bf16[2,224,128]{2,1,0:T(8,128)(2,1)S(1)}, bf16[2,224,128]{2,1,0:T(8,128)(2,1)S(1)}, bf16[2,224,128]{2,1,0:T(8,128)(2,1)S(1)}) custom-call(s32[4]{0:T(128)S(1)} %pad_add_fusion.1.me_ref.ids, s32[64]{0:T(128)S(1)} %pad_add_fusion.2.tab, f32[8,1024]{1,0:T(8,128)S(1)} %broadcast_select_fusion.kpos, ...), custom_call_target="tpu_custom_call" | custom-call | tf_op jit(solution)/shard_map/attend/pallas_call | solution.py:283
  59.3 3.8 %collective-permute-start.21 = (bf16[2,224,128]{2,1,0:T(8,128)(2,1)S(1)}, bf16[2,224,128]{2,1,0:T(8,128)(2,1)S(1)}, u32[]{:S(2)}, u32[]{:S(2)}) collective-permute-start(bf16[2,224,128]{2,1,0:T(8,128)(2,1)S(1)} %get-tuple-element.103), channel_id=1, source_target_pairs={{0,112},{16,96},{32,80},{48,64},{64,48},{80,32},{96,16},{112,0},{1... | collective-permute-start | bytes 344072 | tf_op jit(solution)/shard_map/ppermute | solution.py:45
  63.1 1.3 %collective-permute-done.19.refs_1_ = bf16[2,224,128]{2,1,0:T(8,128)(2,1)S(1)} collective-permute-done((bf16[2,224,128]{2,1,0:T(8,128)(2,1)S(1)}, bf16[2,224,128]{2,1,0:T(8,128)(2,1)S(1)}, u32[]{:S(2)}, u32[]{:S(2)}) %collective-permute-start.19) | collective-permute-done | bytes 114720 | tf_op jit(solution)/shard_map/ppermute | solution.py:45
  64.4 2.7 %collective-permute-done.21.refs_3_ = bf16[2,224,128]{2,1,0:T(8,128)(2,1)S(1)} collective-permute-done((bf16[2,224,128]{2,1,0:T(8,128)(2,1)S(1)}, bf16[2,224,128]{2,1,0:T(8,128)(2,1)S(1)}, u32[]{:S(2)}, u32[]{:S(2)}) %collective-permute-start.21) | collective-permute-done | bytes 114720 | tf_op jit(solution)/shard_map/ppermute | solution.py:45
  68.8 3.9 %collective-permute-start.30 = (bf16[208,256]{1,0:T(8,128)(2,1)S(1)}, bf16[208,256]{1,0:T(8,128)(2,1)S(1)}, u32[]{:S(2)}, u32[]{:S(2)}) collective-permute-start(bf16[208,256]{1,0:T(8,128)(2,1)S(1)} %merge.1.refs_0_), channel_id=1, source_target_pairs={{0,5},{1,4},{2,7},{3,6},{4,1},{5,0},{6,3},{7,2},{8,13},{9,12},{10,... | collective-permute-start | bytes 319496 | tf_op jit(solution)/shard_map/ppermute | solution.py:56
  72.8 1.6 %collective-permute-start.28 = (bf16[208,256]{1,0:T(8,128)(2,1)S(1)}, bf16[208,256]{1,0:T(8,128)(2,1)S(1)}, u32[]{:S(2)}, u32[]{:S(2)}) collective-permute-start(bf16[208,256]{1,0:T(8,128)(2,1)S(1)} %merge.1.refs_0_), channel_id=1, source_target_pairs={{0,7},{1,6},{2,5},{3,4},{4,3},{5,2},{6,1},{7,0},{8,11},{9,10},{10,... | collective-permute-start | bytes 319496 | tf_op jit(solution)/shard_map/ppermute | solution.py:56
  74.4 2.7 %collective-permute-start.26 = (bf16[208,256]{1,0:T(8,128)(2,1)S(1)}, bf16[208,256]{1,0:T(8,128)(2,1)S(1)}, u32[]{:S(2)}, u32[]{:S(2)}) collective-permute-start(bf16[208,256]{1,0:T(8,128)(2,1)S(1)} %merge.1.refs_0_), channel_id=1, source_target_pairs={{0,3},{1,2},{2,1},{3,0},{4,7},{5,6},{6,5},{7,4},{8,15},{9,14},{10,... | collective-permute-start | bytes 319496 | tf_op jit(solution)/shard_map/ppermute | solution.py:56
  77.1 2.8 %collective-permute-start.29 = (bf16[208,256]{1,0:T(8,128)(2,1)S(1)}, bf16[208,256]{1,0:T(8,128)(2,1)S(1)}, u32[]{:S(2)}, u32[]{:S(2)}) collective-permute-start(bf16[208,256]{1,0:T(8,128)(2,1)S(1)} %merge.1.refs_0_), channel_id=1, source_target_pairs={{0,4},{1,5},{2,6},{3,7},{4,0},{5,1},{6,2},{7,3},{8,12},{9,13},{10,... | collective-permute-start | bytes 319496 | tf_op jit(solution)/shard_map/ppermute | solution.py:56
  79.9 1.3 %collective-permute-start.27 = (bf16[208,256]{1,0:T(8,128)(2,1)S(1)}, bf16[208,256]{1,0:T(8,128)(2,1)S(1)}, u32[]{:S(2)}, u32[]{:S(2)}) collective-permute-start(bf16[208,256]{1,0:T(8,128)(2,1)S(1)} %merge.1.refs_0_), channel_id=1, source_target_pairs={{0,6},{1,7},{2,4},{3,5},{4,2},{5,3},{6,0},{7,1},{8,10},{9,11},{10,... | collective-permute-start | bytes 319496 | tf_op jit(solution)/shard_map/ppermute | solution.py:56
  81.5 1.5 %collective-permute-start.24 = (bf16[208,256]{1,0:T(8,128)(2,1)S(1)}, bf16[208,256]{1,0:T(8,128)(2,1)S(1)}, u32[]{:S(2)}, u32[]{:S(2)}) collective-permute-start(bf16[208,256]{1,0:T(8,128)(2,1)S(1)} %merge.1.refs_0_), channel_id=1, source_target_pairs={{0,1},{1,0},{2,3},{3,2},{4,5},{5,4},{6,7},{7,6},{8,9},{9,8},{10,11... | collective-permute-start | bytes 319496 | tf_op jit(solution)/shard_map/ppermute | solution.py:56
  82.9 2.7 %collective-permute-done.29.refs_6_ = bf16[208,256]{1,0:T(8,128)(2,1)S(1)} collective-permute-done((bf16[208,256]{1,0:T(8,128)(2,1)S(1)}, bf16[208,256]{1,0:T(8,128)(2,1)S(1)}, u32[]{:S(2)}, u32[]{:S(2)}) %collective-permute-start.29) | collective-permute-done | bytes 106528 | tf_op jit(solution)/shard_map/ppermute | solution.py:56
  85.6 1.4 %collective-permute-done.27.refs_4_ = bf16[208,256]{1,0:T(8,128)(2,1)S(1)} collective-permute-done((bf16[208,256]{1,0:T(8,128)(2,1)S(1)}, bf16[208,256]{1,0:T(8,128)(2,1)S(1)}, u32[]{:S(2)}, u32[]{:S(2)}) %collective-permute-start.27) | collective-permute-done | bytes 106528 | tf_op jit(solution)/shard_map/ppermute | solution.py:56
  87.7 5.2 %feed.1 = (bf16[208,256]{1,0:T(8,128)(2,1)S(1)}, bf16[208,256]{1,0:T(8,128)(2,1)S(1)}, bf16[208,256]{1,0:T(8,128)(2,1)S(1)}, bf16[208,256]{1,0:T(8,128)(2,1)S(1)...) custom-call(s32[4]{0:T(128)S(1)} %pad_add_fusion.1.me_ref.ids, ...), custom_call_target="tpu_custom_call" | custom-call | tf_op jit(solution)/shard_map/feed/pallas_call | solution.py:533
  92.9 5.2 %collective-permute-start.31 = (bf16[208,256]{1,0:T(8,128)(2,1)S(1)}, bf16[208,256]{1,0:T(8,128)(2,1)S(1)}, u32[]{:S(2)}, u32[]{:S(2)}) collective-permute-start(bf16[208,256]{1,0:T(8,128)(2,1)S(1)} %get-tuple-element.114), channel_id=1, source_target_pairs={{0,5},{1,4},{2,7},{3,6},{4,1},{5,0},{6,3},{7,2},{8,13},{9,12},{10,... | collective-permute-start | bytes 319496 | tf_op jit(solution)/shard_map/ppermute | solution.py:45
  98.3 2.0 %collective-permute-start.33 = (bf16[208,256]{1,0:T(8,128)(2,1)S(1)}, bf16[208,256]{1,0:T(8,128)(2,1)S(1)}, u32[]{:S(2)}, u32[]{:S(2)}) collective-permute-start(bf16[208,256]{1,0:T(8,128)(2,1)S(1)} %get-tuple-element.116), channel_id=1, source_target_pairs={{0,7},{1,6},{2,5},{3,4},{4,3},{5,2},{6,1},{7,0},{8,15},{9,14},{10,... | collective-permute-start | bytes 319496 | tf_op jit(solution)/shard_map/ppermute | solution.py:45
  100.4 4.3 %collective-permute-start.34 = (bf16[208,256]{1,0:T(8,128)(2,1)S(1)}, bf16[208,256]{1,0:T(8,128)(2,1)S(1)}, u32[]{:S(2)}, u32[]{:S(2)}) collective-permute-start(bf16[208,256]{1,0:T(8,128)(2,1)S(1)} %get-tuple-element.117), channel_id=1, source_target_pairs={{0,4},{1,5},{2,6},{3,7},{4,0},{5,1},{6,2},{7,3},{8,12},{9,13},{10,... | collective-permute-start | bytes 319496 | tf_op jit(solution)/shard_map/ppermute | solution.py:45
  105.6 1.4 %collective-permute-start.37 = (bf16[208,256]{1,0:T(8,128)(2,1)S(1)}, bf16[208,256]{1,0:T(8,128)(2,1)S(1)}, u32[]{:S(2)}, u32[]{:S(2)}) collective-permute-start(bf16[208,256]{1,0:T(8,128)(2,1)S(1)} %get-tuple-element.120), channel_id=1, source_target_pairs={{0,6},{1,7},{2,4},{3,5},{4,2},{5,3},{6,0},{7,1},{8,14},{9,15},{10,... | collective-permute-start | bytes 319496 | tf_op jit(solution)/shard_map/ppermute | solution.py:45
  108.2 2.6 %collective-permute-done.35 = bf16[208,256]{1,0:T(8,128)(2,1)S(1)} collective-permute-done((bf16[208,256]{1,0:T(8,128)(2,1)S(1)}, bf16[208,256]{1,0:T(8,128)(2,1)S(1)}, u32[]{:S(2)}, u32[]{:S(2)}) %collective-permute-start.35) | collective-permute-done | bytes 106528 | tf_op jit(solution)/shard_map/ppermute | solution.py:45
  (109 shorter events, 16.4 us)
Async XLA Ops:
  3.2 8.6 %collective-permute-start.1 = (bf16[4,1024,128]{2,1,0:T(8,128)(2,1)S(1)}, bf16[4,1024,128]{2,1,0:T(8,128)(2,1)}, u32[]{:S(2)}, u32[]{:S(2)}) collective-permute-start(bf16[4,1024,128]{2,1,0:T(8,128)(2,1)S(1)} %join.2.refs_8_), channel_id=1, source_target_pairs={{0,8},{8,0},{1,9},{9,1},{2,10},{10,2},{3,11},{11,3},{4,12},{12,4},... | collective-permute-start | bytes 3145736 | tf_op jit(solution)/shard_map/ppermute | solution.py:45
  3.3 31.0 %collective-permute-start.10 = (bf16[4,1024,128]{2,1,0:T(8,128)(2,1)S(1)}, bf16[4,1024,128]{2,1,0:T(8,128)(2,1)}, u32[]{:S(2)}, u32[]{:S(2)}) collective-permute-start(bf16[4,1024,128]{2,1,0:T(8,128)(2,1)S(1)} %join.2.refs_8_), channel_id=1, source_target_pairs={{0,16},{16,0},{1,17},{17,1},{2,18},{18,2},{3,19},{19,3},{4,20},{20... | collective-permute-start | bytes 3145736 | tf_op jit(solution)/shard_map/ppermute | solution.py:45
  5.0 6.7 %collective-permute-start = (bf16[208,256]{1,0:T(8,128)(2,1)}, bf16[208,256]{1,0:T(8,128)(2,1)S(1)}, u32[]{:S(2)}, u32[]{:S(2)}) collective-permute-start(bf16[208,256]{1,0:T(8,128)(2,1)} %bitcast.14), channel_id=1, source_target_pairs={{0,1},{1,0},{2,3},{3,2},{4,5},{5,4},{6,7},{7,6},{8,9},{9,8},{10,11... | collective-permute-start | bytes 319496 | tf_op jit(solution)/shard_map/ppermute | solution.py:45
  8.1 15.4 %collective-permute-start.2 = (bf16[128,2048]{1,0:T(8,128)(2,1)S(1)}, bf16[128,2048]{1,0:T(8,128)(2,1)}, u32[]{:S(2)}, u32[]{:S(2)}) collective-permute-start(bf16[128,2048]{1,0:T(8,128)(2,1)S(1)} %constant_dynamic-slice_fusion.5.a_ref), channel_id=1, source_target_pairs={{0,1},{1,0},{2,3},{3,2},{4,5},{5,4},{6,7},{7,6},{8,9},{9,8},{10,11... | collective-permute-start | bytes 1572872 | tf_op jit(solution)/shard_map/ppermute | solution.py:45
  11.8 11.7 %collective-permute-start.3 = (bf16[2,208,256]{2,1,0:T(8,128)(2,1)S(1)}, bf16[2,208,256]{2,1,0:T(8,128)(2,1)S(1)}, u32[]{:S(2)}, u32[]{:S(2)}) collective-permute-start(bf16[2,208,256]{2,1,0:T(8,128)(2,1)S(1)} %pad_maximum_fusion.refs_0_.refs_8_), channel_id=1, source_target_pairs={{0,2},{2,0},{4,6},{6,4},{1,3},{3,1},{5,7},{7,5},{8,10},{10,8},{12,... | collective-permute-start | bytes 638984 | tf_op jit(solution)/shard_map/ppermute | solution.py:45
  13.8 13.5 %collective-permute-start.6 = (bf16[2,208,256]{2,1,0:T(8,128)(2,1)S(1)}, bf16[2,208,256]{2,1,0:T(8,128)(2,1)S(1)}, u32[]{:S(2)}, u32[]{:S(2)}) collective-permute-start(bf16[2,208,256]{2,1,0:T(8,128)(2,1)S(1)} %pad_maximum_fusion.refs_0_.refs_8_), channel_id=1, source_target_pairs={{0,6},{2,4},{4,2},{6,0},{1,7},{3,5},{5,3},{7,1},{8,14},{10,12},{12... | collective-permute-start | bytes 638984 | tf_op jit(solution)/shard_map/ppermute | solution.py:45
  16.4 10.9 %collective-permute-start.5 = (bf16[2,208,256]{2,1,0:T(8,128)(2,1)S(1)}, bf16[2,208,256]{2,1,0:T(8,128)(2,1)S(1)}, u32[]{:S(2)}, u32[]{:S(2)}) collective-permute-start(bf16[2,208,256]{2,1,0:T(8,128)(2,1)S(1)} %pad_maximum_fusion.refs_0_.refs_8_), channel_id=1, source_target_pairs={{0,4},{2,6},{4,0},{6,2},{1,5},{3,7},{5,1},{7,3},{8,12},{10,14},{12... | collective-permute-start | bytes 638984 | tf_op jit(solution)/shard_map/ppermute | solution.py:45
  24.6 15.6 %collective-permute-start.8 = (bf16[256,2048]{1,0:T(8,128)(2,1)S(1)}, bf16[256,2048]{1,0:T(8,128)(2,1)S(1)}, u32[]{:S(2)}, u32[]{:S(2)}) collective-permute-start(bf16[256,2048]{1,0:T(8,128)(2,1)S(1)} %join.3.refs_12_), channel_id=1, source_target_pairs={{0,2},{1,3},{2,0},{3,1},{4,6},{5,7},{6,4},{7,5},{8,14},{9,15},{10,... | collective-permute-start | bytes 3145736 | tf_op jit(solution)/shard_map/ppermute | solution.py:56
  29.5 10.8 %collective-permute-start.12 = (bf16[208,256]{1,0:T(8,128)(2,1)S(1)}, bf16[208,256]{1,0:T(8,128)(2,1)S(1)}, u32[]{:S(2)}, u32[]{:S(2)}) collective-permute-start(bf16[208,256]{1,0:T(8,128)(2,1)S(1)} %get-tuple-element.79.refs_0_), channel_id=1, source_target_pairs={{0,112},{16,96},{32,80},{48,64},{64,48},{80,32},{96,16},{112,0},{1... | collective-permute-start | bytes 319496 | tf_op jit(solution)/shard_map/ppermute | solution.py:45
  32.3 8.4 %collective-permute-start.11 = (bf16[208,256]{1,0:T(8,128)(2,1)S(1)}, bf16[208,256]{1,0:T(8,128)(2,1)S(1)}, u32[]{:S(2)}, u32[]{:S(2)}) collective-permute-start(bf16[208,256]{1,0:T(8,128)(2,1)S(1)} %get-tuple-element.79.refs_0_), channel_id=1, source_target_pairs={{0,64},{16,80},{32,96},{48,112},{64,0},{80,16},{96,32},{112,48},{1... | collective-permute-start | bytes 319496 | tf_op jit(solution)/shard_map/ppermute | solution.py:45
  33.2 6.5 %collective-permute-start.7 = (bf16[208,256]{1,0:T(8,128)(2,1)S(1)}, bf16[208,256]{1,0:T(8,128)(2,1)S(1)}, u32[]{:S(2)}, u32[]{:S(2)}) collective-permute-start(bf16[208,256]{1,0:T(8,128)(2,1)S(1)} %get-tuple-element.79.refs_0_), channel_id=1, source_target_pairs={{0,48},{16,32},{32,16},{48,0},{64,112},{80,96},{96,80},{112,64},{1... | collective-permute-start | bytes 319496 | tf_op jit(solution)/shard_map/ppermute | solution.py:45
  39.7 6.2 %collective-permute-start.16 = (bf16[4,1024,128]{2,1,0:T(8,128)(2,1)}, bf16[4,1024,128]{2,1,0:T(8,128)(2,1)S(1)}, u32[]{:S(2)}, u32[]{:S(2)}) collective-permute-start(bf16[4,1024,128]{2,1,0:T(8,128)(2,1)} %collective-permute-done.10.refs_10_), channel_id=1, source_target_pairs={{0,8},{8,0},{1,9},{9,1},{2,10},{10,2},{3,11},{11,3},{4,12},{12,4},... | collective-permute-start | bytes 3145736 | tf_op jit(solution)/shard_map/ppermute | solution.py:45
  40.3 18.0 %collective-permute-start.17 = (bf16[256,2048]{1,0:T(8,128)(2,1)S(1)}, bf16[256,2048]{1,0:T(8,128)(2,1)S(1)}, u32[]{:S(2)}, u32[]{:S(2)}) collective-permute-start(bf16[256,2048]{1,0:T(8,128)(2,1)S(1)} %join.3.refs_12_), channel_id=1, source_target_pairs={{0,8},{8,0},{1,9},{9,1},{2,10},{10,2},{3,11},{11,3},{4,12},{12,4},... | collective-permute-start | bytes 3145736 | tf_op jit(solution)/shard_map/ppermute | solution.py:45
  40.7 17.5 %collective-permute-start.18 = (bf16[256,2048]{1,0:T(8,128)(2,1)S(1)}, bf16[256,2048]{1,0:T(8,128)(2,1)S(1)}, u32[]{:S(2)}, u32[]{:S(2)}) collective-permute-start(bf16[256,2048]{1,0:T(8,128)(2,1)S(1)} %collective-permute-done.8.refs_13_), channel_id=1, source_target_pairs={{0,8},{8,0},{1,9},{9,1},{2,10},{10,2},{3,11},{11,3},{4,12},{12,4},... | collective-permute-start | bytes 3145736 | tf_op jit(solution)/shard_map/ppermute | solution.py:45
  41.1 26.8 %collective-permute-start.4 = (bf16[256,2048]{1,0:T(8,128)(2,1)S(1)}, bf16[256,2048]{1,0:T(8,128)(2,1)S(1)}, u32[]{:S(2)}, u32[]{:S(2)}) collective-permute-start(bf16[256,2048]{1,0:T(8,128)(2,1)S(1)} %join.3.refs_12_), channel_id=1, source_target_pairs={{0,6},{1,7},{2,4},{3,5},{4,2},{5,3},{6,0},{7,1},{8,10},{9,11},{10,... | collective-permute-start | bytes 3145736 | tf_op jit(solution)/shard_map/ppermute | solution.py:56
  44.3 24.0 %collective-permute-start.9 = (bf16[256,2048]{1,0:T(8,128)(2,1)S(1)}, bf16[256,2048]{1,0:T(8,128)(2,1)S(1)}, u32[]{:S(2)}, u32[]{:S(2)}) collective-permute-start(bf16[256,2048]{1,0:T(8,128)(2,1)S(1)} %collective-permute-done.8.refs_13_), channel_id=1, source_target_pairs={{0,6},{1,7},{2,4},{3,5},{4,2},{5,3},{6,0},{7,1},{8,10},{9,11},{10,... | collective-permute-start | bytes 3145736 | tf_op jit(solution)/shard_map/ppermute | solution.py:56
  58.3 6.1 %collective-permute-start.19 = (bf16[2,224,128]{2,1,0:T(8,128)(2,1)S(1)}, bf16[2,224,128]{2,1,0:T(8,128)(2,1)S(1)}, u32[]{:S(2)}, u32[]{:S(2)}) collective-permute-start(bf16[2,224,128]{2,1,0:T(8,128)(2,1)S(1)} %get-tuple-element.101), channel_id=1, source_target_pairs={{0,48},{16,32},{32,16},{48,0},{64,112},{80,96},{96,80},{112,64},{1... | collective-permute-start | bytes 344072 | tf_op jit(solution)/shard_map/ppermute | solution.py:45
  58.4 6.0 %collective-permute-start.20 = (bf16[2,224,128]{2,1,0:T(8,128)(2,1)S(1)}, bf16[2,224,128]{2,1,0:T(8,128)(2,1)S(1)}, u32[]{:S(2)}, u32[]{:S(2)}) collective-permute-start(bf16[2,224,128]{2,1,0:T(8,128)(2,1)S(1)} %get-tuple-element.102), channel_id=1, source_target_pairs={{0,64},{16,80},{32,96},{48,112},{64,0},{80,16},{96,32},{112,48},{1... | collective-permute-start | bytes 344072 | tf_op jit(solution)/shard_map/ppermute | solution.py:45
  59.3 7.7 %collective-permute-start.21 = (bf16[2,224,128]{2,1,0:T(8,128)(2,1)S(1)}, bf16[2,224,128]{2,1,0:T(8,128)(2,1)S(1)}, u32[]{:S(2)}, u32[]{:S(2)}) collective-permute-start(bf16[2,224,128]{2,1,0:T(8,128)(2,1)S(1)} %get-tuple-element.103), channel_id=1, source_target_pairs={{0,112},{16,96},{32,80},{48,64},{64,48},{80,32},{96,16},{112,0},{1... | collective-permute-start | bytes 344072 | tf_op jit(solution)/shard_map/ppermute | solution.py:45
  68.3 8.7 %collective-permute-start.22 = (bf16[256,2048]{1,0:T(8,128)(2,1)S(1)}, bf16[256,2048]{1,0:T(8,128)(2,1)S(1)}, u32[]{:S(2)}, u32[]{:S(2)}) collective-permute-start(bf16[256,2048]{1,0:T(8,128)(2,1)S(1)} %collective-permute-done.4.refs_14_), channel_id=1, source_target_pairs={{0,8},{8,0},{1,9},{9,1},{2,10},{10,2},{3,11},{11,3},{4,12},{12,4},... | collective-permute-start | bytes 3145736 | tf_op jit(solution)/shard_map/ppermute | solution.py:45
  68.3 8.7 %collective-permute-start.23 = (bf16[256,2048]{1,0:T(8,128)(2,1)S(1)}, bf16[256,2048]{1,0:T(8,128)(2,1)S(1)}, u32[]{:S(2)}, u32[]{:S(2)}) collective-permute-start(bf16[256,2048]{1,0:T(8,128)(2,1)S(1)} %collective-permute-done.9.refs_15_), channel_id=1, source_target_pairs={{0,8},{8,0},{1,9},{9,1},{2,10},{10,2},{3,11},{11,3},{4,12},{12,4},... | collective-permute-start | bytes 3145736 | tf_op jit(solution)/shard_map/ppermute | solution.py:45
  68.8 12.4 %collective-permute-start.30 = (bf16[208,256]{1,0:T(8,128)(2,1)S(1)}, bf16[208,256]{1,0:T(8,128)(2,1)S(1)}, u32[]{:S(2)}, u32[]{:S(2)}) collective-permute-start(bf16[208,256]{1,0:T(8,128)(2,1)S(1)} %merge.1.refs_0_), channel_id=1, source_target_pairs={{0,5},{1,4},{2,7},{3,6},{4,1},{5,0},{6,3},{7,2},{8,13},{9,12},{10,... | collective-permute-start | bytes 319496 | tf_op jit(solution)/shard_map/ppermute | solution.py:56
  72.8 8.7 %collective-permute-start.28 = (bf16[208,256]{1,0:T(8,128)(2,1)S(1)}, bf16[208,256]{1,0:T(8,128)(2,1)S(1)}, u32[]{:S(2)}, u32[]{:S(2)}) collective-permute-start(bf16[208,256]{1,0:T(8,128)(2,1)S(1)} %merge.1.refs_0_), channel_id=1, source_target_pairs={{0,7},{1,6},{2,5},{3,4},{4,3},{5,2},{6,1},{7,0},{8,11},{9,10},{10,... | collective-permute-start | bytes 319496 | tf_op jit(solution)/shard_map/ppermute | solution.py:56
  74.4 8.5 %collective-permute-start.26 = (bf16[208,256]{1,0:T(8,128)(2,1)S(1)}, bf16[208,256]{1,0:T(8,128)(2,1)S(1)}, u32[]{:S(2)}, u32[]{:S(2)}) collective-permute-start(bf16[208,256]{1,0:T(8,128)(2,1)S(1)} %merge.1.refs_0_), channel_id=1, source_target_pairs={{0,3},{1,2},{2,1},{3,0},{4,7},{5,6},{6,5},{7,4},{8,15},{9,14},{10,... | collective-permute-start | bytes 319496 | tf_op jit(solution)/shard_map/ppermute | solution.py:56
  77.1 8.5 %collective-permute-start.29 = (bf16[208,256]{1,0:T(8,128)(2,1)S(1)}, bf16[208,256]{1,0:T(8,128)(2,1)S(1)}, u32[]{:S(2)}, u32[]{:S(2)}) collective-permute-start(bf16[208,256]{1,0:T(8,128)(2,1)S(1)} %merge.1.refs_0_), channel_id=1, source_target_pairs={{0,4},{1,5},{2,6},{3,7},{4,0},{5,1},{6,2},{7,3},{8,12},{9,13},{10,... | collective-permute-start | bytes 319496 | tf_op jit(solution)/shard_map/ppermute | solution.py:56
  79.9 7.2 %collective-permute-start.27 = (bf16[208,256]{1,0:T(8,128)(2,1)S(1)}, bf16[208,256]{1,0:T(8,128)(2,1)S(1)}, u32[]{:S(2)}, u32[]{:S(2)}) collective-permute-start(bf16[208,256]{1,0:T(8,128)(2,1)S(1)} %merge.1.refs_0_), channel_id=1, source_target_pairs={{0,6},{1,7},{2,4},{3,5},{4,2},{5,3},{6,0},{7,1},{8,10},{9,11},{10,... | collective-permute-start | bytes 319496 | tf_op jit(solution)/shard_map/ppermute | solution.py:56
  81.5 6.2 %collective-permute-start.24 = (bf16[208,256]{1,0:T(8,128)(2,1)S(1)}, bf16[208,256]{1,0:T(8,128)(2,1)S(1)}, u32[]{:S(2)}, u32[]{:S(2)}) collective-permute-start(bf16[208,256]{1,0:T(8,128)(2,1)S(1)} %merge.1.refs_0_), channel_id=1, source_target_pairs={{0,1},{1,0},{2,3},{3,2},{4,5},{5,4},{6,7},{7,6},{8,9},{9,8},{10,11... | collective-permute-start | bytes 319496 | tf_op jit(solution)/shard_map/ppermute | solution.py:56
  92.9 12.7 %collective-permute-start.31 = (bf16[208,256]{1,0:T(8,128)(2,1)S(1)}, bf16[208,256]{1,0:T(8,128)(2,1)S(1)}, u32[]{:S(2)}, u32[]{:S(2)}) collective-permute-start(bf16[208,256]{1,0:T(8,128)(2,1)S(1)} %get-tuple-element.114), channel_id=1, source_target_pairs={{0,5},{1,4},{2,7},{3,6},{4,1},{5,0},{6,3},{7,2},{8,13},{9,12},{10,... | collective-permute-start | bytes 319496 | tf_op jit(solution)/shard_map/ppermute | solution.py:45
  98.1 7.5 %collective-permute-start.32 = (bf16[208,256]{1,0:T(8,128)(2,1)S(1)}, bf16[208,256]{1,0:T(8,128)(2,1)S(1)}, u32[]{:S(2)}, u32[]{:S(2)}) collective-permute-start(bf16[208,256]{1,0:T(8,128)(2,1)S(1)} %get-tuple-element.115), channel_id=1, source_target_pairs={{0,3},{1,2},{2,1},{3,0},{4,7},{5,6},{6,5},{7,4},{8,11},{9,10},{10,... | collective-permute-start | bytes 319496 | tf_op jit(solution)/shard_map/ppermute | solution.py:45
  98.3 9.6 %collective-permute-start.33 = (bf16[208,256]{1,0:T(8,128)(2,1)S(1)}, bf16[208,256]{1,0:T(8,128)(2,1)S(1)}, u32[]{:S(2)}, u32[]{:S(2)}) collective-permute-start(bf16[208,256]{1,0:T(8,128)(2,1)S(1)} %get-tuple-element.116), channel_id=1, source_target_pairs={{0,7},{1,6},{2,5},{3,4},{4,3},{5,2},{6,1},{7,0},{8,15},{9,14},{10,... | collective-permute-start | bytes 319496 | tf_op jit(solution)/shard_map/ppermute | solution.py:45
  100.4 7.8 %collective-permute-start.34 = (bf16[208,256]{1,0:T(8,128)(2,1)S(1)}, bf16[208,256]{1,0:T(8,128)(2,1)S(1)}, u32[]{:S(2)}, u32[]{:S(2)}) collective-permute-start(bf16[208,256]{1,0:T(8,128)(2,1)S(1)} %get-tuple-element.117), channel_id=1, source_target_pairs={{0,4},{1,5},{2,6},{3,7},{4,0},{5,1},{6,2},{7,3},{8,12},{9,13},{10,... | collective-permute-start | bytes 319496 | tf_op jit(solution)/shard_map/ppermute | solution.py:45
  104.6 6.2 %collective-permute-start.35 = (bf16[208,256]{1,0:T(8,128)(2,1)S(1)}, bf16[208,256]{1,0:T(8,128)(2,1)S(1)}, u32[]{:S(2)}, u32[]{:S(2)}) collective-permute-start(bf16[208,256]{1,0:T(8,128)(2,1)S(1)} %get-tuple-element.118), channel_id=1, source_target_pairs={{0,1},{1,0},{2,3},{3,2},{4,5},{5,4},{6,7},{7,6},{8,9},{9,8},{10,11... | collective-permute-start | bytes 319496 | tf_op jit(solution)/shard_map/ppermute | solution.py:45
  (22 other events, 429.9 us)

commit v6 on v5

--- a/solution.py
+++ b/solution.py
@@ -118,11 +118,12 @@
         dk = jnp.dot(x, wk[rows, :], preferred_element_type=F32)
         dv = jnp.dot(x, wv[rows, :], preferred_element_type=F32)
         q, k, v = (dq, dk, dv) if q is None else (q + dq, k + dk, v + dv)
+    factor = hd**-0.5 * math.log2(math.e)
     c = cos[...].reshape(q.shape[0], hd)
     s = sin[...].reshape(q.shape[0], hd)
     for h in range(q.shape[1] // hd):
         part = q[:, h * hd : (h + 1) * hd]
-        q_out[:, h * hd : (h + 1) * hd] = rotate(head_norm(part) * qg[...], c, s).astype(BF16)
+        q_out[:, h * hd : (h + 1) * hd] = (rotate(head_norm(part) * qg[...], c, s) * factor).astype(BF16)
     kv_out[:, :hd] = rotate(head_norm(k) * kg[...], c, s).astype(BF16)
     kv_out[:, hd:] = v.astype(BF16)
 
@@ -204,7 +205,6 @@
     run_acc[...] = jnp.zeros(run_acc.shape, F32)
     for c in copies:
         c.wait()
-    factor = hd**-0.5 * math.log2(math.e)
 
     def score(at):
         qi, ki, k_nat, _ = entry(at)
@@ -228,8 +228,8 @@
         scores = jnp.where(places[pl.ds(k_nat, 1), :] <= bound, scores, NEG)
         old = run_m[qi]
         new = jnp.maximum(old, jnp.max(scores, axis=-1, keepdims=True))
-        shrink = jnp.exp2((old - new) * factor)
-        weights = jnp.exp2((scores - new) * factor)
+        shrink = jnp.exp2(old - new)
+        weights = jnp.exp2(scores - new)
         run_m[qi] = new
         run_l[qi] = run_l[qi] * shrink + jnp.sum(weights, axis=-1, keepdims=True)
         return shrink, weights.astype(BF16)
@@ -317,7 +317,7 @@
         tops.append(st[:, 0:2])
         sums.append(st[:, 2:4])
     top = functools.reduce(jnp.maximum, tops)
-    shares = [jnp.exp((m - top) * hd**-0.5) for m in tops]
+    shares = [jnp.exp2(m - top) for m in tops]
     total = functools.reduce(jnp.add, [w * s for w, s in zip(shares, sums)])
     shares = [w / total for w in shares]
     rows = [[], []]

time: 113 us -> 113 us (level)
  waiting for transfers between devices: 28.4 us -> 31.9 us
  Pallas kernels: 21.6 us -> 19 us
    pallas_call x1, Pallas kernels: 12.3 us -> 9.77 us  [attend(): pl.pallas_call(functools.partial(attend_kernel, count), in_specs=[SMEM, S...]
    ppermute x28, waiting for transfers between devices: 22.9 us -> 24.8 us  [swap(): return lax.ppermute(x, axes, [(i, i ^ mask) for i in range(size)])]
    ppermute x10, waiting for transfers between devices: 5.43 us -> 7.06 us  [cross(): return lax.ppermute(x, ('core', 'z', 'xhi'), perm)]
  transfers between devices with their start and end apart: 38 -> 38, of which waited for: 15 -> 16; matrix products, arithmetic and copies ran while one was open for 2% -> 2% of each run, Pallas kernels for 14% -> 12%
where the time goes in v6:
time: 113 us; the launch traced here: 112 us
  starting transfers between devices  54.9 us (49%)
  waiting for transfers between devices  31.9 us (28%)
  Pallas kernels  19 us (17%)
  other arithmetic  3.87 us (3%)
  local copies, waits for them, and re-layouts  2.28 us (2%)
    ppermute x28, starting transfers between devices, swap(): return lax.ppermute(x, axes, [(i, i ^ mask) for i in range(size)])  36 us
    ppermute x28, waiting for transfers between devices, swap(): return lax.ppermute(x, axes, [(i, i ^ mask) for i in range(size)])  24.8 us
    ppermute x10, starting transfers between devices, cross(): return lax.ppermute(x, ('core', 'z', 'xhi'), perm)  18.9 us
    pallas_call x1, Pallas kernels, attend(): pl.pallas_call(functools.partial(attend_kernel, count), in_specs=[SMEM, S...  9.77 us
    ppermute x10, waiting for transfers between devices, cross(): return lax.ppermute(x, ('core', 'z', 'xhi'), perm)  7.06 us
    pallas_call x1, Pallas kernels, on_device(): pl.pallas_call(functools.partial(feed_kernel, n), in_specs=[SMEM] + [VMEM...  5.21 us
  transfers between devices with their start and end apart: 38, of which 16 were waited for; matrix products, arithmetic and copies ran while one was open for 2% of the time, Pallas kernels for 12%

profile of v6, /device:TPU:0, one launch (start us, length us, event | category | flops | bytes accessed | tf_op | source)
XLA Modules:
  0.0 112.4 jit_solution(2443163440469312609)
XLA Ops:
  3.3 1.7 %collective-permute-start.10 = (bf16[4,1024,128]{2,1,0:T(8,128)(2,1)S(1)}, bf16[4,1024,128]{2,1,0:T(8,128)(2,1)}, u32[]{:S(2)}, u32[]{:S(2)}) collective-permute-start(bf16[4,1024,128]{2,1,0:T(8,128)(2,1)S(1)} %join.2.refs_8_), channel_id=1, source_target_pairs={{0,16},{16,0},{1,17},{17,1},{2,18},{18,2},{3,19},{19,3},{4,20},{20... | collective-permute-start | bytes 3145736 | tf_op jit(solution)/shard_map/ppermute | solution.py:45
  5.0 3.0 %collective-permute-start = (bf16[208,256]{1,0:T(8,128)(2,1)}, bf16[208,256]{1,0:T(8,128)(2,1)S(1)}, u32[]{:S(2)}, u32[]{:S(2)}) collective-permute-start(bf16[208,256]{1,0:T(8,128)(2,1)} %bitcast.14), channel_id=1, source_target_pairs={{0,1},{1,0},{2,3},{3,2},{4,5},{5,4},{6,7},{7,6},{8,9},{9,8},{10,11... | collective-permute-start | bytes 319496 | tf_op jit(solution)/shard_map/ppermute | solution.py:45
  8.9 2.9 %collective-permute-done = bf16[208,256]{1,0:T(8,128)(2,1)S(1)} collective-permute-done((bf16[208,256]{1,0:T(8,128)(2,1)}, bf16[208,256]{1,0:T(8,128)(2,1)S(1)}, u32[]{:S(2)}, u32[]{:S(2)}) %collective-permute-start) | collective-permute-done | bytes 106528 | tf_op jit(solution)/shard_map/ppermute | solution.py:45
  11.8 2.0 %collective-permute-start.3 = (bf16[2,208,256]{2,1,0:T(8,128)(2,1)S(1)}, bf16[2,208,256]{2,1,0:T(8,128)(2,1)S(1)}, u32[]{:S(2)}, u32[]{:S(2)}) collective-permute-start(bf16[2,208,256]{2,1,0:T(8,128)(2,1)S(1)} %pad_maximum_fusion.refs_0_.refs_8_), channel_id=1, source_target_pairs={{0,2},{2,0},{4,6},{6,4},{1,3},{3,1},{5,7},{7,5},{8,10},{10,8},{12,... | collective-permute-start | bytes 638984 | tf_op jit(solution)/shard_map/ppermute | solution.py:45
  13.8 2.6 %collective-permute-start.6 = (bf16[2,208,256]{2,1,0:T(8,128)(2,1)S(1)}, bf16[2,208,256]{2,1,0:T(8,128)(2,1)S(1)}, u32[]{:S(2)}, u32[]{:S(2)}) collective-permute-start(bf16[2,208,256]{2,1,0:T(8,128)(2,1)S(1)} %pad_maximum_fusion.refs_0_.refs_8_), channel_id=1, source_target_pairs={{0,6},{2,4},{4,2},{6,0},{1,7},{3,5},{5,3},{7,1},{8,14},{10,12},{12... | collective-permute-start | bytes 638984 | tf_op jit(solution)/shard_map/ppermute | solution.py:45
  16.4 1.2 %collective-permute-start.5 = (bf16[2,208,256]{2,1,0:T(8,128)(2,1)S(1)}, bf16[2,208,256]{2,1,0:T(8,128)(2,1)S(1)}, u32[]{:S(2)}, u32[]{:S(2)}) collective-permute-start(bf16[2,208,256]{2,1,0:T(8,128)(2,1)S(1)} %pad_maximum_fusion.refs_0_.refs_8_), channel_id=1, source_target_pairs={{0,4},{2,6},{4,0},{6,2},{1,5},{3,7},{5,1},{7,3},{8,12},{10,14},{12... | collective-permute-start | bytes 638984 | tf_op jit(solution)/shard_map/ppermute | solution.py:45
  17.6 5.9 %collective-permute-done.2.b_ref = bf16[128,2048]{1,0:T(8,128)(2,1)} collective-permute-done((bf16[128,2048]{1,0:T(8,128)(2,1)S(1)}, bf16[128,2048]{1,0:T(8,128)(2,1)}, u32[]{:S(2)}, u32[]{:S(2)}) %collective-permute-start.2) | collective-permute-done | bytes 524320 | tf_op jit(solution)/shard_map/ppermute | solution.py:45
  23.5 1.1 join.3.refs_12_
  24.6 2.0 %collective-permute-start.8 = (bf16[256,2048]{1,0:T(8,128)(2,1)S(1)}, bf16[256,2048]{1,0:T(8,128)(2,1)S(1)}, u32[]{:S(2)}, u32[]{:S(2)}) collective-permute-start(bf16[256,2048]{1,0:T(8,128)(2,1)S(1)} %join.3.refs_12_), channel_id=1, source_target_pairs={{0,2},{1,3},{2,0},{3,1},{4,6},{5,7},{6,4},{7,5},{8,14},{9,15},{10,... | collective-permute-start | bytes 3145736 | tf_op jit(solution)/shard_map/ppermute | solution.py:56
  27.4 2.0 %project.1 = (bf16[208,256]{1,0:T(8,128)(2,1)S(1)}, bf16[208,256]{1,0:T(8,128)(2,1)S(1)}) custom-call(s32[4]{0:T(128)S(1)} %pad_add_fusion.1.me_ref.ids, bf16[2,208,256]{2,1,0:T(8,128)(2,1)S(1)} %pad_maximum_fusion.refs_0_.refs_8_, bf16[2,208,256]{2,1,0:T(8,128)(2,1)S(1)} %collective-permute-done.3.refs_1_.refs_9_, ...), custom_call_target="tpu_custom_call" | custom-call | tf_op jit(solution)/shard_map/project/pallas_call | solution.py:456
  29.5 2.8 %collective-permute-start.12 = (bf16[208,256]{1,0:T(8,128)(2,1)S(1)}, bf16[208,256]{1,0:T(8,128)(2,1)S(1)}, u32[]{:S(2)}, u32[]{:S(2)}) collective-permute-start(bf16[208,256]{1,0:T(8,128)(2,1)S(1)} %get-tuple-element.79.refs_0_), channel_id=1, source_target_pairs={{0,112},{16,96},{32,80},{48,64},{64,48},{80,32},{96,16},{112,0},{1... | collective-permute-start | bytes 319496 | tf_op jit(solution)/shard_map/ppermute | solution.py:45
  34.4 5.3 %collective-permute-done.7.refs_1_ = bf16[208,256]{1,0:T(8,128)(2,1)S(1)} collective-permute-done((bf16[208,256]{1,0:T(8,128)(2,1)S(1)}, bf16[208,256]{1,0:T(8,128)(2,1)S(1)}, u32[]{:S(2)}, u32[]{:S(2)}) %collective-permute-start.7) | collective-permute-done | bytes 106528 | tf_op jit(solution)/shard_map/ppermute | solution.py:45
  41.1 3.2 %collective-permute-start.4 = (bf16[256,2048]{1,0:T(8,128)(2,1)S(1)}, bf16[256,2048]{1,0:T(8,128)(2,1)S(1)}, u32[]{:S(2)}, u32[]{:S(2)}) collective-permute-start(bf16[256,2048]{1,0:T(8,128)(2,1)S(1)} %join.3.refs_12_), channel_id=1, source_target_pairs={{0,6},{1,7},{2,4},{3,5},{4,2},{5,3},{6,0},{7,1},{8,10},{9,11},{10,... | collective-permute-start | bytes 3145736 | tf_op jit(solution)/shard_map/ppermute | solution.py:56
  46.0 9.8 %attend.1 = (bf16[2,224,128]{2,1,0:T(8,128)(2,1)S(1)}, bf16[2,224,128]{2,1,0:T(8,128)(2,1)S(1)}, bf16[2,224,128]{2,1,0:T(8,128)(2,1)S(1)}, bf16[2,224,128]{2,1,0:T(8,128)(2,1)S(1)}) custom-call(s32[4]{0:T(128)S(1)} %pad_add_fusion.1.me_ref.ids, s32[64]{0:T(128)S(1)} %pad_add_fusion.2.tab, f32[8,1024]{1,0:T(8,128)S(1)} %broadcast_select_fusion.kpos, ...), custom_call_target="tpu_custom_call" | custom-call | tf_op jit(solution)/shard_map/attend/pallas_call | solution.py:283
  55.8 3.3 %collective-permute-start.20 = (bf16[2,224,128]{2,1,0:T(8,128)(2,1)S(1)}, bf16[2,224,128]{2,1,0:T(8,128)(2,1)S(1)}, u32[]{:S(2)}, u32[]{:S(2)}) collective-permute-start(bf16[2,224,128]{2,1,0:T(8,128)(2,1)S(1)} %get-tuple-element.102), channel_id=1, source_target_pairs={{0,64},{16,80},{32,96},{48,112},{64,0},{80,16},{96,32},{112,48},{1... | collective-permute-start | bytes 344072 | tf_op jit(solution)/shard_map/ppermute | solution.py:45
  59.1 1.4 %collective-permute-start.21 = (bf16[2,224,128]{2,1,0:T(8,128)(2,1)S(1)}, bf16[2,224,128]{2,1,0:T(8,128)(2,1)S(1)}, u32[]{:S(2)}, u32[]{:S(2)}) collective-permute-start(bf16[2,224,128]{2,1,0:T(8,128)(2,1)S(1)} %get-tuple-element.103), channel_id=1, source_target_pairs={{0,112},{16,96},{32,80},{48,64},{64,48},{80,32},{96,16},{112,0},{1... | collective-permute-start | bytes 344072 | tf_op jit(solution)/shard_map/ppermute | solution.py:45
  60.5 2.5 %collective-permute-done.19.refs_1_ = bf16[2,224,128]{2,1,0:T(8,128)(2,1)S(1)} collective-permute-done((bf16[2,224,128]{2,1,0:T(8,128)(2,1)S(1)}, bf16[2,224,128]{2,1,0:T(8,128)(2,1)S(1)}, u32[]{:S(2)}, u32[]{:S(2)}) %collective-permute-start.19) | collective-permute-done | bytes 114720 | tf_op jit(solution)/shard_map/ppermute | solution.py:45
  63.1 3.0 %collective-permute-done.21.refs_3_ = bf16[2,224,128]{2,1,0:T(8,128)(2,1)S(1)} collective-permute-done((bf16[2,224,128]{2,1,0:T(8,128)(2,1)S(1)}, bf16[2,224,128]{2,1,0:T(8,128)(2,1)S(1)}, u32[]{:S(2)}, u32[]{:S(2)}) %collective-permute-start.21) | collective-permute-done | bytes 114720 | tf_op jit(solution)/shard_map/ppermute | solution.py:45
  66.9 1.5 %collective-permute-done.9.refs_15_ = bf16[256,2048]{1,0:T(8,128)(2,1)S(1)} collective-permute-done((bf16[256,2048]{1,0:T(8,128)(2,1)S(1)}, bf16[256,2048]{1,0:T(8,128)(2,1)S(1)}, u32[]{:S(2)}, u32[]{:S(2)}) %collective-permute-start.9) | collective-permute-done | bytes 1048608 | tf_op jit(solution)/shard_map/ppermute | solution.py:56
  68.8 3.9 %collective-permute-start.30 = (bf16[208,256]{1,0:T(8,128)(2,1)S(1)}, bf16[208,256]{1,0:T(8,128)(2,1)S(1)}, u32[]{:S(2)}, u32[]{:S(2)}) collective-permute-start(bf16[208,256]{1,0:T(8,128)(2,1)S(1)} %merge.1.refs_0_), channel_id=1, source_target_pairs={{0,5},{1,4},{2,7},{3,6},{4,1},{5,0},{6,3},{7,2},{8,13},{9,12},{10,... | collective-permute-start | bytes 319496 | tf_op jit(solution)/shard_map/ppermute | solution.py:56
  72.8 1.4 %collective-permute-start.28 = (bf16[208,256]{1,0:T(8,128)(2,1)S(1)}, bf16[208,256]{1,0:T(8,128)(2,1)S(1)}, u32[]{:S(2)}, u32[]{:S(2)}) collective-permute-start(bf16[208,256]{1,0:T(8,128)(2,1)S(1)} %merge.1.refs_0_), channel_id=1, source_target_pairs={{0,7},{1,6},{2,5},{3,4},{4,3},{5,2},{6,1},{7,0},{8,11},{9,10},{10,... | collective-permute-start | bytes 319496 | tf_op jit(solution)/shard_map/ppermute | solution.py:56
  74.1 2.9 %collective-permute-start.26 = (bf16[208,256]{1,0:T(8,128)(2,1)S(1)}, bf16[208,256]{1,0:T(8,128)(2,1)S(1)}, u32[]{:S(2)}, u32[]{:S(2)}) collective-permute-start(bf16[208,256]{1,0:T(8,128)(2,1)S(1)} %merge.1.refs_0_), channel_id=1, source_target_pairs={{0,3},{1,2},{2,1},{3,0},{4,7},{5,6},{6,5},{7,4},{8,15},{9,14},{10,... | collective-permute-start | bytes 319496 | tf_op jit(solution)/shard_map/ppermute | solution.py:56
  77.1 2.8 %collective-permute-start.29 = (bf16[208,256]{1,0:T(8,128)(2,1)S(1)}, bf16[208,256]{1,0:T(8,128)(2,1)S(1)}, u32[]{:S(2)}, u32[]{:S(2)}) collective-permute-start(bf16[208,256]{1,0:T(8,128)(2,1)S(1)} %merge.1.refs_0_), channel_id=1, source_target_pairs={{0,4},{1,5},{2,6},{3,7},{4,0},{5,1},{6,2},{7,3},{8,12},{9,13},{10,... | collective-permute-start | bytes 319496 | tf_op jit(solution)/shard_map/ppermute | solution.py:56
  81.5 1.2 %collective-permute-start.24 = (bf16[208,256]{1,0:T(8,128)(2,1)S(1)}, bf16[208,256]{1,0:T(8,128)(2,1)S(1)}, u32[]{:S(2)}, u32[]{:S(2)}) collective-permute-start(bf16[208,256]{1,0:T(8,128)(2,1)S(1)} %merge.1.refs_0_), channel_id=1, source_target_pairs={{0,1},{1,0},{2,3},{3,2},{4,5},{5,4},{6,7},{7,6},{8,9},{9,8},{10,11... | collective-permute-start | bytes 319496 | tf_op jit(solution)/shard_map/ppermute | solution.py:56
  82.8 2.8 %collective-permute-done.29.refs_6_ = bf16[208,256]{1,0:T(8,128)(2,1)S(1)} collective-permute-done((bf16[208,256]{1,0:T(8,128)(2,1)S(1)}, bf16[208,256]{1,0:T(8,128)(2,1)S(1)}, u32[]{:S(2)}, u32[]{:S(2)}) %collective-permute-start.29) | collective-permute-done | bytes 106528 | tf_op jit(solution)/shard_map/ppermute | solution.py:56
  85.6 1.4 %collective-permute-done.27.refs_4_ = bf16[208,256]{1,0:T(8,128)(2,1)S(1)} collective-permute-done((bf16[208,256]{1,0:T(8,128)(2,1)S(1)}, bf16[208,256]{1,0:T(8,128)(2,1)S(1)}, u32[]{:S(2)}, u32[]{:S(2)}) %collective-permute-start.27) | collective-permute-done | bytes 106528 | tf_op jit(solution)/shard_map/ppermute | solution.py:56
  87.7 5.2 %feed.1 = (bf16[208,256]{1,0:T(8,128)(2,1)S(1)}, bf16[208,256]{1,0:T(8,128)(2,1)S(1)}, bf16[208,256]{1,0:T(8,128)(2,1)S(1)}, bf16[208,256]{1,0:T(8,128)(2,1)S(1)...) custom-call(s32[4]{0:T(128)S(1)} %pad_add_fusion.1.me_ref.ids, ...), custom_call_target="tpu_custom_call" | custom-call | tf_op jit(solution)/shard_map/feed/pallas_call | solution.py:533
  92.9 5.2 %collective-permute-start.31 = (bf16[208,256]{1,0:T(8,128)(2,1)S(1)}, bf16[208,256]{1,0:T(8,128)(2,1)S(1)}, u32[]{:S(2)}, u32[]{:S(2)}) collective-permute-start(bf16[208,256]{1,0:T(8,128)(2,1)S(1)} %get-tuple-element.114), channel_id=1, source_target_pairs={{0,5},{1,4},{2,7},{3,6},{4,1},{5,0},{6,3},{7,2},{8,13},{9,12},{10,... | collective-permute-start | bytes 319496 | tf_op jit(solution)/shard_map/ppermute | solution.py:45
  98.3 1.8 %collective-permute-start.33 = (bf16[208,256]{1,0:T(8,128)(2,1)S(1)}, bf16[208,256]{1,0:T(8,128)(2,1)S(1)}, u32[]{:S(2)}, u32[]{:S(2)}) collective-permute-start(bf16[208,256]{1,0:T(8,128)(2,1)S(1)} %get-tuple-element.116), channel_id=1, source_target_pairs={{0,7},{1,6},{2,5},{3,4},{4,3},{5,2},{6,1},{7,0},{8,15},{9,14},{10,... | collective-permute-start | bytes 319496 | tf_op jit(solution)/shard_map/ppermute | solution.py:45
  100.1 4.5 %collective-permute-start.34 = (bf16[208,256]{1,0:T(8,128)(2,1)S(1)}, bf16[208,256]{1,0:T(8,128)(2,1)S(1)}, u32[]{:S(2)}, u32[]{:S(2)}) collective-permute-start(bf16[208,256]{1,0:T(8,128)(2,1)S(1)} %get-tuple-element.117), channel_id=1, source_target_pairs={{0,4},{1,5},{2,6},{3,7},{4,0},{5,1},{6,2},{7,3},{8,12},{9,13},{10,... | collective-permute-start | bytes 319496 | tf_op jit(solution)/shard_map/ppermute | solution.py:45
  106.6 1.4 %collective-permute-done.33 = bf16[208,256]{1,0:T(8,128)(2,1)S(1)} collective-permute-done((bf16[208,256]{1,0:T(8,128)(2,1)S(1)}, bf16[208,256]{1,0:T(8,128)(2,1)S(1)}, u32[]{:S(2)}, u32[]{:S(2)}) %collective-permute-start.33) | collective-permute-done | bytes 106528 | tf_op jit(solution)/shard_map/ppermute | solution.py:45
  108.2 2.6 %collective-permute-done.35 = bf16[208,256]{1,0:T(8,128)(2,1)S(1)} collective-permute-done((bf16[208,256]{1,0:T(8,128)(2,1)S(1)}, bf16[208,256]{1,0:T(8,128)(2,1)S(1)}, u32[]{:S(2)}, u32[]{:S(2)}) %collective-permute-start.35) | collective-permute-done | bytes 106528 | tf_op jit(solution)/shard_map/ppermute | solution.py:45
  (109 shorter events, 17.7 us)
Async XLA Ops:
  3.2 8.6 %collective-permute-start.1 = (bf16[4,1024,128]{2,1,0:T(8,128)(2,1)S(1)}, bf16[4,1024,128]{2,1,0:T(8,128)(2,1)}, u32[]{:S(2)}, u32[]{:S(2)}) collective-permute-start(bf16[4,1024,128]{2,1,0:T(8,128)(2,1)S(1)} %join.2.refs_8_), channel_id=1, source_target_pairs={{0,8},{8,0},{1,9},{9,1},{2,10},{10,2},{3,11},{11,3},{4,12},{12,4},... | collective-permute-start | bytes 3145736 | tf_op jit(solution)/shard_map/ppermute | solution.py:45
  3.3 31.0 %collective-permute-start.10 = (bf16[4,1024,128]{2,1,0:T(8,128)(2,1)S(1)}, bf16[4,1024,128]{2,1,0:T(8,128)(2,1)}, u32[]{:S(2)}, u32[]{:S(2)}) collective-permute-start(bf16[4,1024,128]{2,1,0:T(8,128)(2,1)S(1)} %join.2.refs_8_), channel_id=1, source_target_pairs={{0,16},{16,0},{1,17},{17,1},{2,18},{18,2},{3,19},{19,3},{4,20},{20... | collective-permute-start | bytes 3145736 | tf_op jit(solution)/shard_map/ppermute | solution.py:45
  5.0 6.7 %collective-permute-start = (bf16[208,256]{1,0:T(8,128)(2,1)}, bf16[208,256]{1,0:T(8,128)(2,1)S(1)}, u32[]{:S(2)}, u32[]{:S(2)}) collective-permute-start(bf16[208,256]{1,0:T(8,128)(2,1)} %bitcast.14), channel_id=1, source_target_pairs={{0,1},{1,0},{2,3},{3,2},{4,5},{5,4},{6,7},{7,6},{8,9},{9,8},{10,11... | collective-permute-start | bytes 319496 | tf_op jit(solution)/shard_map/ppermute | solution.py:45
  8.1 15.4 %collective-permute-start.2 = (bf16[128,2048]{1,0:T(8,128)(2,1)S(1)}, bf16[128,2048]{1,0:T(8,128)(2,1)}, u32[]{:S(2)}, u32[]{:S(2)}) collective-permute-start(bf16[128,2048]{1,0:T(8,128)(2,1)S(1)} %constant_dynamic-slice_fusion.5.a_ref), channel_id=1, source_target_pairs={{0,1},{1,0},{2,3},{3,2},{4,5},{5,4},{6,7},{7,6},{8,9},{9,8},{10,11... | collective-permute-start | bytes 1572872 | tf_op jit(solution)/shard_map/ppermute | solution.py:45
  11.8 11.7 %collective-permute-start.3 = (bf16[2,208,256]{2,1,0:T(8,128)(2,1)S(1)}, bf16[2,208,256]{2,1,0:T(8,128)(2,1)S(1)}, u32[]{:S(2)}, u32[]{:S(2)}) collective-permute-start(bf16[2,208,256]{2,1,0:T(8,128)(2,1)S(1)} %pad_maximum_fusion.refs_0_.refs_8_), channel_id=1, source_target_pairs={{0,2},{2,0},{4,6},{6,4},{1,3},{3,1},{5,7},{7,5},{8,10},{10,8},{12,... | collective-permute-start | bytes 638984 | tf_op jit(solution)/shard_map/ppermute | solution.py:45
  13.8 13.5 %collective-permute-start.6 = (bf16[2,208,256]{2,1,0:T(8,128)(2,1)S(1)}, bf16[2,208,256]{2,1,0:T(8,128)(2,1)S(1)}, u32[]{:S(2)}, u32[]{:S(2)}) collective-permute-start(bf16[2,208,256]{2,1,0:T(8,128)(2,1)S(1)} %pad_maximum_fusion.refs_0_.refs_8_), channel_id=1, source_target_pairs={{0,6},{2,4},{4,2},{6,0},{1,7},{3,5},{5,3},{7,1},{8,14},{10,12},{12... | collective-permute-start | bytes 638984 | tf_op jit(solution)/shard_map/ppermute | solution.py:45
  16.4 10.9 %collective-permute-start.5 = (bf16[2,208,256]{2,1,0:T(8,128)(2,1)S(1)}, bf16[2,208,256]{2,1,0:T(8,128)(2,1)S(1)}, u32[]{:S(2)}, u32[]{:S(2)}) collective-permute-start(bf16[2,208,256]{2,1,0:T(8,128)(2,1)S(1)} %pad_maximum_fusion.refs_0_.refs_8_), channel_id=1, source_target_pairs={{0,4},{2,6},{4,0},{6,2},{1,5},{3,7},{5,1},{7,3},{8,12},{10,14},{12... | collective-permute-start | bytes 638984 | tf_op jit(solution)/shard_map/ppermute | solution.py:45
  24.6 15.6 %collective-permute-start.8 = (bf16[256,2048]{1,0:T(8,128)(2,1)S(1)}, bf16[256,2048]{1,0:T(8,128)(2,1)S(1)}, u32[]{:S(2)}, u32[]{:S(2)}) collective-permute-start(bf16[256,2048]{1,0:T(8,128)(2,1)S(1)} %join.3.refs_12_), channel_id=1, source_target_pairs={{0,2},{1,3},{2,0},{3,1},{4,6},{5,7},{6,4},{7,5},{8,14},{9,15},{10,... | collective-permute-start | bytes 3145736 | tf_op jit(solution)/shard_map/ppermute | solution.py:56
  29.5 10.8 %collective-permute-start.12 = (bf16[208,256]{1,0:T(8,128)(2,1)S(1)}, bf16[208,256]{1,0:T(8,128)(2,1)S(1)}, u32[]{:S(2)}, u32[]{:S(2)}) collective-permute-start(bf16[208,256]{1,0:T(8,128)(2,1)S(1)} %get-tuple-element.79.refs_0_), channel_id=1, source_target_pairs={{0,112},{16,96},{32,80},{48,64},{64,48},{80,32},{96,16},{112,0},{1... | collective-permute-start | bytes 319496 | tf_op jit(solution)/shard_map/ppermute | solution.py:45
  32.3 8.4 %collective-permute-start.11 = (bf16[208,256]{1,0:T(8,128)(2,1)S(1)}, bf16[208,256]{1,0:T(8,128)(2,1)S(1)}, u32[]{:S(2)}, u32[]{:S(2)}) collective-permute-start(bf16[208,256]{1,0:T(8,128)(2,1)S(1)} %get-tuple-element.79.refs_0_), channel_id=1, source_target_pairs={{0,64},{16,80},{32,96},{48,112},{64,0},{80,16},{96,32},{112,48},{1... | collective-permute-start | bytes 319496 | tf_op jit(solution)/shard_map/ppermute | solution.py:45
  33.2 6.5 %collective-permute-start.7 = (bf16[208,256]{1,0:T(8,128)(2,1)S(1)}, bf16[208,256]{1,0:T(8,128)(2,1)S(1)}, u32[]{:S(2)}, u32[]{:S(2)}) collective-permute-start(bf16[208,256]{1,0:T(8,128)(2,1)S(1)} %get-tuple-element.79.refs_0_), channel_id=1, source_target_pairs={{0,48},{16,32},{32,16},{48,0},{64,112},{80,96},{96,80},{112,64},{1... | collective-permute-start | bytes 319496 | tf_op jit(solution)/shard_map/ppermute | solution.py:45
  39.7 6.2 %collective-permute-start.16 = (bf16[4,1024,128]{2,1,0:T(8,128)(2,1)}, bf16[4,1024,128]{2,1,0:T(8,128)(2,1)S(1)}, u32[]{:S(2)}, u32[]{:S(2)}) collective-permute-start(bf16[4,1024,128]{2,1,0:T(8,128)(2,1)} %collective-permute-done.10.refs_10_), channel_id=1, source_target_pairs={{0,8},{8,0},{1,9},{9,1},{2,10},{10,2},{3,11},{11,3},{4,12},{12,4},... | collective-permute-start | bytes 3145736 | tf_op jit(solution)/shard_map/ppermute | solution.py:45
  40.3 15.4 %collective-permute-start.17 = (bf16[256,2048]{1,0:T(8,128)(2,1)S(1)}, bf16[256,2048]{1,0:T(8,128)(2,1)S(1)}, u32[]{:S(2)}, u32[]{:S(2)}) collective-permute-start(bf16[256,2048]{1,0:T(8,128)(2,1)S(1)} %join.3.refs_12_), channel_id=1, source_target_pairs={{0,8},{8,0},{1,9},{9,1},{2,10},{10,2},{3,11},{11,3},{4,12},{12,4},... | collective-permute-start | bytes 3145736 | tf_op jit(solution)/shard_map/ppermute | solution.py:45
  40.7 15.0 %collective-permute-start.18 = (bf16[256,2048]{1,0:T(8,128)(2,1)S(1)}, bf16[256,2048]{1,0:T(8,128)(2,1)S(1)}, u32[]{:S(2)}, u32[]{:S(2)}) collective-permute-start(bf16[256,2048]{1,0:T(8,128)(2,1)S(1)} %collective-permute-done.8.refs_13_), channel_id=1, source_target_pairs={{0,8},{8,0},{1,9},{9,1},{2,10},{10,2},{3,11},{11,3},{4,12},{12,4},... | collective-permute-start | bytes 3145736 | tf_op jit(solution)/shard_map/ppermute | solution.py:45
  41.1 25.8 %collective-permute-start.4 = (bf16[256,2048]{1,0:T(8,128)(2,1)S(1)}, bf16[256,2048]{1,0:T(8,128)(2,1)S(1)}, u32[]{:S(2)}, u32[]{:S(2)}) collective-permute-start(bf16[256,2048]{1,0:T(8,128)(2,1)S(1)} %join.3.refs_12_), channel_id=1, source_target_pairs={{0,6},{1,7},{2,4},{3,5},{4,2},{5,3},{6,0},{7,1},{8,10},{9,11},{10,... | collective-permute-start | bytes 3145736 | tf_op jit(solution)/shard_map/ppermute | solution.py:56
  44.3 24.0 %collective-permute-start.9 = (bf16[256,2048]{1,0:T(8,128)(2,1)S(1)}, bf16[256,2048]{1,0:T(8,128)(2,1)S(1)}, u32[]{:S(2)}, u32[]{:S(2)}) collective-permute-start(bf16[256,2048]{1,0:T(8,128)(2,1)S(1)} %collective-permute-done.8.refs_13_), channel_id=1, source_target_pairs={{0,6},{1,7},{2,4},{3,5},{4,2},{5,3},{6,0},{7,1},{8,10},{9,11},{10,... | collective-permute-start | bytes 3145736 | tf_op jit(solution)/shard_map/ppermute | solution.py:56
  55.7 7.3 %collective-permute-start.19 = (bf16[2,224,128]{2,1,0:T(8,128)(2,1)S(1)}, bf16[2,224,128]{2,1,0:T(8,128)(2,1)S(1)}, u32[]{:S(2)}, u32[]{:S(2)}) collective-permute-start(bf16[2,224,128]{2,1,0:T(8,128)(2,1)S(1)} %get-tuple-element.101), channel_id=1, source_target_pairs={{0,48},{16,32},{32,16},{48,0},{64,112},{80,96},{96,80},{112,64},{1... | collective-permute-start | bytes 344072 | tf_op jit(solution)/shard_map/ppermute | solution.py:45
  55.8 7.2 %collective-permute-start.20 = (bf16[2,224,128]{2,1,0:T(8,128)(2,1)S(1)}, bf16[2,224,128]{2,1,0:T(8,128)(2,1)S(1)}, u32[]{:S(2)}, u32[]{:S(2)}) collective-permute-start(bf16[2,224,128]{2,1,0:T(8,128)(2,1)S(1)} %get-tuple-element.102), channel_id=1, source_target_pairs={{0,64},{16,80},{32,96},{48,112},{64,0},{80,16},{96,32},{112,48},{1... | collective-permute-start | bytes 344072 | tf_op jit(solution)/shard_map/ppermute | solution.py:45
  59.1 6.9 %collective-permute-start.21 = (bf16[2,224,128]{2,1,0:T(8,128)(2,1)S(1)}, bf16[2,224,128]{2,1,0:T(8,128)(2,1)S(1)}, u32[]{:S(2)}, u32[]{:S(2)}) collective-permute-start(bf16[2,224,128]{2,1,0:T(8,128)(2,1)S(1)} %get-tuple-element.103), channel_id=1, source_target_pairs={{0,112},{16,96},{32,80},{48,64},{64,48},{80,32},{96,16},{112,0},{1... | collective-permute-start | bytes 344072 | tf_op jit(solution)/shard_map/ppermute | solution.py:45
  68.3 8.7 %collective-permute-start.22 = (bf16[256,2048]{1,0:T(8,128)(2,1)S(1)}, bf16[256,2048]{1,0:T(8,128)(2,1)S(1)}, u32[]{:S(2)}, u32[]{:S(2)}) collective-permute-start(bf16[256,2048]{1,0:T(8,128)(2,1)S(1)} %collective-permute-done.4.refs_14_), channel_id=1, source_target_pairs={{0,8},{8,0},{1,9},{9,1},{2,10},{10,2},{3,11},{11,3},{4,12},{12,4},... | collective-permute-start | bytes 3145736 | tf_op jit(solution)/shard_map/ppermute | solution.py:45
  68.3 8.7 %collective-permute-start.23 = (bf16[256,2048]{1,0:T(8,128)(2,1)S(1)}, bf16[256,2048]{1,0:T(8,128)(2,1)S(1)}, u32[]{:S(2)}, u32[]{:S(2)}) collective-permute-start(bf16[256,2048]{1,0:T(8,128)(2,1)S(1)} %collective-permute-done.9.refs_15_), channel_id=1, source_target_pairs={{0,8},{8,0},{1,9},{9,1},{2,10},{10,2},{3,11},{11,3},{4,12},{12,4},... | collective-permute-start | bytes 3145736 | tf_op jit(solution)/shard_map/ppermute | solution.py:45
  68.8 11.8 %collective-permute-start.30 = (bf16[208,256]{1,0:T(8,128)(2,1)S(1)}, bf16[208,256]{1,0:T(8,128)(2,1)S(1)}, u32[]{:S(2)}, u32[]{:S(2)}) collective-permute-start(bf16[208,256]{1,0:T(8,128)(2,1)S(1)} %merge.1.refs_0_), channel_id=1, source_target_pairs={{0,5},{1,4},{2,7},{3,6},{4,1},{5,0},{6,3},{7,2},{8,13},{9,12},{10,... | collective-permute-start | bytes 319496 | tf_op jit(solution)/shard_map/ppermute | solution.py:56
  72.8 8.7 %collective-permute-start.28 = (bf16[208,256]{1,0:T(8,128)(2,1)S(1)}, bf16[208,256]{1,0:T(8,128)(2,1)S(1)}, u32[]{:S(2)}, u32[]{:S(2)}) collective-permute-start(bf16[208,256]{1,0:T(8,128)(2,1)S(1)} %merge.1.refs_0_), channel_id=1, source_target_pairs={{0,7},{1,6},{2,5},{3,4},{4,3},{5,2},{6,1},{7,0},{8,11},{9,10},{10,... | collective-permute-start | bytes 319496 | tf_op jit(solution)/shard_map/ppermute | solution.py:56
  74.1 8.7 %collective-permute-start.26 = (bf16[208,256]{1,0:T(8,128)(2,1)S(1)}, bf16[208,256]{1,0:T(8,128)(2,1)S(1)}, u32[]{:S(2)}, u32[]{:S(2)}) collective-permute-start(bf16[208,256]{1,0:T(8,128)(2,1)S(1)} %merge.1.refs_0_), channel_id=1, source_target_pairs={{0,3},{1,2},{2,1},{3,0},{4,7},{5,6},{6,5},{7,4},{8,15},{9,14},{10,... | collective-permute-start | bytes 319496 | tf_op jit(solution)/shard_map/ppermute | solution.py:56
  77.1 8.5 %collective-permute-start.29 = (bf16[208,256]{1,0:T(8,128)(2,1)S(1)}, bf16[208,256]{1,0:T(8,128)(2,1)S(1)}, u32[]{:S(2)}, u32[]{:S(2)}) collective-permute-start(bf16[208,256]{1,0:T(8,128)(2,1)S(1)} %merge.1.refs_0_), channel_id=1, source_target_pairs={{0,4},{1,5},{2,6},{3,7},{4,0},{5,1},{6,2},{7,3},{8,12},{9,13},{10,... | collective-permute-start | bytes 319496 | tf_op jit(solution)/shard_map/ppermute | solution.py:56
  79.9 7.2 %collective-permute-start.27 = (bf16[208,256]{1,0:T(8,128)(2,1)S(1)}, bf16[208,256]{1,0:T(8,128)(2,1)S(1)}, u32[]{:S(2)}, u32[]{:S(2)}) collective-permute-start(bf16[208,256]{1,0:T(8,128)(2,1)S(1)} %merge.1.refs_0_), channel_id=1, source_target_pairs={{0,6},{1,7},{2,4},{3,5},{4,2},{5,3},{6,0},{7,1},{8,10},{9,11},{10,... | collective-permute-start | bytes 319496 | tf_op jit(solution)/shard_map/ppermute | solution.py:56
  80.6 6.4 %collective-permute-start.25 = (bf16[208,256]{1,0:T(8,128)(2,1)S(1)}, bf16[208,256]{1,0:T(8,128)(2,1)S(1)}, u32[]{:S(2)}, u32[]{:S(2)}) collective-permute-start(bf16[208,256]{1,0:T(8,128)(2,1)S(1)} %merge.1.refs_0_), channel_id=1, source_target_pairs={{0,2},{1,3},{2,0},{3,1},{4,6},{5,7},{6,4},{7,5},{8,14},{9,15},{10,... | collective-permute-start | bytes 319496 | tf_op jit(solution)/shard_map/ppermute | solution.py:56
  92.9 12.7 %collective-permute-start.31 = (bf16[208,256]{1,0:T(8,128)(2,1)S(1)}, bf16[208,256]{1,0:T(8,128)(2,1)S(1)}, u32[]{:S(2)}, u32[]{:S(2)}) collective-permute-start(bf16[208,256]{1,0:T(8,128)(2,1)S(1)} %get-tuple-element.114), channel_id=1, source_target_pairs={{0,5},{1,4},{2,7},{3,6},{4,1},{5,0},{6,3},{7,2},{8,13},{9,12},{10,... | collective-permute-start | bytes 319496 | tf_op jit(solution)/shard_map/ppermute | solution.py:45
  98.1 7.5 %collective-permute-start.32 = (bf16[208,256]{1,0:T(8,128)(2,1)S(1)}, bf16[208,256]{1,0:T(8,128)(2,1)S(1)}, u32[]{:S(2)}, u32[]{:S(2)}) collective-permute-start(bf16[208,256]{1,0:T(8,128)(2,1)S(1)} %get-tuple-element.115), channel_id=1, source_target_pairs={{0,3},{1,2},{2,1},{3,0},{4,7},{5,6},{6,5},{7,4},{8,11},{9,10},{10,... | collective-permute-start | bytes 319496 | tf_op jit(solution)/shard_map/ppermute | solution.py:45
  98.3 9.6 %collective-permute-start.33 = (bf16[208,256]{1,0:T(8,128)(2,1)S(1)}, bf16[208,256]{1,0:T(8,128)(2,1)S(1)}, u32[]{:S(2)}, u32[]{:S(2)}) collective-permute-start(bf16[208,256]{1,0:T(8,128)(2,1)S(1)} %get-tuple-element.116), channel_id=1, source_target_pairs={{0,7},{1,6},{2,5},{3,4},{4,3},{5,2},{6,1},{7,0},{8,15},{9,14},{10,... | collective-permute-start | bytes 319496 | tf_op jit(solution)/shard_map/ppermute | solution.py:45
  100.1 8.1 %collective-permute-start.34 = (bf16[208,256]{1,0:T(8,128)(2,1)S(1)}, bf16[208,256]{1,0:T(8,128)(2,1)S(1)}, u32[]{:S(2)}, u32[]{:S(2)}) collective-permute-start(bf16[208,256]{1,0:T(8,128)(2,1)S(1)} %get-tuple-element.117), channel_id=1, source_target_pairs={{0,4},{1,5},{2,6},{3,7},{4,0},{5,1},{6,2},{7,3},{8,12},{9,13},{10,... | collective-permute-start | bytes 319496 | tf_op jit(solution)/shard_map/ppermute | solution.py:45
  104.6 6.2 %collective-permute-start.35 = (bf16[208,256]{1,0:T(8,128)(2,1)S(1)}, bf16[208,256]{1,0:T(8,128)(2,1)S(1)}, u32[]{:S(2)}, u32[]{:S(2)}) collective-permute-start(bf16[208,256]{1,0:T(8,128)(2,1)S(1)} %get-tuple-element.118), channel_id=1, source_target_pairs={{0,1},{1,0},{2,3},{3,2},{4,5},{5,4},{6,7},{7,6},{8,9},{9,8},{10,11... | collective-permute-start | bytes 319496 | tf_op jit(solution)/shard_map/ppermute | solution.py:45
  (22 other events, 430.2 us)
